TPU v7x, 32 devices: a whole 2x2x4 slice. The times are simulated.
32 devices in a mesh: slab: 8 (over z, core), dom: 4 (over y, x).
Axes of the slice: x: 2, y: 2, z: 4, core: 2. Of those that a mesh axis runs over, the one named last changes fastest.
Arguments:
- positions: float32 [3, 16384], P(None, ('slab', 'dom')), may hold values from -0.5 to 32.5, as said below
- burgers: float32 [3, 16384], P(None, ('slab', 'dom')), may hold values from -6 to 6
- mobility: float32 [16384], P(('slab', 'dom')), may hold values from 0.5 to 2
- block_cells: int32 [128], P(('slab', 'dom')), may hold values from 0 to 127, as said below
- pairs: int32 [2048, 2], P(('slab', 'dom')), may hold values from 0 to 127, as said below
- pair_count: int32 [32], P(('slab', 'dom')), may hold values from 8 to 64, as said below
Outputs:
- moved: float32 [3, 16384], P(None, ('slab', 'dom'))
- velocity: float32 [3, 16384], P(None, ('slab', 'dom'))
Inputs may be any that keep to these rules, and one draw needn't show every extreme that they name: `block_cells`: block k lies in slab k // (4 * 4) and its cell is 16 times that slab plus 0 to 15. `positions`: each segment lies within 2.5 of its block's cell centre along x and within 1.5 along y and z. `pairs`: device d = s * 4 + e owns blocks d * 4 to (d + 1) * 4 - 1. In device d's slots the first block is one of its own; the second is owned by a device of slab s - 1, s or s + 1 at dom position e - 1, e or e + 1, and differs from the first. Every slot holds such a pair, used or not. `pair_count`: in each slab exactly one device has 64 used slots; the others have at most 32.
All inputs are finite; a program needn't handle non-finite values.
Results may differ from a plain program's by a relative error of at most 0.0003.
Values sent between devices are 32-bit elements; how exact they have to be, the bound alone decides.
No kernel may reach another device: no remote copies, remote signals or barrier semaphores. Data moves between devices by JAX's collectives and lax.ppermute only.
A program may use at most 64 MiB of HBM per device.

v0:
```python
import math

import jax
import jax.numpy as jnp
from jax import lax
from jax.sharding import PartitionSpec as P

BLOCK_SEGS = 128


core_near = 0.25
core_far = 9.0
time_increment = 0.25
pair_batch = 4
hi_prec = lax.Precision.HIGHEST


def padded(x, sides, width):
    for axis, dim in sides:
        peers, length = (lax.axis_size(axis), x.shape[dim])
        up = [(i, (i + 1) % peers) for i in range(peers - 1)]
        down = [(j, i) for i, j in up]
        last = lax.slice_in_dim(x, length - width, length, axis=dim)
        initial = lax.slice_in_dim(x, 0, width, axis=dim)
        before = lax.ppermute(last, axis, up)
        after = lax.ppermute(initial, axis, down)
        x = jnp.concatenate([before, x, after], axis=dim)
    return x


def shifted(block, axis, distance):
    devices = range(lax.axis_size(axis))
    route = [(i - distance, i) for i in devices if i - distance in devices]
    return lax.ppermute(block, axis, route)


def centers(cells):
    slabs = cells // 16
    rest = cells % 16
    return jnp.stack([4 * slabs + 2, 2 * (rest // 4) + 1, 2 * (rest % 4) + 1]).astype(jnp.float32)


def block_moments(posit, burg, cells, ncells, width, base_cell):
    nblk = cells.shape[0]
    offset = posit.reshape(3, nblk, width) - centers(cells)[:, :, None]
    vec = burg.reshape(3, nblk, width)
    first = (vec[:, None] * offset[None]).reshape(9, nblk, width)
    second = (vec[:, None, None] * offset[None, :, None] * offset[None, None, :]).reshape(
        27, nblk, width
    )
    rows = jnp.sum(jnp.concatenate([vec, first, second], axis=0), axis=2)
    onehot = ((cells - base_cell)[:, None] == jnp.arange(ncells, dtype=jnp.int32)[None, :]).astype(
        jnp.float32
    )
    return jnp.dot(rows, onehot, precision=hi_prec)


def far_field(posit, burg, moments):
    ncells = moments.shape[1]
    nblk = ncells // 64
    zeds = centers(jnp.arange(ncells, dtype=jnp.int32)).reshape(3, nblk, 64).transpose(1, 0, 2)
    mblk = moments.reshape(39, nblk, 64).transpose(1, 0, 2)

    def visit(acc, item):
        zpart, mpart = item
        r = posit[:, None, :] - zpart[:, :, None]
        sq = r[0] * r[0] + r[1] * r[1] + r[2] * r[2] + core_far
        inv3 = 1.0 / (sq * jnp.sqrt(sq))
        inv5 = inv3 / sq
        inv7 = inv5 / sq
        qzero = jnp.einsum("kc,kn->cn", mpart[0:3], burg, precision=hi_prec)
        qone = jnp.einsum("kac,kn->acn", mpart[3:12].reshape(3, 3, 64), burg, precision=hi_prec)
        qtwo = jnp.einsum(
            "kabc,kn->abcn", mpart[12:39].reshape(3, 3, 3, 64), burg, precision=hi_prec
        )
        qone_r = jnp.sum(qone * r, axis=0)
        qtwo_r = jnp.sum(qtwo * r[None], axis=1)
        rqr = jnp.sum(r * qtwo_r, axis=0)
        trace = qtwo[0, 0] + qtwo[1, 1] + qtwo[2, 2]
        scal = qzero * inv3 + 3.0 * qone_r * inv5 - 1.5 * trace * inv5 + 7.5 * rqr * inv7
        force = r * scal[None] - qone * inv3[None] - 3.0 * qtwo_r * inv5[None]
        return (acc + jnp.sum(force, axis=1), None)

    start = jnp.zeros(posit.shape, jnp.float32)
    total, unused = lax.scan(visit, start, (zeds, mblk))
    return total


def pair_forces(pos_a, bur_a, pos_b, bur_b, weight):
    r = pos_a[:, :, :, None] - pos_b[:, :, None, :]
    sq = r[0] * r[0] + r[1] * r[1] + r[2] * r[2]
    near_s = sq + core_near
    far_s = sq + core_far
    kern = 1.0 / (near_s * jnp.sqrt(near_s)) - 1.0 / (far_s * jnp.sqrt(far_s))
    coef = jnp.sum(bur_a[:, :, :, None] * bur_b[:, :, None, :], axis=0)
    wgt = weight[:, None, None] * coef * kern
    wr = wgt[None] * r
    return (jnp.sum(wr, axis=3), -jnp.sum(wr, axis=2))


def around_all(stacked):
    grown = padded(stacked[:, None, None, :], (("slab", 1), ("dom", 2)), 1)
    return grown.reshape(stacked.shape[0], -1)


def give_around(window_force, per_dev):
    grid = window_force.reshape(3, 3, 3, per_dev)
    from_above = shifted(grid[:, 0], "slab", -1)
    from_below = shifted(grid[:, 2], "slab", 1)
    row = grid[:, 1] + from_above + from_below
    from_right = shifted(row[:, 0], "dom", -1)
    from_left = shifted(row[:, 2], "dom", 1)
    return row[:, 1] + from_right + from_left


def body(positions, burgers, mobility, block_cells, pairs, pair_count):
    count_segs = positions.shape[1]
    width = BLOCK_SEGS
    n_slab = lax.axis_size("slab")
    n_dom = lax.axis_size("dom")
    ncells = 16 * n_slab
    blk_dev = block_cells.shape[0]
    far_scale = math.sqrt(ncells / (count_segs * n_slab * n_dom))
    slots = pairs.shape[0]
    my_slab = lax.axis_index("slab")
    my_dom = lax.axis_index("dom")
    used = pair_count[0]

    def locate(rotation_slots):
        return pairs[jnp.minimum(rotation_slots, slots - 1)]

    def to_window(blocks):
        owner = blocks // blk_dev
        within = blocks % blk_dev
        row_off = owner // n_dom - my_slab + 1
        col_off = owner % n_dom - my_dom + 1
        return jnp.clip((row_off * 3 + col_off) * blk_dev + within, 0, 9 * blk_dev - 1)

    def near(window):
        pos_win = window[0:3].reshape(3, -1, width)
        bur_win = window[3:6].reshape(3, -1, width)

        def turn(index, acc):
            rotation_slots = index * pair_batch + jnp.arange(pair_batch, dtype=jnp.int32)
            weight = (rotation_slots < used).astype(jnp.float32)
            chosen = locate(rotation_slots)
            first_blk = to_window(chosen[:, 0])
            second_blk = to_window(chosen[:, 1])
            force_a, force_b = pair_forces(
                pos_win[:, first_blk],
                bur_win[:, first_blk],
                pos_win[:, second_blk],
                bur_win[:, second_blk],
                weight,
            )
            return acc.at[:, first_blk].add(force_a).at[:, second_blk].add(force_b)

        groups = (used + pair_batch - 1) // pair_batch
        start = jnp.zeros(pos_win.shape, jnp.float32)
        return lax.fori_loop(0, groups, turn, start).reshape(3, -1)

    def gather_moments(posit):
        local = block_moments(posit, burgers, block_cells, 16, width, 16 * my_slab)
        summed = lax.psum(local, "dom")
        return lax.all_gather(summed, "slab", axis=1, tiled=True)

    def speed(posit, window):
        moments = gather_moments(posit)
        far = far_field(posit, burgers, moments)
        near_own = give_around(near(window), count_segs)
        return mobility[None, :] * (far_scale * far + near_own)

    stacked = jnp.concatenate([positions, burgers], axis=0)
    leading_window = around_all(stacked)
    first_v = speed(positions, leading_window)
    stepped = positions + time_increment * first_v
    restacked = jnp.concatenate([stepped, burgers], axis=0)
    window_second = around_all(restacked)
    second_v = speed(stepped, window_second)
    total = first_v + second_v
    return (positions + 0.5 * time_increment * total, 0.5 * total)


def solution(mesh):
    placed = (
        P(None, ("slab", "dom")),
        P(None, ("slab", "dom")),
        P(("slab", "dom")),
        P(("slab", "dom")),
        P(("slab", "dom"), None),
        P(("slab", "dom")),
    )
    return jax.shard_map(
        body,
        mesh=mesh,
        in_specs=placed,
        out_specs=(P(None, ("slab", "dom")), P(None, ("slab", "dom"))),
        check_vma=False,
    )
```

profile of v0, /device:TPU:0, one launch (start us, length us, event | category | flops | bytes accessed | tf_op | source)
XLA Modules:
  0.0 326.1 jit_solution(1120146685088651747)
XLA Ops:
  1.4 1.3 collective-permute-start.1
  2.6 3.0 collective-permute-start
  8.4 1.3 collective-permute-start.3
  9.7 5.5 %collective-permute-start.2 = (f32[6,3,1,512]{3,0,2,1:T(8,128)S(1)}, f32[6,3,1,512]{3,0,2,1:T(8,128)S(1)}, u32[]{:S(2)}, u32[]{:S(2)}) collective-permute-start(f32[6,3,1,512]{3,0,2,1:T(8,128)S(1)} %pad_maximum_fusion.4), channel_id=1, source_target_pairs={{0,1},{1,2},{2,3},{4,5},{5,6},{6,7},{8,9},{9,10},{10,11},{12,13},{... | collective-permute-start | bytes 110600 | tf_op jit(solution)/shard_map/ppermute | solution.py:25
  17.0 19.7 %while.48 = (s32[]{:T(128)}, f32[3,36,128]{2,0,1:T(4,128)S(1)}, s32[]{:T(128)}, s32[64,2]{1,0:T(8,128)S(1)}, s32[]{:T(128)}, /*index=5*/s32[]{:T(128)}, s32[]{:T...) while((s32[]{:T(128)}, f32[3,36,128]{2,0,1:T(4,128)S(1)}, ...), condition=%wide.region_14.15_spmd, body=%wide.region_8.14_spmd.sunk | while | flops 2233267 | bytes 2855389 | solution.py:160
  36.8 1.3 collective-permute-start.4
  38.1 29.7 %collective-permute-start.5 = (f32[3,3,512]{2,0,1:T(4,128)S(1)}, f32[3,3,512]{2,0,1:T(4,128)S(1)}, u32[]{:S(2)}, u32[]{:S(2)}) collective-permute-start(f32[3,3,512]{2,0,1:T(4,128)S(1)} %get-tuple-element.571), channel_id=1, source_target_pairs={{0,4},{4,8},{8,12},{12,16},{16,20},{20,24},{24,28},{1,5},{5,9},{9,... | collective-permute-start | bytes 55304 | tf_op jit(solution)/shard_map/ppermute | solution.py:34
  67.9 70.2 %psum.14 = f32[39,16]{0,1:T(8,128)S(1)} all-reduce(f32[39,16]{0,1:T(8,128)S(1)} %fusion.151), channel_id=1, replica_groups=mesh['slab'=8,'dom'=4] {'dom'}, use_global_device_ids=true, to_apply=%region_1.2 | all-reduce | flops 624 | bytes 4992 | tf_op jit(solution)/shard_map/psum | solution.py:164
  138.1 14.2 %all_gather.6 = f32[39,128]{0,1:T(8,128)S(1)} all-gather(f32[39,16]{0,1:T(8,128)S(1)} %psum.14), channel_id=1, replica_groups=mesh['slab'=8,'dom'=4] {'slab'}, dimensions={1}, use_global_device_ids=true | all-gather | bytes 22464 | tf_op jit(solution)/shard_map/all_gather | solution.py:165
  152.4 1.3 collective-permute-start.6
  153.7 4.6 %collective-permute-start.7 = (f32[3,512]{1,0:T(4,128)S(1)}, f32[3,512]{1,0:T(4,128)S(1)}, u32[]{:S(2)}, u32[]{:S(2)}) collective-permute-start(f32[3,512]{1,0:T(4,128)S(1)} %get-tuple-element.575), channel_id=1, source_target_pairs={{0,1},{1,2},{2,3},{4,5},{5,6},{6,7},{8,9},{9,10},{10,11},{12,13},{... | collective-permute-start | bytes 18440 | tf_op jit(solution)/shard_map/ppermute | solution.py:34
  158.3 5.3 %while.50 = (s32[]{:T(128)}, f32[3,512]{1,0:T(4,128)S(1)}, f32[3,512]{1,0:T(4,128)S(1)}, f32[2,3,64]{2,1,0:T(4,128)S(1)}, f32[2,39,64]{2,1,0:T(8,128)S(1)}, /*in...) while((s32[]{:T(128)}, f32[3,512]{1,0:T(4,128)S(1)}, f32[3,512]{1,0:T(4,128)S(1)}, ...), condition=%wide.region_7.8_spmd.clone, body=%wide.region_2.7_spmd.clone.sunk | while | flops 18023940 | bytes 6538151 | solution.py:85
  163.7 1.3 collective-permute-start.9
  165.0 3.0 collective-permute-start.8
  170.1 5.5 %collective-permute-start.10 = (f32[6,3,1,512]{3,0,2,1:T(8,128)S(1)}, f32[6,3,1,512]{3,0,2,1:T(8,128)S(1)}, u32[]{:S(2)}, u32[]{:S(2)}) collective-permute-start(f32[6,3,1,512]{3,0,2,1:T(8,128)S(1)} %pad_maximum_fusion.5), channel_id=1, source_target_pairs={{0,1},{1,2},{2,3},{4,5},{5,6},{6,7},{8,9},{9,10},{10,11},{12,13},{... | collective-permute-start | bytes 110600 | tf_op jit(solution)/shard_map/ppermute | solution.py:25
  175.9 1.7 collective-permute-done.10
  177.7 19.7 %while.49 = (s32[]{:T(128)}, f32[3,36,128]{2,0,1:T(4,128)S(1)}, s32[]{:T(128)}, s32[64,2]{1,0:T(8,128)S(1)}, s32[]{:T(128)}, /*index=5*/s32[]{:T(128)}, s32[]{:T...) while((s32[]{:T(128)}, f32[3,36,128]{2,0,1:T(4,128)S(1)}, ...), condition=%wide.region_29.30_spmd, body=%wide.region_23.29_spmd.sunk | while | flops 2233267 | bytes 2855389 | solution.py:160
  197.5 1.3 collective-permute-start.12
  198.8 29.1 %collective-permute-start.13 = (f32[3,3,512]{2,0,1:T(4,128)S(1)}, f32[3,3,512]{2,0,1:T(4,128)S(1)}, u32[]{:S(2)}, u32[]{:S(2)}) collective-permute-start(f32[3,3,512]{2,0,1:T(4,128)S(1)} %get-tuple-element.569), channel_id=1, source_target_pairs={{0,4},{4,8},{8,12},{12,16},{16,20},{20,24},{24,28},{1,5},{5,9},{9,... | collective-permute-start | bytes 55304 | tf_op jit(solution)/shard_map/ppermute | solution.py:34
  228.2 70.2 %psum.15 = f32[39,16]{0,1:T(8,128)S(1)} all-reduce(f32[39,16]{0,1:T(8,128)S(1)} %fusion.150), channel_id=1, replica_groups=mesh['slab'=8,'dom'=4] {'dom'}, use_global_device_ids=true, to_apply=%region_16.17 | all-reduce | flops 624 | bytes 4992 | tf_op jit(solution)/shard_map/psum | solution.py:164
  298.4 15.1 %all_gather.7 = f32[39,128]{0,1:T(8,128)S(1)} all-gather(f32[39,16]{0,1:T(8,128)S(1)} %psum.15), channel_id=1, replica_groups=mesh['slab'=8,'dom'=4] {'slab'}, dimensions={1}, use_global_device_ids=true | all-gather | bytes 22464 | tf_op jit(solution)/shard_map/all_gather | solution.py:165
  313.6 1.3 collective-permute-start.14
  314.9 4.6 %collective-permute-start.15 = (f32[3,512]{1,0:T(4,128)S(1)}, f32[3,512]{1,0:T(4,128)S(1)}, u32[]{:S(2)}, u32[]{:S(2)}) collective-permute-start(f32[3,512]{1,0:T(4,128)S(1)} %get-tuple-element.573), channel_id=1, source_target_pairs={{0,1},{1,2},{2,3},{4,5},{5,6},{6,7},{8,9},{9,10},{10,11},{12,13},{... | collective-permute-start | bytes 18440 | tf_op jit(solution)/shard_map/ppermute | solution.py:34
  319.6 5.3 %while.51 = (s32[]{:T(128)}, f32[3,512]{1,0:T(4,128)S(1)}, f32[3,512]{1,0:T(4,128)S(1)}, f32[2,3,64]{2,1,0:T(4,128)S(1)}, f32[2,39,64]{2,1,0:T(8,128)S(1)}, /*in...) while((s32[]{:T(128)}, f32[3,512]{1,0:T(4,128)S(1)}, f32[3,512]{1,0:T(4,128)S(1)}, ...), condition=%wide.region_22.23_spmd.clone, body=%wide.region_17.22_spmd.clone.sunk | while | flops 18023940 | bytes 6538151 | solution.py:85
  (256 shorter events, 57.9 us)
Async XLA Ops:
  1.4 7.0 %collective-permute-start.1 = (f32[6,1,1,512]{3,0,2,1:T(8,128)S(1)}, f32[6,1,1,512]{3,0,2,1:T(8,128)S(1)}, u32[]{:S(2)}, u32[]{:S(2)}) collective-permute-start(f32[6,1,1,512]{3,0,2,1:T(8,128)S(1)} %fusion.138), channel_id=1, source_target_pairs={{4,0},{8,4},{12,8},{16,12},{20,16},{24,20},{28,24},{5,1},{9,5},{13... | collective-permute-start | bytes 36872 | tf_op jit(solution)/shard_map/ppermute | solution.py:26
  2.6 5.7 %collective-permute-start = (f32[6,1,1,512]{3,0,2,1:T(8,128)S(1)}, f32[6,1,1,512]{3,0,2,1:T(8,128)S(1)}, u32[]{:S(2)}, u32[]{:S(2)}) collective-permute-start(f32[6,1,1,512]{3,0,2,1:T(8,128)S(1)} %fusion.138), channel_id=1, source_target_pairs={{0,4},{4,8},{8,12},{12,16},{16,20},{20,24},{24,28},{1,5},{5,9},{9,... | collective-permute-start | bytes 36872 | tf_op jit(solution)/shard_map/ppermute | solution.py:25
  8.4 8.3 %collective-permute-start.3 = (f32[6,3,1,512]{3,0,2,1:T(8,128)S(1)}, f32[6,3,1,512]{3,0,2,1:T(8,128)S(1)}, u32[]{:S(2)}, u32[]{:S(2)}) collective-permute-start(f32[6,3,1,512]{3,0,2,1:T(8,128)S(1)} %pad_maximum_fusion.4), channel_id=1, source_target_pairs={{1,0},{2,1},{3,2},{5,4},{6,5},{7,6},{9,8},{10,9},{11,10},{13,12},{... | collective-permute-start | bytes 110600 | tf_op jit(solution)/shard_map/ppermute | solution.py:26
  9.7 7.2 %collective-permute-start.2 = (f32[6,3,1,512]{3,0,2,1:T(8,128)S(1)}, f32[6,3,1,512]{3,0,2,1:T(8,128)S(1)}, u32[]{:S(2)}, u32[]{:S(2)}) collective-permute-start(f32[6,3,1,512]{3,0,2,1:T(8,128)S(1)} %pad_maximum_fusion.4), channel_id=1, source_target_pairs={{0,1},{1,2},{2,3},{4,5},{5,6},{6,7},{8,9},{9,10},{10,11},{12,13},{... | collective-permute-start | bytes 110600 | tf_op jit(solution)/shard_map/ppermute | solution.py:25
  17.0 141.3 %copy-start = (f32[3,512]{1,0:T(4,128)S(1)}, f32[3,512]{1,0:T(4,128)}, u32[]{:S(2)}) copy-start(f32[3,512]{1,0:T(4,128)} %param.15) | copy-start | bytes 18436
  17.0 141.3 %copy-start.1 = (f32[3,512]{1,0:T(4,128)S(1)}, f32[3,512]{1,0:T(4,128)}, u32[]{:S(2)}) copy-start(f32[3,512]{1,0:T(4,128)} %param.14) | copy-start | bytes 18436
  36.8 115.6 %collective-permute-start.4 = (f32[3,3,512]{2,0,1:T(4,128)S(1)}, f32[3,3,512]{2,0,1:T(4,128)S(1)}, u32[]{:S(2)}, u32[]{:S(2)}) collective-permute-start(f32[3,3,512]{2,0,1:T(4,128)S(1)} %get-tuple-element.570), channel_id=1, source_target_pairs={{4,0},{8,4},{12,8},{16,12},{20,16},{24,20},{28,24},{5,1},{9,5},{13... | collective-permute-start | bytes 55304 | tf_op jit(solution)/shard_map/ppermute | solution.py:34
  38.1 114.3 %collective-permute-start.5 = (f32[3,3,512]{2,0,1:T(4,128)S(1)}, f32[3,3,512]{2,0,1:T(4,128)S(1)}, u32[]{:S(2)}, u32[]{:S(2)}) collective-permute-start(f32[3,3,512]{2,0,1:T(4,128)S(1)} %get-tuple-element.571), channel_id=1, source_target_pairs={{0,4},{4,8},{8,12},{12,16},{16,20},{20,24},{24,28},{1,5},{5,9},{9,... | collective-permute-start | bytes 55304 | tf_op jit(solution)/shard_map/ppermute | solution.py:34
  152.4 11.2 %collective-permute-start.6 = (f32[3,512]{1,0:T(4,128)S(1)}, f32[3,512]{1,0:T(4,128)S(1)}, u32[]{:S(2)}, u32[]{:S(2)}) collective-permute-start(f32[3,512]{1,0:T(4,128)S(1)} %get-tuple-element.574), channel_id=1, source_target_pairs={{1,0},{2,1},{3,2},{5,4},{6,5},{7,6},{9,8},{10,9},{11,10},{13,12},{... | collective-permute-start | bytes 18440 | tf_op jit(solution)/shard_map/ppermute | solution.py:34
  153.7 9.9 %collective-permute-start.7 = (f32[3,512]{1,0:T(4,128)S(1)}, f32[3,512]{1,0:T(4,128)S(1)}, u32[]{:S(2)}, u32[]{:S(2)}) collective-permute-start(f32[3,512]{1,0:T(4,128)S(1)} %get-tuple-element.575), channel_id=1, source_target_pairs={{0,1},{1,2},{2,3},{4,5},{5,6},{6,7},{8,9},{9,10},{10,11},{12,13},{... | collective-permute-start | bytes 18440 | tf_op jit(solution)/shard_map/ppermute | solution.py:34
  158.3 5.4 %copy-start.2 = (f32[512]{0:T(512)S(1)}, f32[512]{0:T(512)}, u32[]{:S(2)}) copy-start(f32[512]{0:T(512)} %param.16) | copy-start | bytes 6148
  163.7 4.4 %collective-permute-start.9 = (f32[6,1,1,512]{3,0,2,1:T(8,128)S(1)}, f32[6,1,1,512]{3,0,2,1:T(8,128)S(1)}, u32[]{:S(2)}, u32[]{:S(2)}) collective-permute-start(f32[6,1,1,512]{3,0,2,1:T(8,128)S(1)} %fusion.139), channel_id=1, source_target_pairs={{4,0},{8,4},{12,8},{16,12},{20,16},{24,20},{28,24},{5,1},{9,5},{13... | collective-permute-start | bytes 36872 | tf_op jit(solution)/shard_map/ppermute | solution.py:26
  165.0 3.9 %collective-permute-start.8 = (f32[6,1,1,512]{3,0,2,1:T(8,128)S(1)}, f32[6,1,1,512]{3,0,2,1:T(8,128)S(1)}, u32[]{:S(2)}, u32[]{:S(2)}) collective-permute-start(f32[6,1,1,512]{3,0,2,1:T(8,128)S(1)} %fusion.139), channel_id=1, source_target_pairs={{0,4},{4,8},{8,12},{12,16},{16,20},{20,24},{24,28},{1,5},{5,9},{9,... | collective-permute-start | bytes 36872 | tf_op jit(solution)/shard_map/ppermute | solution.py:25
  168.9 7.0 %collective-permute-start.11 = (f32[6,3,1,512]{3,0,2,1:T(8,128)S(1)}, f32[6,3,1,512]{3,0,2,1:T(8,128)S(1)}, u32[]{:S(2)}, u32[]{:S(2)}) collective-permute-start(f32[6,3,1,512]{3,0,2,1:T(8,128)S(1)} %pad_maximum_fusion.5), channel_id=1, source_target_pairs={{1,0},{2,1},{3,2},{5,4},{6,5},{7,6},{9,8},{10,9},{11,10},{13,12},{... | collective-permute-start | bytes 110600 | tf_op jit(solution)/shard_map/ppermute | solution.py:26
  170.1 7.5 %collective-permute-start.10 = (f32[6,3,1,512]{3,0,2,1:T(8,128)S(1)}, f32[6,3,1,512]{3,0,2,1:T(8,128)S(1)}, u32[]{:S(2)}, u32[]{:S(2)}) collective-permute-start(f32[6,3,1,512]{3,0,2,1:T(8,128)S(1)} %pad_maximum_fusion.5), channel_id=1, source_target_pairs={{0,1},{1,2},{2,3},{4,5},{5,6},{6,7},{8,9},{9,10},{10,11},{12,13},{... | collective-permute-start | bytes 110600 | tf_op jit(solution)/shard_map/ppermute | solution.py:25
  197.5 116.1 %collective-permute-start.12 = (f32[3,3,512]{2,0,1:T(4,128)S(1)}, f32[3,3,512]{2,0,1:T(4,128)S(1)}, u32[]{:S(2)}, u32[]{:S(2)}) collective-permute-start(f32[3,3,512]{2,0,1:T(4,128)S(1)} %get-tuple-element.568), channel_id=1, source_target_pairs={{4,0},{8,4},{12,8},{16,12},{20,16},{24,20},{28,24},{5,1},{9,5},{13... | collective-permute-start | bytes 55304 | tf_op jit(solution)/shard_map/ppermute | solution.py:34
  198.8 114.8 %collective-permute-start.13 = (f32[3,3,512]{2,0,1:T(4,128)S(1)}, f32[3,3,512]{2,0,1:T(4,128)S(1)}, u32[]{:S(2)}, u32[]{:S(2)}) collective-permute-start(f32[3,3,512]{2,0,1:T(4,128)S(1)} %get-tuple-element.569), channel_id=1, source_target_pairs={{0,4},{4,8},{8,12},{12,16},{16,20},{20,24},{24,28},{1,5},{5,9},{9,... | collective-permute-start | bytes 55304 | tf_op jit(solution)/shard_map/ppermute | solution.py:34
  313.6 11.3 %collective-permute-start.14 = (f32[3,512]{1,0:T(4,128)S(1)}, f32[3,512]{1,0:T(4,128)S(1)}, u32[]{:S(2)}, u32[]{:S(2)}) collective-permute-start(f32[3,512]{1,0:T(4,128)S(1)} %get-tuple-element.572), channel_id=1, source_target_pairs={{1,0},{2,1},{3,2},{5,4},{6,5},{7,6},{9,8},{10,9},{11,10},{13,12},{... | collective-permute-start | bytes 18440 | tf_op jit(solution)/shard_map/ppermute | solution.py:34
  314.9 10.0 %collective-permute-start.15 = (f32[3,512]{1,0:T(4,128)S(1)}, f32[3,512]{1,0:T(4,128)S(1)}, u32[]{:S(2)}, u32[]{:S(2)}) collective-permute-start(f32[3,512]{1,0:T(4,128)S(1)} %get-tuple-element.573), channel_id=1, source_target_pairs={{0,1},{1,2},{2,3},{4,5},{5,6},{6,7},{8,9},{9,10},{10,11},{12,13},{... | collective-permute-start | bytes 18440 | tf_op jit(solution)/shard_map/ppermute | solution.py:34
where the time goes:
time: 326 us
  blocking collectives  170 us (52%)
  starting transfers between devices  95.4 us (29%)
  other arithmetic  26.6 us (8%)
  local copies, waits for them, and re-layouts  20 us (6%)
  matrix products  8.83 us (3%)
    psum x2, blocking collectives, gather_moments(): summed = lax.psum(local, 'dom')  140 us
    ppermute x8, starting transfers between devices, shifted(): return lax.ppermute(block, axis, route)  73.3 us
    all_gather x2, blocking collectives, gather_moments(): return lax.all_gather(summed, 'slab', axis=1, tiled=True)  29.2 us
    ppermute x4, starting transfers between devices, padded(): before = lax.ppermute(last, axis, up)  17 us
    scatter-add x12, other arithmetic, turn(): return acc.at[:, first_blk].add(force_a).at[:, second_blk].add(force_b)  7.75 us
  transfers between devices with their start and end apart: 16, of which 4 were waited for; matrix products, arithmetic and copies ran while one was open for 4% of the time, Pallas kernels for 0%

commit v1 on v0

v1 whole, which is shorter than its diff:
```python
import functools
import math

import jax
import jax.numpy as jnp
from jax import lax
from jax.experimental import pallas as pl
from jax.experimental.pallas import tpu as pltpu
from jax.sharding import PartitionSpec as P

LANES = 128
SUB = 8
CORE_NEAR = 0.25
CORE_FAR = 9.0
TIME_INCREMENT = 0.25
EXACT = lax.Precision.HIGHEST
VMEM = pl.BlockSpec(memory_space=pltpu.VMEM)
SMEM = pl.BlockSpec(memory_space=pltpu.SMEM)
PARAMS = pltpu.CompilerParams(vmem_limit_bytes=24 * 1024 * 1024)
SYM = ((0, 0), (0, 1), (0, 2), (1, 1), (1, 2), (2, 2))
MOMS = 3 + 9 + 18


def dot_lanes(a, b, precision=EXACT):
    return lax.dot_general(
        a, b, (((1,), (1,)), ((), ())), precision=precision, preferred_element_type=jnp.float32
    )


def center_of(cell):
    slab = jnp.floor(cell * 0.0625)
    rest = cell - 16.0 * slab
    row = jnp.floor(rest * 0.25)
    col = rest - 4.0 * row
    return (4.0 * slab + 2.0, 2.0 * row + 1.0, 2.0 * col + 1.0)


def column_of(values, like):
    index = lax.broadcasted_iota(jnp.int32, like, 0)
    out = jnp.full(like, values[-1], jnp.float32)
    for j, value in enumerate(values[:-1]):
        out = jnp.where(index == j, value, out)
    return out


def moment_row(pos, bur, cells_ref, stack_ref):
    nblk = pos[0].shape[0]
    cell = column_of([cells_ref[b].astype(jnp.float32) for b in range(nblk)], pos[0].shape)
    z = center_of(cell)
    d = [pos[k] - z[k] for k in range(3)]
    dd = [d[a] * d[e] for a, e in SYM]
    stack_ref[...] = jnp.zeros_like(stack_ref)
    m = 0
    for k in range(3):
        stack_ref[m * nblk : (m + 1) * nblk, :] = bur[k]
        m += 1
    for k in range(3):
        for a in range(3):
            stack_ref[m * nblk : (m + 1) * nblk, :] = bur[k] * d[a]
            m += 1
    for k in range(3):
        for j in range(6):
            stack_ref[m * nblk : (m + 1) * nblk, :] = bur[k] * dd[j]
            m += 1
    sums = dot_lanes(jnp.ones((SUB, LANES), jnp.float32), stack_ref[...])[0:1, :]
    lane = lax.broadcasted_iota(jnp.int32, (1, LANES), 1)
    for b in range(nblk):
        sums = jnp.where(lane == MOMS * nblk + b, cells_ref[b].astype(jnp.float32), sums)
    return sums


def spread(out_ref, value):
    count = out_ref.shape[0]

    def put(d, carry):
        out_ref[d] = value
        return carry

    lax.fori_loop(0, count, put, 0, unroll=math.gcd(count, 32))


def first_kernel(cells_ref, count_ref, pos_ref, bur_ref, pairs_ref, out_ref, stack_ref, load_ref, ids_ref):
    nblk = cells_ref.shape[0]
    slots = pairs_ref.shape[0]
    pos, bur = [], []
    for k in range(3):
        for b in range(nblk):
            load_ref[k * nblk + b : k * nblk + b + 1, :] = pos_ref[k : k + 1, b * LANES : (b + 1) * LANES]
            load_ref[(3 + k) * nblk + b : (3 + k) * nblk + b + 1, :] = bur_ref[
                k : k + 1, b * LANES : (b + 1) * LANES
            ]
    for k in range(3):
        pos.append(load_ref[k * nblk : (k + 1) * nblk, :])
        bur.append(load_ref[(3 + k) * nblk : (4 + k) * nblk, :])
    base = 6 * nblk
    lane = lax.broadcasted_iota(jnp.int32, (slots, LANES), 1)
    row = lax.broadcasted_iota(jnp.int32, (slots, LANES), 0)
    ids = jnp.where(lane < slots, pairs_ref[:, 0:1], pairs_ref[:, 1:2])
    hit = (lane == row) | (lane == row + slots)
    listed = jnp.sum(jnp.where(hit, ids, 0), axis=0, keepdims=True)
    slot = lax.broadcasted_iota(jnp.int32, (1, LANES), 1)
    slot = jnp.where(slot < slots, slot, slot - slots)
    listed = jnp.where(slot < count_ref[0], listed, -1).astype(jnp.float32)
    load_ref[base : base + 1, :] = listed
    load_ref[base + 1 : base + 2, :] = moment_row(pos, bur, cells_ref, stack_ref)
    rows = base + 2
    for r in range(rows):
        ids_ref[:, r * LANES : (r + 1) * LANES] = load_ref[r : r + 1, :]
    spread(out_ref, ids_ref[...])


def far_into(pos_row, bur_row, mom_ref, far_ref, nblk, ndev):
    def visit(g, carry):
        block = mom_ref[pl.ds(g * SUB, SUB), :]
        zall = center_of(block)

        def wide(x, lane):
            return jnp.broadcast_to(x[:, lane : lane + 1], (SUB, LANES))

        acc = list(carry)
        for b in range(nblk):
            mom = [wide(block, m * nblk + b) for m in range(MOMS)]
            z = [wide(zall[k], MOMS * nblk + b) for k in range(3)]
            for t in range(nblk):
                p = [pos_row(k, t) for k in range(3)]
                c = [bur_row(k, t) for k in range(3)]
                q0 = c[0] * mom[0] + c[1] * mom[1] + c[2] * mom[2]
                q1 = [c[0] * mom[3 + a] + c[1] * mom[6 + a] + c[2] * mom[9 + a] for a in range(3)]
                q2 = [c[0] * mom[12 + j] + c[1] * mom[18 + j] + c[2] * mom[24 + j] for j in range(6)]
                r = [p[k] - z[k] for k in range(3)]
                sq = r[0] * r[0] + r[1] * r[1] + (r[2] * r[2] + CORE_FAR)
                inv = lax.rsqrt(sq)
                inv2 = inv * inv
                inv3 = inv2 * inv
                u = [
                    q2[0] * r[0] + q2[1] * r[1] + q2[2] * r[2],
                    q2[1] * r[0] + q2[3] * r[1] + q2[4] * r[2],
                    q2[2] * r[0] + q2[4] * r[1] + q2[5] * r[2],
                ]
                q1r = q1[0] * r[0] + q1[1] * r[1] + q1[2] * r[2]
                rqr = u[0] * r[0] + u[1] * r[1] + u[2] * r[2]
                trace = q2[0] + q2[3] + q2[5]
                inner = (3.0 * q1r - 1.5 * trace) + (7.5 * rqr) * inv2
                scal = q0 + inner * inv2
                three = 3.0 * inv2
                for k in range(3):
                    f = (r[k] * scal - (q1[k] + three * u[k])) * inv3
                    acc[k * nblk + t] = acc[k * nblk + t] + f
        return tuple(acc)

    zero = jnp.zeros((SUB, LANES), jnp.float32)
    total = lax.fori_loop(0, ndev // SUB, visit, (zero,) * (3 * nblk))
    for j in range(3 * nblk):
        far_ref[j : j + 1, :] = jnp.sum(total[j], axis=0, keepdims=True)


def near_into(pos_of, bur_of, own_ref, list_ref, mult_ref, used_ref, acc_ref, near_ref, nblk):
    for a in range(nblk):
        acc_ref[...] = jnp.zeros_like(acc_ref)

        def visit(n, carry):
            g = list_ref[a, n]
            mult = mult_ref[a, n]
            p = [jnp.broadcast_to(pos_of(g, k), (SUB, LANES)) for k in range(3)]
            c = [jnp.broadcast_to(bur_of(g, k) * mult, (SUB, LANES)) for k in range(3)]
            for t in range(LANES // SUB):
                rows = slice(t * SUB, (t + 1) * SUB)
                r = [own_ref[a, k, rows, :] - p[k] for k in range(3)]
                sq = r[0] * r[0] + r[1] * r[1] + (r[2] * r[2] + CORE_NEAR)
                u = lax.rsqrt(sq)
                w = lax.rsqrt(sq + (CORE_FAR - CORE_NEAR))
                kern = u * u * u - w * w * w
                coef = (
                    own_ref[a, 3, rows, :] * c[0]
                    + own_ref[a, 4, rows, :] * c[1]
                    + own_ref[a, 5, rows, :] * c[2]
                )
                wgt = coef * kern
                for k in range(3):
                    acc_ref[k, rows, :] = acc_ref[k, rows, :] + wgt * r[k]
            return carry

        lax.fori_loop(0, used_ref[a], visit, 0)
        ones = jnp.ones((SUB, LANES), jnp.float32)
        for k in range(3):
            near_ref[k * nblk + a : k * nblk + a + 1, :] = dot_lanes(ones, acc_ref[k])[0:1, :]


def widen_own(row_of, own_ref, nblk, kinds):
    for a in range(nblk):
        for k in kinds:
            own_ref[a, k] = jnp.transpose(jnp.broadcast_to(row_of(k, a), (LANES, LANES)))


def build_lists(got_ref, rows, nblk, my_slab, my_dom, n_slab, n_dom, count_ref, count_smem, sem, list_ref, mult_ref, used_ref):
    base = 6 * nblk
    wide = 9 * nblk
    high = -(-wide // SUB) * SUB
    index = lax.broadcasted_iota(jnp.int32, (high, LANES), 0)
    gid = jnp.full((high, LANES), -2.0, jnp.float32)
    for k in range(9):
        ds, dd = k // 3 - 1, k % 3 - 1
        s, e = my_slab + ds, my_dom + dd
        inside = (s >= 0) & (s < n_slab) & (e >= 0) & (e < n_dom)
        first = jnp.where(inside, (s * n_dom + e) * nblk - k * nblk, -100000)
        here = (index >= k * nblk) & (index < (k + 1) * nblk)
        gid = jnp.where(here, (index + first).astype(jnp.float32), gid)
    own = (my_slab * n_dom + my_dom) * nblk
    small = lax.broadcasted_iota(jnp.int32, (SUB, LANES), 0)
    mine = jnp.where(small < nblk, small + own, -3).astype(jnp.float32)
    total = jnp.zeros((SUB, high), jnp.float32)
    for k in range(9):
        ds, dd = k // 3 - 1, k % 3 - 1
        s, e = my_slab + ds, my_dom + dd
        inside = (s >= 0) & (s < n_slab) & (e >= 0) & (e < n_dom)
        dev = jnp.clip(s, 0, n_slab - 1) * n_dom + jnp.clip(e, 0, n_dom - 1)
        row = got_ref[dev * rows + base]
        row = jnp.where(inside, row, -1.0)
        other = pltpu.roll(row, LANES // 2, 1)
        left = (mine == row).astype(jnp.float32)
        right = (gid == other).astype(jnp.float32)
        total = total + dot_lanes(left, right, None)
    count_ref[:, 0:high] = total
    copy = pltpu.make_async_copy(count_ref, count_smem, sem)
    copy.start()
    copy.wait()

    def visit(w, carry):
        k = w // nblk
        s = my_slab + k // 3 - 1
        e = my_dom + k % 3 - 1
        g = (s * n_dom + e) * nblk + w % nblk
        out = []
        for a in range(nblk):
            c = count_smem[a, w]
            list_ref[a, carry[a]] = g
            mult_ref[a, carry[a]] = c
            out.append(carry[a] + jnp.where(c > 0.5, 1, 0).astype(jnp.int32))
        return tuple(out)

    ends = lax.fori_loop(0, wide, visit, (jnp.int32(0),) * nblk)
    for a in range(nblk):
        used_ref[a] = ends[a]


def gather_moments(got_ref, rows, mom_ref, ndev):
    def take(d, carry):
        mom_ref[pl.ds(d, 1), :] = got_ref[d * rows + rows - 1]
        return carry

    lax.fori_loop(0, ndev, take, 0, unroll=math.gcd(ndev, 32))


def second_kernel(
    n_slab, n_dom, far_scale,
    cells_ref, mob_ref, got_ref,
    out_ref, vel_ref, list_ref, mult_ref, used_ref,
    stack_ref, own_ref, acc_ref, near_ref, far_ref, mom_ref, count_ref, next_ref, flat_ref, count_smem, sem,
):
    nblk = cells_ref.shape[0]
    ndev = n_slab * n_dom
    rows = got_ref.shape[0] // ndev
    my_slab, my_dom = lax.axis_index("slab"), lax.axis_index("dom")
    me = my_slab * n_dom + my_dom

    def own_row(k, b):
        return got_ref[me * rows + k * nblk + b]

    def block_row(g, k):
        return got_ref[(g // nblk) * rows + g % nblk + k * nblk]

    build_lists(
        got_ref, rows, nblk, my_slab, my_dom, n_slab, n_dom,
        count_ref, count_smem, sem, list_ref, mult_ref, used_ref,
    )
    gather_moments(got_ref, rows, mom_ref, ndev)
    widen_own(own_row, own_ref, nblk, range(6))
    near_into(
        block_row, lambda g, k: block_row(g, k + 3), own_ref, list_ref, mult_ref, used_ref,
        acc_ref, near_ref, nblk,
    )
    far_into(own_row, lambda k, b: own_row(k + 3, b), mom_ref, far_ref, nblk, ndev)
    pos, bur = [], []
    for k in range(3):
        here = slice(k * nblk, (k + 1) * nblk)
        vel = mob_ref[...] * (far_scale * far_ref[here, :] + near_ref[here, :])
        vel_ref[here, :] = vel
        for b in range(nblk):
            next_ref[k * nblk + b : k * nblk + b + 1, :] = own_row(k, b)
            next_ref[(3 + k) * nblk + b : (3 + k) * nblk + b + 1, :] = own_row(3 + k, b)
        moved = next_ref[here, :] + TIME_INCREMENT * vel
        next_ref[here, :] = moved
        pos.append(moved)
        bur.append(next_ref[(3 + k) * nblk : (4 + k) * nblk, :])
    last = moment_row(pos, bur, cells_ref, stack_ref)
    for r in range(3 * nblk):
        flat_ref[:, r * LANES : (r + 1) * LANES] = next_ref[r : r + 1, :]
    flat_ref[:, 3 * nblk * LANES :] = last
    spread(out_ref, flat_ref[...])


def third_kernel(
    n_slab, n_dom, far_scale,
    mob_ref, pos_ref, vel_ref, old_ref, got_ref, list_ref, mult_ref, used_ref,
    moved_ref, velocity_ref,
    own_ref, acc_ref, near_ref, far_ref, mom_ref,
):
    nblk = mob_ref.shape[0]
    ndev = n_slab * n_dom
    rows = got_ref.shape[0] // ndev
    old_rows = old_ref.shape[0] // ndev
    me = lax.axis_index("slab") * n_dom + lax.axis_index("dom")

    def row_of(k, b):
        if k < 3:
            return got_ref[me * rows + k * nblk + b]
        return old_ref[me * old_rows + k * nblk + b]

    gather_moments(got_ref, rows, mom_ref, ndev)
    widen_own(row_of, own_ref, nblk, range(6))
    near_into(
        lambda g, k: got_ref[(g // nblk) * rows + g % nblk + k * nblk],
        lambda g, k: old_ref[(g // nblk) * old_rows + g % nblk + (3 + k) * nblk],
        own_ref, list_ref, mult_ref, used_ref, acc_ref, near_ref, nblk,
    )
    far_into(row_of, lambda k, b: row_of(k + 3, b), mom_ref, far_ref, nblk, ndev)
    for k in range(3):
        here = slice(k * nblk, (k + 1) * nblk)
        vel = mob_ref[...] * (far_scale * far_ref[here, :] + near_ref[here, :])
        near_ref[here, :] = 0.5 * (vel_ref[here, :] + vel)
        for b in range(nblk):
            lanes = slice(b * LANES, (b + 1) * LANES)
            mean = near_ref[k * nblk + b : k * nblk + b + 1, :]
            velocity_ref[k : k + 1, lanes] = mean
            moved_ref[k : k + 1, lanes] = pos_ref[k : k + 1, lanes] + TIME_INCREMENT * mean


def body(positions, burgers, mobility, block_cells, pairs, pair_count):
    f32 = jnp.float32
    segs = positions.shape[1]
    nblk = block_cells.shape[0]
    n_slab, n_dom = lax.axis_size("slab"), lax.axis_size("dom")
    ndev = n_slab * n_dom
    far_scale = math.sqrt(16 * n_slab / (segs * ndev))
    rows, rows2 = 6 * nblk + 2, 3 * nblk + 1
    wide = 9 * nblk
    mob = mobility.reshape(nblk, LANES)
    high = -(-(3 * nblk) // SUB) * SUB
    scratch = [
        pltpu.VMEM((nblk, 6, LANES, LANES), f32),
        pltpu.VMEM((3, LANES, LANES), f32),
        pltpu.VMEM((high, LANES), f32),
        pltpu.VMEM((high, LANES), f32),
        pltpu.VMEM((ndev, LANES), f32),
    ]
    load = pl.pallas_call(
        first_kernel,
        out_shape=jax.ShapeDtypeStruct((ndev, 1, rows * LANES), f32),
        in_specs=[SMEM, SMEM, VMEM, VMEM, VMEM],
        out_specs=VMEM,
        scratch_shapes=[
            pltpu.VMEM((LANES, LANES), f32),
            pltpu.VMEM((-(-rows // SUB) * SUB, LANES), f32),
            pltpu.VMEM((1, rows * LANES), f32),
        ],
        compiler_params=PARAMS,
        name="pack",
    )(block_cells, pair_count, positions, burgers, pairs)
    got = lax.all_to_all(load, ("slab", "dom"), 0, 0, tiled=True).reshape(ndev * rows, 1, LANES)
    load2, vel, lists, mult, used = pl.pallas_call(
        functools.partial(second_kernel, n_slab, n_dom, far_scale),
        out_shape=(
            jax.ShapeDtypeStruct((ndev, 1, rows2 * LANES), f32),
            jax.ShapeDtypeStruct((3 * nblk, LANES), f32),
            jax.ShapeDtypeStruct((nblk, wide + 1), jnp.int32),
            jax.ShapeDtypeStruct((nblk, wide + 1), f32),
            jax.ShapeDtypeStruct((nblk,), jnp.int32),
        ),
        in_specs=[SMEM, VMEM, VMEM],
        out_specs=(VMEM, VMEM, SMEM, SMEM, SMEM),
        scratch_shapes=[pltpu.VMEM((LANES, LANES), f32)]
        + scratch
        + [
            pltpu.VMEM((SUB, LANES), f32),
            pltpu.VMEM((6 * nblk, LANES), f32),
            pltpu.VMEM((1, rows2 * LANES), f32),
            pltpu.SMEM((SUB, LANES), f32),
            pltpu.SemaphoreType.DMA(()),
        ],
        compiler_params=PARAMS,
        name="step_one",
    )(block_cells, mob, got)
    got2 = lax.all_to_all(load2, ("slab", "dom"), 0, 0, tiled=True).reshape(ndev * rows2, 1, LANES)
    return pl.pallas_call(
        functools.partial(third_kernel, n_slab, n_dom, far_scale),
        out_shape=(jax.ShapeDtypeStruct((3, segs), f32),) * 2,
        in_specs=[VMEM, VMEM, VMEM, VMEM, VMEM, SMEM, SMEM, SMEM],
        out_specs=(VMEM, VMEM),
        scratch_shapes=scratch,
        compiler_params=PARAMS,
        name="step_two",
    )(mob, positions, vel, got, got2, lists, mult, used)


def solution(mesh):
    placed = (
        P(None, ("slab", "dom")),
        P(None, ("slab", "dom")),
        P(("slab", "dom")),
        P(("slab", "dom")),
        P(("slab", "dom"), None),
        P(("slab", "dom")),
    )
    return jax.shard_map(
        body,
        mesh=mesh,
        in_specs=placed,
        out_specs=(P(None, ("slab", "dom")), P(None, ("slab", "dom"))),
        check_vma=False,
    )
```

time: 326 us -> 57.8 us (0.18)
  blocking collectives: 170 us -> 34.8 us
  starting transfers between devices: 95.4 us -> 0 us
  other arithmetic: 26.6 us -> 0 us
  Pallas kernels: 0 us -> 20 us
  local copies, waits for them, and re-layouts: 20 us -> 1.39 us
  matrix products: 8.83 us -> 0 us
    psum x2 -> x0, blocking collectives: 140 us -> none  [gather_moments(): summed = lax.psum(local, 'dom')]
    ppermute x16 -> x0, starting transfers between devices: 95.4 us -> none  [the longest x8 73.3 us: shifted(): return lax.ppermute(block, axis, route)]
    all_to_all x0 -> x2, blocking collectives: none -> 34.8 us  [the longest x1 21.4 us: body(): lax.all_to_all(load, ('slab', 'dom'), 0, 0, tiled=True)]
    all_gather x2 -> x0, blocking collectives: 29.2 us -> none  [gather_moments(): return lax.all_gather(summed, 'slab', axis=1, tiled=True)]
    pallas_call x0 -> x3, Pallas kernels: none -> 20 us  [the longest x1 10.5 us: body(): pl.pallas_call(functools.partial(second_kernel, n_slab, n_dom, far_scale)...]
    gather x54 -> x0, local copies, waits for them, and re-layouts: 17.2 us -> none  [the longest x12 3.46 us: turn(): pos_win[:, second_blk]]
    dot_general x14 -> x0, matrix products: 8.83 us -> none  [the longest x4 4.75 us: visit(): jnp.einsum('kabc,kn->abcn', mpart[12:39].reshape(3, 3, 3, 64), burg, prec...]
    scatter-add x12 -> x0, other arithmetic: 7.75 us -> none  [turn(): return acc.at[:, first_blk].add(force_a).at[:, second_blk].add(force_b)]
  transfers between devices with their start and end apart: 16 -> 0, of which waited for: 4 -> 0; matrix products, arithmetic and copies ran while one was open for 4% -> 0% of each run, Pallas kernels for 0% -> 0%
where the time goes in v1:
time: 57.8 us; the launch traced here: 57.5 us
  blocking collectives  34.8 us (60%)
  Pallas kernels  20 us (35%)
  local copies, waits for them, and re-layouts  1.39 us (2%)
  between operations  1.34 us (2%)
    all_to_all x1, blocking collectives, body(): lax.all_to_all(load, ('slab', 'dom'), 0, 0, tiled=True)  21.4 us
    all_to_all x1, blocking collectives, body(): lax.all_to_all(load2, ('slab', 'dom'), 0, 0, tiled=True)  13.4 us
    pallas_call x1, Pallas kernels, body(): pl.pallas_call(functools.partial(second_kernel, n_slab, n_dom, far_scale)...  10.5 us
    pallas_call x1, Pallas kernels, body(): pl.pallas_call(functools.partial(third_kernel, n_slab, n_dom, far_scale),...  8.69 us
    unnamed x11, local copies, waits for them, and re-layouts  1.39 us

profile of v1, /device:TPU:0, one launch (start us, length us, event | category | flops | bytes accessed | tf_op | source)
XLA Modules:
  0.0 57.5 jit_solution(7295675479581498285)
XLA Ops:
  0.6 0.0 copy-start.4
  1.3 0.0 copy-done.4
  1.3 0.0 copy-start
  1.3 0.0 copy-start.2
  1.3 0.0 copy-start.3
  1.3 0.1 copy.8.pairs_ref
  1.4 0.6 copy-done
  2.0 0.0 copy-done.2
  2.0 0.0 copy-done.3
  2.0 0.8 %pack.1 = f32[32,1,3328]{2,1,0:T(1,128)S(1)} custom-call(s32[4]{0:T(128)S(1)} %copy-done.3, s32[1]{0:T(128)S(6)} %copy.9.count_ref, f32[3,512]{1,0:T(4,128)S(1)} %copy-done, f32[3,512]{1,0:T(4,128)S(1)} %copy-done.2, s32[64,2]{1,0:T(8,128)S(1)} %copy.8.pairs_ref), custom_call_target="tpu_custom_call" | custom-call | tf_op jit(solution)/shard_map/pack/pallas_call | solution.py:356
  2.9 21.4 %all_to_all.10 = f32[32,1,3328]{2,1,0:T(1,128)S(1)} all-to-all(f32[32,1,3328]{2,1,0:T(1,128)S(1)} %pack.1), channel_id=1, replica_groups=mesh['slab'=8,'dom'=4] {'slab','dom'}, dimensions={0} | all-to-all | bytes 851968 | tf_op jit(solution)/shard_map/all_to_all | solution.py:369
  24.3 0.0 copy-start.1
  24.3 0.7 %copy-done.1 = f32[512]{0:T(512)S(1)} copy-done((f32[512]{0:T(512)S(1)}, f32[512]{0:T(512)}, u32[]{:S(2)}) %copy-start.1) | copy-done | bytes 2072
  25.0 10.5 %step_one.1 = (f32[32,1,1664]{2,1,0:T(1,128)S(1)}, f32[12,128]{1,0:T(8,128)S(1)}, s32[4,37]{1,0:T(4,128)S(1)}, f32[4,37]{1,0:T(4,128)S(1)}, s32[4]{0:T(128)S(1)}) custom-call(s32[4]{0:T(128)S(1)} %copy-done.3, f32[4,128]{1,0:T(4,128)S(1)} %bitcast.6, f32[832,1,128]{2,1,0:T(1,128)S(1)} %bitcast.3), custom_call_target="tpu_custom_call" | custom-call | tf_op jit(solution)/shard_map/step_one/pallas_call | solution.py:370
  35.4 13.4 %all_to_all.11 = f32[32,1,1664]{2,1,0:T(1,128)S(1)} all-to-all(f32[32,1,1664]{2,1,0:T(1,128)S(1)} %get-tuple-element.8), channel_id=1, replica_groups=mesh['slab'=8,'dom'=4] {'slab','dom'}, dimensions={0} | all-to-all | bytes 425984 | tf_op jit(solution)/shard_map/all_to_all | solution.py:393
  48.8 8.7 %step_two.1 = (f32[3,512]{1,0:T(4,128)}, f32[3,512]{1,0:T(4,128)}) custom-call(f32[4,128]{1,0:T(4,128)S(1)} %bitcast.7, f32[3,512]{1,0:T(4,128)S(1)} %copy-done, f32[12,128]{1,0:T(8,128)S(1)} %get-tuple-element.7.vel_ref, f32[832,1,128]{2,1,0:T(1,128)S(1)} %bitcast.4, f32[416,1,128]{2,1,0:T(1,128)S(1)} %bitcast.5, s32[4,37]{1,0:T(4,128)S(1)} %get-tuple-element.9.list_ref, ...), custom_call_target="tpu_custom_call" | custom-call | tf_op jit(solution)/shard_map/step_two/pallas_call | solution.py:394
Async XLA Ops:
  0.6 0.7 %copy-start.4 = (s32[64,2]{0,1:T(2,128)S(1)}, s32[64,2]{0,1:T(2,128)}, u32[]{:S(2)}) copy-start(s32[64,2]{0,1:T(2,128)} %param.10) | copy-start | bytes 1540
  1.3 0.7 %copy-start = (f32[3,512]{1,0:T(4,128)S(1)}, f32[3,512]{1,0:T(4,128)}, u32[]{:S(2)}) copy-start(f32[3,512]{1,0:T(4,128)} %pos_ref.3) | copy-start | bytes 18436
  1.3 0.7 %copy-start.2 = (f32[3,512]{1,0:T(4,128)S(1)}, f32[3,512]{1,0:T(4,128)}, u32[]{:S(2)}) copy-start(f32[3,512]{1,0:T(4,128)} %bur_ref.1) | copy-start | bytes 18436
  1.3 0.7 %copy-start.3 = (s32[4]{0:T(128)S(1)}, s32[4]{0:T(128)}, u32[]{:S(2)}) copy-start(s32[4]{0:T(128)} %cells_ref.3) | copy-start | bytes 52
  24.3 0.7 %copy-start.1 = (f32[512]{0:T(512)S(1)}, f32[512]{0:T(512)}, u32[]{:S(2)}) copy-start(f32[512]{0:T(512)} %param.8) | copy-start | bytes 6148

commit v2 on v1

v2 whole, which is shorter than its diff:
```python
import functools
import math

import jax
import jax.numpy as jnp
from jax import lax
from jax.experimental import pallas as pl
from jax.experimental.pallas import tpu as pltpu
from jax.sharding import PartitionSpec as P

LANES = 128
SUB = 8
CORE_NEAR = 0.25
CORE_FAR = 9.0
TIME_INCREMENT = 0.25
EXACT = lax.Precision.HIGHEST
VMEM = pl.BlockSpec(memory_space=pltpu.VMEM)
SMEM = pl.BlockSpec(memory_space=pltpu.SMEM)
PARAMS = pltpu.CompilerParams(vmem_limit_bytes=24 * 1024 * 1024)
SYM = ((0, 0), (0, 1), (0, 2), (1, 1), (1, 2), (2, 2))
MOMS = 3 + 9 + 18


def dot_lanes(a, b, precision=EXACT):
    return lax.dot_general(
        a, b, (((1,), (1,)), ((), ())), precision=precision, preferred_element_type=jnp.float32
    )


def center_of(cell):
    slab = jnp.floor(cell * 0.0625)
    rest = cell - 16.0 * slab
    row = jnp.floor(rest * 0.25)
    col = rest - 4.0 * row
    return (4.0 * slab + 2.0, 2.0 * row + 1.0, 2.0 * col + 1.0)


def column_of(values, like):
    index = lax.broadcasted_iota(jnp.int32, like, 0)
    out = jnp.full(like, values[-1], jnp.float32)
    for j, value in enumerate(values[:-1]):
        out = jnp.where(index == j, value, out)
    return out


def moment_row(pos, bur, cells_ref, stack_ref):
    nblk = pos[0].shape[0]
    cell = column_of([cells_ref[b].astype(jnp.float32) for b in range(nblk)], pos[0].shape)
    z = center_of(cell)
    d = [pos[k] - z[k] for k in range(3)]
    dd = [d[a] * d[e] for a, e in SYM]
    stack_ref[...] = jnp.zeros_like(stack_ref)
    m = 0
    for k in range(3):
        stack_ref[m * nblk : (m + 1) * nblk, :] = bur[k]
        m += 1
    for k in range(3):
        for a in range(3):
            stack_ref[m * nblk : (m + 1) * nblk, :] = bur[k] * d[a]
            m += 1
    for k in range(3):
        for j in range(6):
            stack_ref[m * nblk : (m + 1) * nblk, :] = bur[k] * dd[j]
            m += 1
    sums = dot_lanes(jnp.ones((SUB, LANES), jnp.float32), stack_ref[...])[0:1, :]
    lane = lax.broadcasted_iota(jnp.int32, (1, LANES), 1)
    for b in range(nblk):
        sums = jnp.where(lane == MOMS * nblk + b, cells_ref[b].astype(jnp.float32), sums)
    return sums


def spread(out_ref, value):
    count = out_ref.shape[0]

    def put(d, carry):
        out_ref[d] = value
        return carry

    lax.fori_loop(0, count, put, 0, unroll=math.gcd(count, 32))


def first_kernel(
    cells_ref, count_ref, pos_ref, bur_ref, pairs_ref, mob_in_ref, out_ref, mob_ref, stack_ref, load_ref, ids_ref
):
    mob_ref[...] = mob_in_ref[...]
    nblk = cells_ref.shape[0]
    slots = pairs_ref.shape[0]
    pos, bur = [], []
    for k in range(3):
        for b in range(nblk):
            load_ref[k * nblk + b : k * nblk + b + 1, :] = pos_ref[k : k + 1, b * LANES : (b + 1) * LANES]
            load_ref[(3 + k) * nblk + b : (3 + k) * nblk + b + 1, :] = bur_ref[
                k : k + 1, b * LANES : (b + 1) * LANES
            ]
    for k in range(3):
        pos.append(load_ref[k * nblk : (k + 1) * nblk, :])
        bur.append(load_ref[(3 + k) * nblk : (4 + k) * nblk, :])
    base = 6 * nblk
    lane = lax.broadcasted_iota(jnp.int32, (slots, LANES), 1)
    row = lax.broadcasted_iota(jnp.int32, (slots, LANES), 0)
    ids = jnp.where(lane < slots, pairs_ref[:, 0:1], pairs_ref[:, 1:2])
    hit = (lane == row) | (lane == row + slots)
    listed = jnp.sum(jnp.where(hit, ids, 0), axis=0, keepdims=True)
    slot = lax.broadcasted_iota(jnp.int32, (1, LANES), 1)
    slot = jnp.where(slot < slots, slot, slot - slots)
    listed = jnp.where(slot < count_ref[0], listed, -1).astype(jnp.float32)
    load_ref[base : base + 1, :] = listed
    load_ref[base + 1 : base + 2, :] = moment_row(pos, bur, cells_ref, stack_ref)
    rows = base + 2
    for r in range(rows):
        ids_ref[:, r * LANES : (r + 1) * LANES] = load_ref[r : r + 1, :]
    spread(out_ref, ids_ref[...])


def far_into(own_ref, mom_ref, center_ref, acc_ref, nblk, chunks):
    def visit(c, a, first):
        for t in range(LANES // SUB):
            rows = slice(t * SUB, (t + 1) * SUB)

            def mom(m):
                return mom_ref[c, m * nblk : m * nblk + 1, :]

            b = [own_ref[a, 3 + k, rows, :] for k in range(3)]
            r = [own_ref[a, k, rows, :] - center_ref[c, k : k + 1, :] for k in range(3)]
            sq = r[0] * r[0] + r[1] * r[1] + (r[2] * r[2] + CORE_FAR)
            inv = lax.rsqrt(sq)
            inv2 = inv * inv
            inv3 = inv2 * inv
            q0 = b[0] * mom(0) + b[1] * mom(1) + b[2] * mom(2)
            q1 = [b[0] * mom(3 + e) + b[1] * mom(6 + e) + b[2] * mom(9 + e) for e in range(3)]
            q2 = [b[0] * mom(12 + j) + b[1] * mom(18 + j) + b[2] * mom(24 + j) for j in range(6)]
            u = [
                q2[0] * r[0] + q2[1] * r[1] + q2[2] * r[2],
                q2[1] * r[0] + q2[3] * r[1] + q2[4] * r[2],
                q2[2] * r[0] + q2[4] * r[1] + q2[5] * r[2],
            ]
            q1r = q1[0] * r[0] + q1[1] * r[1] + q1[2] * r[2]
            rqr = u[0] * r[0] + u[1] * r[1] + u[2] * r[2]
            trace = q2[0] + q2[3] + q2[5]
            inner = (3.0 * q1r - 0.5 * trace) + (2.5 * rqr) * inv2
            scal = q0 + inner * inv2
            for k in range(3):
                f = (r[k] * scal - (q1[k] + inv2 * u[k])) * inv3
                acc_ref[a, k, rows, :] = f if first else acc_ref[a, k, rows, :] + f

    def start(a, carry):
        visit(0, a, True)
        return carry

    def more(n, carry):
        visit(1 + n // nblk, n % nblk, False)
        return carry

    lax.fori_loop(0, nblk, start, 0)
    if chunks > 1:
        lax.fori_loop(0, nblk * (chunks - 1), more, 0)


def near_into(row_pos, coef_of, own_ref, used_of, acc_ref, nblk):
    for a in range(nblk):

        def visit(n, carry):
            pair = (2 * n, 2 * n + 1)
            p = [[jnp.broadcast_to(row_pos(a, e, k), (SUB, LANES)) for k in range(3)] for e in pair]
            weigh = [coef_of(a, e) for e in pair]
            for t in range(LANES // SUB):
                rows = slice(t * SUB, (t + 1) * SUB)
                own = [own_ref[a, k, rows, :] for k in range(3)]
                f = []
                for j in range(2):
                    r = [own[k] - p[j][k] for k in range(3)]
                    sq = r[0] * r[0] + r[1] * r[1] + (r[2] * r[2] + CORE_NEAR)
                    u = lax.rsqrt(sq)
                    w = lax.rsqrt(sq + (CORE_FAR - CORE_NEAR))
                    wgt = weigh[j](t, rows) * (u * u * u - w * w * w)
                    f.append([wgt * r[k] for k in range(3)])
                for k in range(3):
                    acc_ref[a, k, rows, :] = acc_ref[a, k, rows, :] + (f[0][k] + f[1][k])
            return carry

        lax.fori_loop(0, (used_of(a) + 1) // 2, visit, 0)


def sum_lanes(acc_ref, force_ref, nblk):
    lane = lax.broadcasted_iota(jnp.int32, (SUB, LANES), 1)
    offset = lane - lax.broadcasted_iota(jnp.int32, (SUB, LANES), 0)
    for a in range(nblk):
        for k in range(3):
            out = jnp.zeros((SUB, LANES), jnp.float32)
            for t in range(LANES // SUB):
                total = jnp.sum(acc_ref[a, k, t * SUB : (t + 1) * SUB, :], axis=1, keepdims=True)
                out = jnp.where(offset == t * SUB, total, out)
            force_ref[k * nblk + a : k * nblk + a + 1, :] = jnp.sum(out, axis=0, keepdims=True)


def widen_own(row_of, own_ref, nblk, kinds):
    for a in range(nblk):
        for k in kinds:
            own_ref[a, k] = jnp.transpose(jnp.broadcast_to(row_of(k, a), (LANES, LANES)))


def window_ids(index, my_slab, my_dom, n_slab, n_dom, nblk):
    ids = jnp.full(index.shape, -2.0, jnp.float32)
    for k in range(9):
        s, e = my_slab + k // 3 - 1, my_dom + k % 3 - 1
        inside = (s >= 0) & (s < n_slab) & (e >= 0) & (e < n_dom)
        first = jnp.where(inside, (s * n_dom + e) * nblk - k * nblk, -100000)
        here = (index >= k * nblk) & (index < (k + 1) * nblk)
        ids = jnp.where(here, (index + first).astype(jnp.float32), ids)
    return ids


def build_lists(got_ref, rows, nblk, my_slab, my_dom, n_slab, n_dom, count_ref, list_ref, mult_ref):
    base = 6 * nblk
    high = -(-9 * nblk // SUB) * SUB
    place = (my_slab, my_dom, n_slab, n_dom, nblk)
    gid = window_ids(lax.broadcasted_iota(jnp.int32, (high, LANES), 0), *place)
    own = (my_slab * n_dom + my_dom) * nblk
    sub = lax.broadcasted_iota(jnp.int32, (SUB, LANES), 0)
    lane = lax.broadcasted_iota(jnp.int32, (SUB, LANES), 1)
    mine = jnp.where(sub < nblk, sub + own, -3).astype(jnp.float32)
    total = jnp.zeros((SUB, high), jnp.float32)
    for k in range(9):
        s, e = my_slab + k // 3 - 1, my_dom + k % 3 - 1
        inside = (s >= 0) & (s < n_slab) & (e >= 0) & (e < n_dom)
        dev = jnp.clip(s, 0, n_slab - 1) * n_dom + jnp.clip(e, 0, n_dom - 1)
        row = jnp.where(inside, got_ref[dev * rows + base], -1.0)
        other = pltpu.roll(row, LANES // 2, 1)
        left = (mine == row).astype(jnp.float32)
        right = (gid == other).astype(jnp.float32)
        total = total + dot_lanes(left, right, None)
    count_ref[...] = jnp.zeros_like(count_ref)
    count_ref[:, 0:high] = total
    count = count_ref[...]
    met = jnp.where(count > 0.5, 1.0, 0.0)
    before = lax.broadcasted_iota(jnp.int32, (LANES, LANES), 1) < lax.broadcasted_iota(
        jnp.int32, (LANES, LANES), 0
    )
    rank = dot_lanes(met, before.astype(jnp.float32), None)
    used = jnp.sum(met, axis=1, keepdims=True).astype(jnp.int32)
    list_ref[...] = jnp.where(lane == LANES - 1, used, 0)
    mult_ref[...] = jnp.zeros_like(mult_ref)
    line = window_ids(lane, *place)
    spot = lax.broadcasted_iota(jnp.int32, (high, LANES), 0).astype(jnp.float32)
    for a in range(nblk):
        pick = (rank[a : a + 1, :] == spot) & (met[a : a + 1, :] > 0.5)
        what = jnp.where(sub == 0, line, jnp.where(sub == 1, count[a : a + 1, :], 0.0))
        out = dot_lanes(what, pick.astype(jnp.float32))
        list_ref[a : a + 1, 0:high] = (out[0:1, :] + 0.5).astype(jnp.int32)
        mult_ref[a : a + 1, 0:high] = out[1:2, :]


def gather_moments(got_ref, rows, mom_ref, center_ref, take_ref, nblk, ndev, far_scale):
    width = LANES // nblk
    for c in range(ndev // width):

        def take(d, carry):
            take_ref[pl.ds(d, 1), :] = got_ref[(c * width + d) * rows + rows - 1]
            return carry

        lax.fori_loop(0, width, take, 0, unroll=True)
        block = take_ref[...]
        turned = [block] + [pltpu.roll(block, LANES - b, 1) for b in range(1, nblk)]
        flat = jnp.transpose(jnp.concatenate(turned, axis=0))
        z = center_of(flat[MOMS * nblk : MOMS * nblk + 1, :])
        for k in range(3):
            center_ref[c, k : k + 1, :] = z[k]
        row = lax.broadcasted_iota(jnp.int32, (LANES, LANES), 0)
        mom_ref[c] = flat * jnp.where(row < 12 * nblk, far_scale, 3.0 * far_scale)


def second_kernel(
    n_slab, n_dom, far_scale,
    cells_ref, mob_ref, got_ref,
    out_ref, vel_ref, list_ref, coef_ref,
    stack_ref, own_ref, acc_ref, force_ref, mom_ref, center_ref, take_ref,
    count_ref, mult_ref, next_ref, flat_ref, list_smem, mult_smem, sem,
):
    nblk = cells_ref.shape[0]
    ndev = n_slab * n_dom
    rows = got_ref.shape[0] // ndev
    each = coef_ref.shape[0] // nblk
    my_slab, my_dom = lax.axis_index("slab"), lax.axis_index("dom")
    me = my_slab * n_dom + my_dom

    def own_row(k, b):
        return got_ref[me * rows + k * nblk + b]

    def block_row(g, k):
        return got_ref[(g // nblk) * rows + g % nblk + k * nblk]

    def coef_of(a, e):
        g, mult = list_smem[a, e], mult_smem[a, e]
        c = [jnp.broadcast_to(block_row(g, 3 + k) * mult, (SUB, LANES)) for k in range(3)]

        def tile(t, rows):
            value = (
                own_ref[a, 3, rows, :] * c[0] + own_ref[a, 4, rows, :] * c[1] + own_ref[a, 5, rows, :] * c[2]
            )
            coef_ref[a * each + e, rows, :] = value
            return value

        return tile

    build_lists(got_ref, rows, nblk, my_slab, my_dom, n_slab, n_dom, count_ref, list_ref, mult_ref)
    copies = [
        pltpu.make_async_copy(list_ref, list_smem, sem.at[0]),
        pltpu.make_async_copy(mult_ref, mult_smem, sem.at[1]),
    ]
    for copy in copies:
        copy.start()
    gather_moments(got_ref, rows, mom_ref, center_ref, take_ref, nblk, ndev, far_scale)
    widen_own(own_row, own_ref, nblk, range(6))
    far_into(own_ref, mom_ref, center_ref, acc_ref, nblk, mom_ref.shape[0])
    for copy in copies:
        copy.wait()
    near_into(
        lambda a, e, k: block_row(list_smem[a, e], k), coef_of, own_ref,
        lambda a: list_smem[a, LANES - 1], acc_ref, nblk,
    )
    sum_lanes(acc_ref, force_ref, nblk)
    pos, bur = [], []
    for k in range(3):
        here = slice(k * nblk, (k + 1) * nblk)
        vel = mob_ref[...] * force_ref[here, :]
        vel_ref[here, :] = vel
        for b in range(nblk):
            next_ref[k * nblk + b : k * nblk + b + 1, :] = own_row(k, b)
            next_ref[(3 + k) * nblk + b : (3 + k) * nblk + b + 1, :] = own_row(3 + k, b)
        moved = next_ref[here, :] + TIME_INCREMENT * vel
        next_ref[here, :] = moved
        pos.append(moved)
        bur.append(next_ref[(3 + k) * nblk : (4 + k) * nblk, :])
    last = moment_row(pos, bur, cells_ref, stack_ref)
    for r in range(3 * nblk):
        flat_ref[:, r * LANES : (r + 1) * LANES] = next_ref[r : r + 1, :]
    flat_ref[:, 3 * nblk * LANES :] = last
    spread(out_ref, flat_ref[...])


def third_kernel(
    n_slab, n_dom, far_scale,
    list_smem, mob_ref, pos_ref, vel_ref, old_ref, got_ref, coef_ref,
    moved_ref, velocity_ref,
    own_ref, acc_ref, force_ref, mom_ref, center_ref, take_ref,
):
    nblk = mob_ref.shape[0]
    ndev = n_slab * n_dom
    rows = got_ref.shape[0] // ndev
    old_rows = old_ref.shape[0] // ndev
    each = coef_ref.shape[0] // nblk
    me = lax.axis_index("slab") * n_dom + lax.axis_index("dom")

    def row_of(k, b):
        if k < 3:
            return got_ref[me * rows + k * nblk + b]
        return old_ref[me * old_rows + k * nblk + b]

    def block_row(a, e, k):
        g = list_smem[a, e]
        return got_ref[(g // nblk) * rows + g % nblk + k * nblk]

    def coef_of(a, e):
        return lambda t, rows: coef_ref[a * each + e, rows, :]

    gather_moments(got_ref, rows, mom_ref, center_ref, take_ref, nblk, ndev, far_scale)
    widen_own(row_of, own_ref, nblk, range(6))
    far_into(own_ref, mom_ref, center_ref, acc_ref, nblk, mom_ref.shape[0])
    near_into(block_row, coef_of, own_ref, lambda a: list_smem[a, LANES - 1], acc_ref, nblk)
    sum_lanes(acc_ref, force_ref, nblk)
    for k in range(3):
        here = slice(k * nblk, (k + 1) * nblk)
        force_ref[here, :] = 0.5 * (vel_ref[here, :] + mob_ref[...] * force_ref[here, :])
        for b in range(nblk):
            lanes = slice(b * LANES, (b + 1) * LANES)
            mean = force_ref[k * nblk + b : k * nblk + b + 1, :]
            velocity_ref[k : k + 1, lanes] = mean
            moved_ref[k : k + 1, lanes] = pos_ref[k : k + 1, lanes] + TIME_INCREMENT * mean


def body(positions, burgers, mobility, block_cells, pairs, pair_count):
    f32 = jnp.float32
    segs = positions.shape[1]
    nblk = block_cells.shape[0]
    n_slab, n_dom = lax.axis_size("slab"), lax.axis_size("dom")
    ndev = n_slab * n_dom
    far_scale = math.sqrt(16 * n_slab / (segs * ndev))
    rows, rows2 = 6 * nblk + 2, 3 * nblk + 1
    each = 9 * nblk + 2
    chunks = ndev * nblk // LANES
    high = -(-(3 * nblk) // SUB) * SUB
    scratch = [
        pltpu.VMEM((nblk, 6, LANES, LANES), f32),
        pltpu.VMEM((nblk, 3, LANES, LANES), f32),
        pltpu.VMEM((high, LANES), f32),
        pltpu.VMEM((chunks, LANES, LANES), f32),
        pltpu.VMEM((chunks, SUB, LANES), f32),
        pltpu.VMEM((LANES // nblk, LANES), f32),
    ]
    load, mob = pl.pallas_call(
        first_kernel,
        out_shape=(
            jax.ShapeDtypeStruct((ndev, 1, rows * LANES), f32),
            jax.ShapeDtypeStruct((nblk, LANES), f32),
        ),
        in_specs=[SMEM, SMEM, VMEM, VMEM, VMEM, VMEM],
        out_specs=(VMEM, VMEM),
        scratch_shapes=[
            pltpu.VMEM((LANES, LANES), f32),
            pltpu.VMEM((-(-rows // SUB) * SUB, LANES), f32),
            pltpu.VMEM((1, rows * LANES), f32),
        ],
        compiler_params=PARAMS,
        name="pack",
    )(block_cells, pair_count, positions, burgers, pairs, mobility.reshape(nblk, LANES))
    got = lax.all_to_all(load, ("slab", "dom"), 0, 0, tiled=True).reshape(ndev * rows, 1, LANES)
    load2, vel, lists, coef = pl.pallas_call(
        functools.partial(second_kernel, n_slab, n_dom, far_scale),
        out_shape=(
            jax.ShapeDtypeStruct((ndev, 1, rows2 * LANES), f32),
            jax.ShapeDtypeStruct((3 * nblk, LANES), f32),
            jax.ShapeDtypeStruct((SUB, LANES), jnp.int32),
            jax.ShapeDtypeStruct((nblk * each, LANES, LANES), f32),
        ),
        in_specs=[SMEM, VMEM, VMEM],
        out_specs=(VMEM, VMEM, VMEM, VMEM),
        scratch_shapes=[pltpu.VMEM((LANES, LANES), f32)]
        + scratch
        + [
            pltpu.VMEM((SUB, LANES), f32),
            pltpu.VMEM((SUB, LANES), f32),
            pltpu.VMEM((6 * nblk, LANES), f32),
            pltpu.VMEM((1, rows2 * LANES), f32),
            pltpu.SMEM((SUB, LANES), jnp.int32),
            pltpu.SMEM((SUB, LANES), f32),
            pltpu.SemaphoreType.DMA((2,)),
        ],
        compiler_params=PARAMS,
        name="step_one",
    )(block_cells, mob, got)
    got2 = lax.all_to_all(load2, ("slab", "dom"), 0, 0, tiled=True).reshape(ndev * rows2, 1, LANES)
    return pl.pallas_call(
        functools.partial(third_kernel, n_slab, n_dom, far_scale),
        out_shape=(jax.ShapeDtypeStruct((3, segs), f32),) * 2,
        in_specs=[SMEM, VMEM, VMEM, VMEM, VMEM, VMEM, VMEM],
        out_specs=(VMEM, VMEM),
        scratch_shapes=scratch,
        compiler_params=PARAMS,
        name="step_two",
    )(lists, mob, positions, vel, got, got2, coef)


def solution(mesh):
    placed = (
        P(None, ("slab", "dom")),
        P(None, ("slab", "dom")),
        P(("slab", "dom")),
        P(("slab", "dom")),
        P(("slab", "dom"), None),
        P(("slab", "dom")),
    )
    return jax.shard_map(
        body,
        mesh=mesh,
        in_specs=placed,
        out_specs=(P(None, ("slab", "dom")), P(None, ("slab", "dom"))),
        check_vma=False,
    )
```

time: 57.8 us -> 52.5 us (0.908); the launches traced: 57.5 us -> 51.5 us
  Pallas kernels: 20 us -> 11.1 us
  local copies, waits for them, and re-layouts: 1.39 us -> 4.19 us
    pallas_call x1, Pallas kernels: 10.5 us -> 5.25 us  [body(): pl.pallas_call(functools.partial(second_kernel, n_slab, n_dom, far_scale)...]
    pallas_call x1, Pallas kernels: 8.69 us -> 5.06 us  [body(): pl.pallas_call(functools.partial(third_kernel, n_slab, n_dom, far_scale),...]
    unnamed x11, local copies, waits for them, and re-layouts: 1.39 us -> 4.19 us
where the time goes in v2:
time: 52.5 us; the launch traced here: 51.5 us
  blocking collectives  34.9 us (66%)
  Pallas kernels  11.1 us (21%)
  local copies, waits for them, and re-layouts  4.19 us (8%)
  between operations  1.3 us (2%)
    all_to_all x1, blocking collectives, body(): lax.all_to_all(load, ('slab', 'dom'), 0, 0, tiled=True)  21.4 us
    all_to_all x1, blocking collectives, body(): lax.all_to_all(load2, ('slab', 'dom'), 0, 0, tiled=True)  13.5 us
    pallas_call x1, Pallas kernels, body(): pl.pallas_call(functools.partial(second_kernel, n_slab, n_dom, far_scale)...  5.25 us
    pallas_call x1, Pallas kernels, body(): pl.pallas_call(functools.partial(third_kernel, n_slab, n_dom, far_scale),...  5.06 us
    unnamed x11, local copies, waits for them, and re-layouts  4.19 us

profile of v2, /device:TPU:0, one launch (start us, length us, event | category | flops | bytes accessed | tf_op | source)
XLA Modules:
  0.0 51.5 jit_solution(4005183044535279331)
XLA Ops:
  1.3 0.8 %copy.8.pairs_ref = s32[64,2]{1,0:T(8,128)S(1)} copy(s32[64,2]{0,1:T(2,128)} %param.10) | data formatting | bytes 1024 | tf_op args[4]
  2.0 0.0 copy-start
  2.0 0.7 %copy-done = f32[3,512]{1,0:T(4,128)S(1)} copy-done((f32[3,512]{1,0:T(4,128)S(1)}, f32[3,512]{1,0:T(4,128)}, u32[]{:S(2)}) %copy-start) | copy-done | bytes 6168
  2.7 0.0 copy-start.2
  2.7 0.7 %copy-done.2 = f32[3,512]{1,0:T(4,128)S(1)} copy-done((f32[3,512]{1,0:T(4,128)S(1)}, f32[3,512]{1,0:T(4,128)}, u32[]{:S(2)}) %copy-start.2) | copy-done | bytes 6168
  3.4 0.0 copy-start.3
  3.4 0.7 %copy-done.3 = s32[4]{0:T(128)S(1)} copy-done((s32[4]{0:T(128)S(1)}, s32[4]{0:T(128)}, u32[]{:S(2)}) %copy-start.3) | copy-done | bytes 40
  4.1 0.0 copy-start.4
  4.1 0.7 %copy-done.4 = f32[512]{0:T(512)S(1)} copy-done((f32[512]{0:T(512)S(1)}, f32[512]{0:T(512)}, u32[]{:S(2)}) %copy-start.4) | copy-done | bytes 2072
  4.8 0.8 %pack.1 = (f32[32,1,3328]{2,1,0:T(1,128)S(1)}, f32[4,128]{1,0:T(4,128)S(1)}) custom-call(s32[4]{0:T(128)S(1)} %copy-done.3, s32[1]{0:T(128)S(6)} %copy.9.count_ref, f32[3,512]{1,0:T(4,128)S(1)} %copy-done, f32[3,512]{1,0:T(4,128)S(1)} %copy-done.2, s32[64,2]{1,0:T(8,128)S(1)} %copy.8.pairs_ref, f32[4,128]{1,0:T(4,128)S(1)} %bitcast.6), custom_call_target="tpu_custom_call" | custom-call | tf_op jit(solution)/shard_map/pack/pallas_call | solution.py:400
  5.6 21.4 %all_to_all.10 = f32[32,1,3328]{2,1,0:T(1,128)S(1)} all-to-all(f32[32,1,3328]{2,1,0:T(1,128)S(1)} %get-tuple-element.9), channel_id=1, replica_groups=mesh['slab'=8,'dom'=4] {'slab','dom'}, dimensions={0} | all-to-all | bytes 851968 | tf_op jit(solution)/shard_map/all_to_all | solution.py:416
  27.0 5.3 %step_one.1 = (f32[32,1,1664]{2,1,0:T(1,128)S(1)}, f32[12,128]{1,0:T(8,128)S(1)}, s32[8,128]{1,0:T(8,128)S(1)}, f32[152,128,128]{2,1,0:T(8,128)S(1)}) custom-call(s32[4]{0:T(128)S(1)} %copy-done.3, f32[4,128]{1,0:T(4,128)S(1)} %get-tuple-element.8.mob_ref, f32[832,1,128]{2,1,0:T(1,128)S(1)} %bitcast.3), custom_call_target="tpu_custom_call" | custom-call | tf_op jit(solution)/shard_map/step_one/pallas_call | solution.py:417
  32.3 13.5 %all_to_all.11 = f32[32,1,1664]{2,1,0:T(1,128)S(1)} all-to-all(f32[32,1,1664]{2,1,0:T(1,128)S(1)} %get-tuple-element.12), channel_id=1, replica_groups=mesh['slab'=8,'dom'=4] {'slab','dom'}, dimensions={0} | all-to-all | bytes 425984 | tf_op jit(solution)/shard_map/all_to_all | solution.py:441
  45.8 0.0 copy-start.1
  45.8 0.7 %copy-done.1 = f32[3,512]{1,0:T(4,128)S(1)} copy-done((f32[3,512]{1,0:T(4,128)S(1)}, f32[3,512]{1,0:T(4,128)}, u32[]{:S(2)}) %copy-start.1) | copy-done | bytes 6168
  46.5 5.1 %step_two.1 = (f32[3,512]{1,0:T(4,128)}, f32[3,512]{1,0:T(4,128)}) custom-call(s32[8,128]{1,0:T(8,128)S(1)} %get-tuple-element.10.list_smem, f32[4,128]{1,0:T(4,128)S(1)} %get-tuple-element.8.mob_ref, f32[3,512]{1,0:T(4,128)S(1)} %copy-done.1, f32[12,128]{1,0:T(8,128)S(1)} %get-tuple-element.11.vel_ref, f32[832,1,128]{2,1,0:T(1,128)S(1)} %bitcast.4, ...), custom_call_target="tpu_custom_call" | custom-call | tf_op jit(solution)/shard_map/step_two/pallas_call | solution.py:442
Async XLA Ops:
  2.0 0.7 %copy-start = (f32[3,512]{1,0:T(4,128)S(1)}, f32[3,512]{1,0:T(4,128)}, u32[]{:S(2)}) copy-start(f32[3,512]{1,0:T(4,128)} %pos_ref.3) | copy-start | bytes 18436
  2.7 0.7 %copy-start.2 = (f32[3,512]{1,0:T(4,128)S(1)}, f32[3,512]{1,0:T(4,128)}, u32[]{:S(2)}) copy-start(f32[3,512]{1,0:T(4,128)} %bur_ref.1) | copy-start | bytes 18436
  3.4 0.7 %copy-start.3 = (s32[4]{0:T(128)S(1)}, s32[4]{0:T(128)}, u32[]{:S(2)}) copy-start(s32[4]{0:T(128)} %cells_ref.3) | copy-start | bytes 52
  4.1 0.7 %copy-start.4 = (f32[512]{0:T(512)S(1)}, f32[512]{0:T(512)}, u32[]{:S(2)}) copy-start(f32[512]{0:T(512)} %param.8) | copy-start | bytes 6148
  45.8 0.7 %copy-start.1 = (f32[3,512]{1,0:T(4,128)S(1)}, f32[3,512]{1,0:T(4,128)}, u32[]{:S(2)}) copy-start(f32[3,512]{1,0:T(4,128)} %pos_ref.3) | copy-start | bytes 18436

commit v3 on v2

--- a/solution.py
+++ b/solution.py
@@ -7,6 +7,7 @@
 from jax.experimental import pallas as pl
 from jax.experimental.pallas import tpu as pltpu
 from jax.sharding import PartitionSpec as P
+
 
 LANES = 128
 SUB = 8
@@ -16,7 +17,8 @@
 EXACT = lax.Precision.HIGHEST
 VMEM = pl.BlockSpec(memory_space=pltpu.VMEM)
 SMEM = pl.BlockSpec(memory_space=pltpu.SMEM)
-PARAMS = pltpu.CompilerParams(vmem_limit_bytes=24 * 1024 * 1024)
+HBM = pl.BlockSpec(memory_space=pltpu.HBM)
+PARAMS = pltpu.CompilerParams(vmem_limit_bytes=8 * 1024 * 1024)
 SYM = ((0, 0), (0, 1), (0, 2), (1, 1), (1, 2), (2, 2))
 MOMS = 3 + 9 + 18
 
@@ -80,39 +82,45 @@
 
 
 def first_kernel(
-    cells_ref, count_ref, pos_ref, bur_ref, pairs_ref, mob_in_ref, out_ref, mob_ref, stack_ref, load_ref, ids_ref
+    count_ref, cells_hbm, pos_hbm, bur_hbm, pairs_hbm, mob_hbm,
+    out_ref, win_ref, mob_ref, cells_out_ref,
+    pos_ref, bur_ref, pairs_ref, cells_ref, stack_ref, load_ref, flat_ref, ids_ref, sem,
 ):
-    mob_ref[...] = mob_in_ref[...]
+    moves = (
+        (cells_hbm, cells_ref), (pos_hbm, pos_ref), (bur_hbm, bur_ref),
+        (pairs_hbm, pairs_ref), (mob_hbm, mob_ref), (cells_hbm, cells_out_ref),
+    )
+    copies = [pltpu.make_async_copy(src, dst, sem.at[j]) for j, (src, dst) in enumerate(moves)]
+    for copy in copies:
+        copy.start()
+    for copy in copies:
+        copy.wait()
     nblk = cells_ref.shape[0]
-    slots = pairs_ref.shape[0]
+    slots = pairs_ref.shape[1]
     pos, bur = [], []
     for k in range(3):
         for b in range(nblk):
-            load_ref[k * nblk + b : k * nblk + b + 1, :] = pos_ref[k : k + 1, b * LANES : (b + 1) * LANES]
-            load_ref[(3 + k) * nblk + b : (3 + k) * nblk + b + 1, :] = bur_ref[
-                k : k + 1, b * LANES : (b + 1) * LANES
-            ]
+            lanes = slice(b * LANES, (b + 1) * LANES)
+            load_ref[k * nblk + b : k * nblk + b + 1, :] = pos_ref[k : k + 1, lanes]
+            load_ref[(3 + k) * nblk + b : (3 + k) * nblk + b + 1, :] = bur_ref[k : k + 1, lanes]
     for k in range(3):
         pos.append(load_ref[k * nblk : (k + 1) * nblk, :])
         bur.append(load_ref[(3 + k) * nblk : (4 + k) * nblk, :])
-    base = 6 * nblk
-    lane = lax.broadcasted_iota(jnp.int32, (slots, LANES), 1)
-    row = lax.broadcasted_iota(jnp.int32, (slots, LANES), 0)
-    ids = jnp.where(lane < slots, pairs_ref[:, 0:1], pairs_ref[:, 1:2])
-    hit = (lane == row) | (lane == row + slots)
-    listed = jnp.sum(jnp.where(hit, ids, 0), axis=0, keepdims=True)
+    ids_ref[0:1, 0:slots] = pairs_ref[0:1, :]
+    ids_ref[0:1, slots : 2 * slots] = pairs_ref[1:2, :]
     slot = lax.broadcasted_iota(jnp.int32, (1, LANES), 1)
     slot = jnp.where(slot < slots, slot, slot - slots)
-    listed = jnp.where(slot < count_ref[0], listed, -1).astype(jnp.float32)
-    load_ref[base : base + 1, :] = listed
-    load_ref[base + 1 : base + 2, :] = moment_row(pos, bur, cells_ref, stack_ref)
-    rows = base + 2
-    for r in range(rows):
-        ids_ref[:, r * LANES : (r + 1) * LANES] = load_ref[r : r + 1, :]
-    spread(out_ref, ids_ref[...])
-
-
-def far_into(own_ref, mom_ref, center_ref, acc_ref, nblk, chunks):
+    listed = jnp.where(slot < count_ref[0], ids_ref[0:1, :], -1).astype(jnp.float32)
+    for r in range(3 * nblk):
+        lanes = slice(r * LANES, (r + 1) * LANES)
+        flat_ref[:, lanes] = load_ref[r : r + 1, :]
+        win_ref[0, :, lanes] = load_ref[3 * nblk + r : 3 * nblk + r + 1, :]
+    win_ref[0, :, 3 * nblk * LANES :] = listed
+    flat_ref[:, 3 * nblk * LANES :] = moment_row(pos, bur, cells_ref, stack_ref)
+    spread(out_ref, flat_ref[...])
+
+
+def far_into(own_ref, bur_ref, mom_ref, center_ref, acc_ref, nblk, chunks):
     def visit(c, a, first):
         for t in range(LANES // SUB):
             rows = slice(t * SUB, (t + 1) * SUB)
@@ -120,7 +128,7 @@
             def mom(m):
                 return mom_ref[c, m * nblk : m * nblk + 1, :]
 
-            b = [own_ref[a, 3 + k, rows, :] for k in range(3)]
+            b = [bur_ref[a, k, rows, :] for k in range(3)]
             r = [own_ref[a, k, rows, :] - center_ref[c, k : k + 1, :] for k in range(3)]
             sq = r[0] * r[0] + r[1] * r[1] + (r[2] * r[2] + CORE_FAR)
             inv = lax.rsqrt(sq)
@@ -193,16 +201,16 @@
             force_ref[k * nblk + a : k * nblk + a + 1, :] = jnp.sum(out, axis=0, keepdims=True)
 
 
-def widen_own(row_of, own_ref, nblk, kinds):
+def widen_own(row_of, own_ref, nblk):
     for a in range(nblk):
-        for k in kinds:
+        for k in range(3):
             own_ref[a, k] = jnp.transpose(jnp.broadcast_to(row_of(k, a), (LANES, LANES)))
 
 
 def window_ids(index, my_slab, my_dom, n_slab, n_dom, nblk):
     ids = jnp.full(index.shape, -2.0, jnp.float32)
     for k in range(9):
-        s, e = my_slab + k // 3 - 1, my_dom + k % 3 - 1
+        s, e = my_slab + k % 3 - 1, my_dom + k // 3 - 1
         inside = (s >= 0) & (s < n_slab) & (e >= 0) & (e < n_dom)
         first = jnp.where(inside, (s * n_dom + e) * nblk - k * nblk, -100000)
         here = (index >= k * nblk) & (index < (k + 1) * nblk)
@@ -210,8 +218,7 @@
     return ids
 
 
-def build_lists(got_ref, rows, nblk, my_slab, my_dom, n_slab, n_dom, count_ref, list_ref, mult_ref):
-    base = 6 * nblk
+def build_lists(win_ref, rows, nblk, my_slab, my_dom, n_slab, n_dom, count_ref, list_ref, mult_ref):
     high = -(-9 * nblk // SUB) * SUB
     place = (my_slab, my_dom, n_slab, n_dom, nblk)
     gid = window_ids(lax.broadcasted_iota(jnp.int32, (high, LANES), 0), *place)
@@ -221,10 +228,9 @@
     mine = jnp.where(sub < nblk, sub + own, -3).astype(jnp.float32)
     total = jnp.zeros((SUB, high), jnp.float32)
     for k in range(9):
-        s, e = my_slab + k // 3 - 1, my_dom + k % 3 - 1
+        s, e = my_slab + k % 3 - 1, my_dom + k // 3 - 1
         inside = (s >= 0) & (s < n_slab) & (e >= 0) & (e < n_dom)
-        dev = jnp.clip(s, 0, n_slab - 1) * n_dom + jnp.clip(e, 0, n_dom - 1)
-        row = jnp.where(inside, got_ref[dev * rows + base], -1.0)
+        row = jnp.where(inside, win_ref[k * rows + rows - 1], -1.0)
         other = pltpu.roll(row, LANES // 2, 1)
         left = (mine == row).astype(jnp.float32)
         right = (gid == other).astype(jnp.float32)
@@ -241,13 +247,15 @@
     list_ref[...] = jnp.where(lane == LANES - 1, used, 0)
     mult_ref[...] = jnp.zeros_like(mult_ref)
     line = window_ids(lane, *place)
+    here = lane.astype(jnp.float32)
     spot = lax.broadcasted_iota(jnp.int32, (high, LANES), 0).astype(jnp.float32)
     for a in range(nblk):
         pick = (rank[a : a + 1, :] == spot) & (met[a : a + 1, :] > 0.5)
-        what = jnp.where(sub == 0, line, jnp.where(sub == 1, count[a : a + 1, :], 0.0))
+        what = jnp.where(sub == 0, line, jnp.where(sub == 1, count[a : a + 1, :], here))
         out = dot_lanes(what, pick.astype(jnp.float32))
         list_ref[a : a + 1, 0:high] = (out[0:1, :] + 0.5).astype(jnp.int32)
         mult_ref[a : a + 1, 0:high] = out[1:2, :]
+        list_ref[nblk + a : nblk + a + 1, 0:high] = (out[2:3, :] + 0.5).astype(jnp.int32)
 
 
 def gather_moments(got_ref, rows, mom_ref, center_ref, take_ref, nblk, ndev, far_scale):
@@ -271,10 +279,10 @@
 
 def second_kernel(
     n_slab, n_dom, far_scale,
-    cells_ref, mob_ref, got_ref,
-    out_ref, vel_ref, list_ref, coef_ref,
+    cells_ref, mob_ref, got_ref, low_ref, mid_ref, high_ref,
+    out_ref, vel_ref, list_ref, coef_ref, wide_ref, moved_ref,
     stack_ref, own_ref, acc_ref, force_ref, mom_ref, center_ref, take_ref,
-    count_ref, mult_ref, next_ref, flat_ref, list_smem, mult_smem, sem,
+    win_ref, count_ref, mult_ref, next_ref, flat_ref, list_smem, mult_smem, sem,
 ):
     nblk = cells_ref.shape[0]
     ndev = n_slab * n_dom
@@ -282,27 +290,34 @@
     each = coef_ref.shape[0] // nblk
     my_slab, my_dom = lax.axis_index("slab"), lax.axis_index("dom")
     me = my_slab * n_dom + my_dom
+    third = low_ref.shape[0]
+    places = third // 3
+    for j, ref in enumerate((low_ref, mid_ref, high_ref)):
+        win_ref[j * third : (j + 1) * third] = ref[...]
 
     def own_row(k, b):
         return got_ref[me * rows + k * nblk + b]
 
-    def block_row(g, k):
+    def own_bur(k, b):
+        return win_ref[4 * places + k * nblk + b]
+
+    def block_row(a, e, k):
+        g = list_smem[a, e]
         return got_ref[(g // nblk) * rows + g % nblk + k * nblk]
 
     def coef_of(a, e):
-        g, mult = list_smem[a, e], mult_smem[a, e]
-        c = [jnp.broadcast_to(block_row(g, 3 + k) * mult, (SUB, LANES)) for k in range(3)]
+        w, mult = list_smem[nblk + a, e], mult_smem[a, e]
+        first = (w // nblk) * places + w % nblk
+        c = [jnp.broadcast_to(win_ref[first + k * nblk] * mult, (SUB, LANES)) for k in range(3)]
 
         def tile(t, rows):
-            value = (
-                own_ref[a, 3, rows, :] * c[0] + own_ref[a, 4, rows, :] * c[1] + own_ref[a, 5, rows, :] * c[2]
-            )
+            value = wide_ref[a, 0, rows, :] * c[0] + wide_ref[a, 1, rows, :] * c[1] + wide_ref[a, 2, rows, :] * c[2]
             coef_ref[a * each + e, rows, :] = value
             return value
 
         return tile
 
-    build_lists(got_ref, rows, nblk, my_slab, my_dom, n_slab, n_dom, count_ref, list_ref, mult_ref)
+    build_lists(win_ref, places, nblk, my_slab, my_dom, n_slab, n_dom, count_ref, list_ref, mult_ref)
     copies = [
         pltpu.make_async_copy(list_ref, list_smem, sem.at[0]),
         pltpu.make_async_copy(mult_ref, mult_smem, sem.at[1]),
@@ -310,14 +325,12 @@
     for copy in copies:
         copy.start()
     gather_moments(got_ref, rows, mom_ref, center_ref, take_ref, nblk, ndev, far_scale)
-    widen_own(own_row, own_ref, nblk, range(6))
-    far_into(own_ref, mom_ref, center_ref, acc_ref, nblk, mom_ref.shape[0])
+    widen_own(own_row, own_ref, nblk)
+    widen_own(own_bur, wide_ref, nblk)
+    far_into(own_ref, wide_ref, mom_ref, center_ref, acc_ref, nblk, mom_ref.shape[0])
     for copy in copies:
         copy.wait()
-    near_into(
-        lambda a, e, k: block_row(list_smem[a, e], k), coef_of, own_ref,
-        lambda a: list_smem[a, LANES - 1], acc_ref, nblk,
-    )
+    near_into(block_row, coef_of, own_ref, lambda a: list_smem[a, LANES - 1], acc_ref, nblk)
     sum_lanes(acc_ref, force_ref, nblk)
     pos, bur = [], []
     for k in range(3):
@@ -326,35 +339,29 @@
         vel_ref[here, :] = vel
         for b in range(nblk):
             next_ref[k * nblk + b : k * nblk + b + 1, :] = own_row(k, b)
-            next_ref[(3 + k) * nblk + b : (3 + k) * nblk + b + 1, :] = own_row(3 + k, b)
+            next_ref[(3 + k) * nblk + b : (3 + k) * nblk + b + 1, :] = own_bur(k, b)
         moved = next_ref[here, :] + TIME_INCREMENT * vel
-        next_ref[here, :] = moved
+        moved_ref[here, :] = moved
         pos.append(moved)
         bur.append(next_ref[(3 + k) * nblk : (4 + k) * nblk, :])
     last = moment_row(pos, bur, cells_ref, stack_ref)
     for r in range(3 * nblk):
-        flat_ref[:, r * LANES : (r + 1) * LANES] = next_ref[r : r + 1, :]
+        flat_ref[:, r * LANES : (r + 1) * LANES] = moved_ref[r : r + 1, :]
     flat_ref[:, 3 * nblk * LANES :] = last
     spread(out_ref, flat_ref[...])
 
 
 def third_kernel(
     n_slab, n_dom, far_scale,
-    list_smem, mob_ref, pos_ref, vel_ref, old_ref, got_ref, coef_ref,
+    list_smem, mob_ref, vel_ref, old_ref, got_ref, coef_ref, wide_ref, next_ref,
     moved_ref, velocity_ref,
     own_ref, acc_ref, force_ref, mom_ref, center_ref, take_ref,
 ):
     nblk = mob_ref.shape[0]
     ndev = n_slab * n_dom
     rows = got_ref.shape[0] // ndev
-    old_rows = old_ref.shape[0] // ndev
     each = coef_ref.shape[0] // nblk
     me = lax.axis_index("slab") * n_dom + lax.axis_index("dom")
-
-    def row_of(k, b):
-        if k < 3:
-            return got_ref[me * rows + k * nblk + b]
-        return old_ref[me * old_rows + k * nblk + b]
 
     def block_row(a, e, k):
         g = list_smem[a, e]
@@ -363,9 +370,9 @@
     def coef_of(a, e):
         return lambda t, rows: coef_ref[a * each + e, rows, :]
 
+    widen_own(lambda k, b: next_ref[k * nblk + b : k * nblk + b + 1, :], own_ref, nblk)
     gather_moments(got_ref, rows, mom_ref, center_ref, take_ref, nblk, ndev, far_scale)
-    widen_own(row_of, own_ref, nblk, range(6))
-    far_into(own_ref, mom_ref, center_ref, acc_ref, nblk, mom_ref.shape[0])
+    far_into(own_ref, wide_ref, mom_ref, center_ref, acc_ref, nblk, mom_ref.shape[0])
     near_into(block_row, coef_of, own_ref, lambda a: list_smem[a, LANES - 1], acc_ref, nblk)
     sum_lanes(acc_ref, force_ref, nblk)
     for k in range(3):
@@ -375,79 +382,109 @@
             lanes = slice(b * LANES, (b + 1) * LANES)
             mean = force_ref[k * nblk + b : k * nblk + b + 1, :]
             velocity_ref[k : k + 1, lanes] = mean
-            moved_ref[k : k + 1, lanes] = pos_ref[k : k + 1, lanes] + TIME_INCREMENT * mean
+            moved_ref[k : k + 1, lanes] = old_ref[me * rows + k * nblk + b] + TIME_INCREMENT * mean
+
+
+def neighbours(x, axis):
+    count = lax.axis_size(axis)
+    below = lax.ppermute(x, axis, [(i, (i + 1) % count) for i in range(count)])
+    above = lax.ppermute(x, axis, [((i + 1) % count, i) for i in range(count)])
+    return below, above
 
 
 def body(positions, burgers, mobility, block_cells, pairs, pair_count):
     f32 = jnp.float32
     segs = positions.shape[1]
     nblk = block_cells.shape[0]
+    slots = pairs.shape[0]
     n_slab, n_dom = lax.axis_size("slab"), lax.axis_size("dom")
     ndev = n_slab * n_dom
     far_scale = math.sqrt(16 * n_slab / (segs * ndev))
-    rows, rows2 = 6 * nblk + 2, 3 * nblk + 1
+    rows = 3 * nblk + 1
     each = 9 * nblk + 2
     chunks = ndev * nblk // LANES
     high = -(-(3 * nblk) // SUB) * SUB
+    wide = jax.ShapeDtypeStruct((nblk, 3, LANES, LANES), f32)
+    payload = jax.ShapeDtypeStruct((ndev, 1, rows * LANES), f32)
     scratch = [
-        pltpu.VMEM((nblk, 6, LANES, LANES), f32),
         pltpu.VMEM((nblk, 3, LANES, LANES), f32),
         pltpu.VMEM((high, LANES), f32),
         pltpu.VMEM((chunks, LANES, LANES), f32),
         pltpu.VMEM((chunks, SUB, LANES), f32),
         pltpu.VMEM((LANES // nblk, LANES), f32),
     ]
-    load, mob = pl.pallas_call(
+    load, window, mob, cells = pl.pallas_call(
         first_kernel,
         out_shape=(
-            jax.ShapeDtypeStruct((ndev, 1, rows * LANES), f32),
+            payload,
+            jax.ShapeDtypeStruct((1, 1, rows * LANES), f32),
             jax.ShapeDtypeStruct((nblk, LANES), f32),
+            jax.ShapeDtypeStruct((nblk,), jnp.int32),
         ),
-        in_specs=[SMEM, SMEM, VMEM, VMEM, VMEM, VMEM],
-        out_specs=(VMEM, VMEM),
+        in_specs=[SMEM] + [HBM] * 5,
+        out_specs=(VMEM,) * 4,
         scratch_shapes=[
+            pltpu.VMEM((3, segs), f32),
+            pltpu.VMEM((3, segs), f32),
+            pltpu.VMEM((2, slots), jnp.int32),
+            pltpu.SMEM((nblk,), jnp.int32),
             pltpu.VMEM((LANES, LANES), f32),
-            pltpu.VMEM((-(-rows // SUB) * SUB, LANES), f32),
+            pltpu.VMEM((-(-6 * nblk // SUB) * SUB, LANES), f32),
             pltpu.VMEM((1, rows * LANES), f32),
+            pltpu.VMEM((SUB, LANES), jnp.int32),
+            pltpu.SemaphoreType.DMA((6,)),
         ],
         compiler_params=PARAMS,
         name="pack",
-    )(block_cells, pair_count, positions, burgers, pairs, mobility.reshape(nblk, LANES))
+    )(
+        pair_count,
+        *(
+            pltpu.with_memory_space_constraint(x, pltpu.HBM)
+            for x in (block_cells, positions, burgers, pairs.T, mobility.reshape(nblk, LANES))
+        ),
+    )
     got = lax.all_to_all(load, ("slab", "dom"), 0, 0, tiled=True).reshape(ndev * rows, 1, LANES)
-    load2, vel, lists, coef = pl.pallas_call(
+    below, above = neighbours(window, "slab")
+    column = jnp.concatenate([below, window, above], axis=0)
+    left, right = neighbours(column, "dom")
+    left, column, right = (x.reshape(3 * rows, 1, LANES) for x in (left, column, right))
+    load2, vel, lists, coef, bur_wide, moved = pl.pallas_call(
         functools.partial(second_kernel, n_slab, n_dom, far_scale),
         out_shape=(
-            jax.ShapeDtypeStruct((ndev, 1, rows2 * LANES), f32),
+            payload,
             jax.ShapeDtypeStruct((3 * nblk, LANES), f32),
             jax.ShapeDtypeStruct((SUB, LANES), jnp.int32),
             jax.ShapeDtypeStruct((nblk * each, LANES, LANES), f32),
+            wide,
+            jax.ShapeDtypeStruct((3 * nblk, LANES), f32),
         ),
-        in_specs=[SMEM, VMEM, VMEM],
-        out_specs=(VMEM, VMEM, VMEM, VMEM),
-        scratch_shapes=[pltpu.VMEM((LANES, LANES), f32)]
+        in_specs=[SMEM] + [VMEM] * 5,
+        out_specs=(VMEM,) * 6,
+        scratch_shapes=[pltpu.VMEM((LANES, LANES), f32), pltpu.VMEM((nblk, 3, LANES, LANES), f32)]
         + scratch
         + [
+            pltpu.VMEM((9 * rows, 1, LANES), f32),
             pltpu.VMEM((SUB, LANES), f32),
             pltpu.VMEM((SUB, LANES), f32),
             pltpu.VMEM((6 * nblk, LANES), f32),
-            pltpu.VMEM((1, rows2 * LANES), f32),
+            pltpu.VMEM((1, rows * LANES), f32),
             pltpu.SMEM((SUB, LANES), jnp.int32),
             pltpu.SMEM((SUB, LANES), f32),
             pltpu.SemaphoreType.DMA((2,)),
         ],
         compiler_params=PARAMS,
         name="step_one",
-    )(block_cells, mob, got)
-    got2 = lax.all_to_all(load2, ("slab", "dom"), 0, 0, tiled=True).reshape(ndev * rows2, 1, LANES)
+    )(cells, mob, got, left, column, right)
+    got2 = lax.all_to_all(load2, ("slab", "dom"), 0, 0, tiled=True).reshape(ndev * rows, 1, LANES)
     return pl.pallas_call(
         functools.partial(third_kernel, n_slab, n_dom, far_scale),
         out_shape=(jax.ShapeDtypeStruct((3, segs), f32),) * 2,
-        in_specs=[SMEM, VMEM, VMEM, VMEM, VMEM, VMEM, VMEM],
+        in_specs=[SMEM] + [VMEM] * 7,
         out_specs=(VMEM, VMEM),
-        scratch_shapes=scratch,
+        scratch_shapes=[pltpu.VMEM((nblk, 3, LANES, LANES), f32)] + scratch,
         compiler_params=PARAMS,
         name="step_two",
-    )(lists, mob, positions, vel, got, got2, coef)
+    )(lists, mob, vel, got, got2, coef, bur_wide, moved)
 
 
 def solution(mesh):

time: 52.5 us -> 47.5 us (0.905); the launches traced: 51.5 us -> 47.3 us
  blocking collectives: 34.9 us -> 12.7 us
  starting transfers between devices: 0 us -> 11.8 us
  waiting for transfers between devices: 0 us -> 7.07 us
  local copies, waits for them, and re-layouts: 4.19 us -> 0.02 us
  Pallas kernels: 11.1 us -> 14.3 us
    all_to_all x1 -> x0, blocking collectives: 21.4 us -> none  [body(): lax.all_to_all(load, ('slab', 'dom'), 0, 0, tiled=True)]
    ppermute x0 -> x4, starting transfers between devices: none -> 7.36 us  [the longest x2 6.81 us: neighbours(): above = lax.ppermute(x, axis, [((i + 1) % count, i) for i in range(count)])]
    ppermute x0 -> x4, waiting for transfers between devices: none -> 4.73 us  [the longest x2 3.25 us: neighbours(): below = lax.ppermute(x, axis, [(i, (i + 1) % count) for i in range(count)])]
    all_to_all x0 -> x1, starting transfers between devices: none -> 4.49 us  [body(): lax.all_to_all(load, ('slab', 'dom'), 0, 0, tiled=True)]
    unnamed x11 -> x2, local copies, waits for them, and re-layouts: 4.19 us -> 0.01 us
    all_to_all x0 -> x1, waiting for transfers between devices: none -> 2.34 us  [body(): lax.all_to_all(load, ('slab', 'dom'), 0, 0, tiled=True)]
    pallas_call x1, Pallas kernels: 5.25 us -> 6.57 us  [body(): pl.pallas_call(functools.partial(second_kernel, n_slab, n_dom, far_scale)...]
    pallas_call x1, Pallas kernels: 5.06 us -> 5.96 us  [body(): pl.pallas_call(functools.partial(third_kernel, n_slab, n_dom, far_scale),...]
  transfers between devices with their start and end apart: 0 -> 5, of which waited for: 0 -> 3; matrix products, arithmetic and copies ran while one was open for 0% -> 0% of each run, Pallas kernels for 0% -> 0%
where the time goes in v3:
time: 47.5 us; the launch traced here: 47.3 us
  Pallas kernels  14.3 us (30%)
  blocking collectives  12.7 us (27%)
  starting transfers between devices  11.8 us (25%)
  waiting for transfers between devices  7.07 us (15%)
  between operations  1.34 us (3%)
    all_to_all x1, blocking collectives, body(): lax.all_to_all(load2, ('slab', 'dom'), 0, 0, tiled=True)  12.7 us
    ppermute x2, starting transfers between devices, neighbours(): above = lax.ppermute(x, axis, [((i + 1) % count, i) for i in range(count)])  6.81 us
    pallas_call x1, Pallas kernels, body(): pl.pallas_call(functools.partial(second_kernel, n_slab, n_dom, far_scale)...  6.57 us
    pallas_call x1, Pallas kernels, body(): pl.pallas_call(functools.partial(third_kernel, n_slab, n_dom, far_scale),...  5.96 us
    all_to_all x1, starting transfers between devices, body(): lax.all_to_all(load, ('slab', 'dom'), 0, 0, tiled=True)  4.49 us
    ppermute x2, waiting for transfers between devices, neighbours(): below = lax.ppermute(x, axis, [(i, (i + 1) % count) for i in range(count)])  3.25 us
    all_to_all x1, waiting for transfers between devices, body(): lax.all_to_all(load, ('slab', 'dom'), 0, 0, tiled=True)  2.34 us
    pallas_call x1, Pallas kernels, body(): pl.pallas_call(first_kernel, out_shape=(payload, jax.ShapeDtypeStruct((1,...  1.73 us
  transfers between devices with their start and end apart: 5, of which 3 were waited for; matrix products, arithmetic and copies ran while one was open for 0% of the time, Pallas kernels for 0%

profile of v3, /device:TPU:0, one launch (start us, length us, event | category | flops | bytes accessed | tf_op | source)
XLA Modules:
  0.0 47.3 jit_solution(9606746360864081895)
XLA Ops:
  1.3 1.7 %pack.1 = (f32[32,1,1664]{2,1,0:T(1,128)}, f32[1,1,1664]{2,1,0:T(1,128)S(1)}, f32[4,128]{1,0:T(4,128)S(1)}, s32[4]{0:T(128)S(1)}) custom-call(s32[1]{0:T(128)S(6)} %copy.10.count_ref, s32[4]{0:T(128)} %cells_hbm.1, f32[3,512]{1,0:T(4,128)} %pos_hbm.1, f32[3,512]{1,0:T(4,128)} %bur_hbm.1, s32[2,64]{1,0:T(2,128)} %bitcast.14, f32[4,128]{1,0:T(4,128)} %bitcast.13), custom_call_target="tpu_custom_call" | custom-call | tf_op jit(solution)/shard_map/pack/pallas_call | solution.py:416
  3.0 0.5 %collective-permute-start = (f32[1,1,1664]{2,1,0:T(1,128)S(1)}, f32[1,1,1664]{2,1,0:T(1,128)S(1)}, u32[]{:S(2)}, u32[]{:S(2)}) collective-permute-start(f32[1,1,1664]{2,1,0:T(1,128)S(1)} %get-tuple-element.15), channel_id=1, source_target_pairs={{0,4},{4,8},{8,12},{12,16},{16,20},{20,24},{24,28},{28,0},{1,5},{5... | collective-permute-start | bytes 19976 | tf_op jit(solution)/shard_map/ppermute | solution.py:390
  3.6 4.1 %collective-permute-start.1 = (f32[1,1,1664]{2,1,0:T(1,128)S(1)}, f32[1,1,1664]{2,1,0:T(1,128)S(1)}, u32[]{:S(2)}, u32[]{:S(2)}) collective-permute-start(f32[1,1,1664]{2,1,0:T(1,128)S(1)} %get-tuple-element.15), channel_id=1, source_target_pairs={{4,0},{8,4},{12,8},{16,12},{20,16},{24,20},{28,24},{0,28},{5,1},{9... | collective-permute-start | bytes 19976 | tf_op jit(solution)/shard_map/ppermute | solution.py:391
  7.7 4.5 %all-to-all-start = ((f32[32,1,1664]{2,1,0:T(1,128)}), f32[32,1,1664]{2,1,0:T(1,128)S(1)}, u32[]{:S(2)}, u32[]{:S(2)}) async-start(f32[32,1,1664]{2,1,0:T(1,128)} %get-tuple-element.14), calls=%async_computation | async-start | bytes 425984 | tf_op jit(solution)/shard_map/all_to_all | solution.py:446
  12.1 0.0 collective-permute-done
  12.2 0.0 collective-permute-done.1
  12.2 2.7 %collective-permute-start.3 = (f32[3,1,1664]{2,1,0:T(1,128)S(1)}, f32[3,1,1664]{2,1,0:T(1,128)S(1)}, u32[]{:S(2)}, u32[]{:S(2)}) collective-permute-start(f32[3,1,1664]{2,1,0:T(1,128)S(1)} %constant_dynamic-update-slice_fusion), channel_id=1, source_target_pairs={{1,0},{2,1},{3,2},{0,3},{5,4},{6,5},{7,6},{4,7},{9,8},{10,9},{11,1... | collective-permute-start | bytes 59912 | tf_op jit(solution)/shard_map/ppermute | solution.py:391
  14.9 0.0 collective-permute-start.2
  14.9 1.5 %collective-permute-done.3 = f32[3,1,1664]{2,1,0:T(1,128)S(1)} collective-permute-done((f32[3,1,1664]{2,1,0:T(1,128)S(1)}, f32[3,1,1664]{2,1,0:T(1,128)S(1)}, u32[]{:S(2)}, u32[]{:S(2)}) %collective-permute-start.3) | collective-permute-done | bytes 20000 | tf_op jit(solution)/shard_map/ppermute | solution.py:391
  16.4 3.2 %collective-permute-done.2 = f32[3,1,1664]{2,1,0:T(1,128)S(1)} collective-permute-done((f32[3,1,1664]{2,1,0:T(1,128)S(1)}, f32[3,1,1664]{2,1,0:T(1,128)S(1)}, u32[]{:S(2)}, u32[]{:S(2)}) %collective-permute-start.2) | collective-permute-done | bytes 20000 | tf_op jit(solution)/shard_map/ppermute | solution.py:390
  19.7 2.3 %all-to-all-done = f32[32,1,1664]{2,1,0:T(1,128)S(1)} async-done(((f32[32,1,1664]{2,1,0:T(1,128)}), f32[32,1,1664]{2,1,0:T(1,128)S(1)}, u32[]{:S(2)}, u32[]{:S(2)}) %all-to-all-start) | async-done | bytes 213024 | tf_op jit(solution)/shard_map/all_to_all | solution.py:446
  22.0 6.6 %step_one.1 = (f32[32,1,1664]{2,1,0:T(1,128)S(1)}, f32[12,128]{1,0:T(8,128)S(1)}, s32[8,128]{1,0:T(8,128)S(1)}, f32[152,128,128]{2,1,0:T(8,128)S(1)}, f32[4,3,12...) custom-call(s32[4]{0:T(128)S(1)} %get-tuple-element.12.cells_ref, f32[4,128]{1,0:T(4,128)S(1)} %get-tuple-element.13.mob_ref, ...), custom_call_target="tpu_custom_call" | custom-call | tf_op jit(solution)/shard_map/step_one/pallas_call | solution.py:451
  28.6 12.7 %all_to_all.10 = f32[32,1,1664]{2,1,0:T(1,128)S(1)} all-to-all(f32[32,1,1664]{2,1,0:T(1,128)S(1)} %get-tuple-element.18), channel_id=1, replica_groups=mesh['slab'=8,'dom'=4] {'slab','dom'}, dimensions={0} | all-to-all | bytes 425984 | tf_op jit(solution)/shard_map/all_to_all | solution.py:478
  41.3 6.0 %step_two.1 = (f32[3,512]{1,0:T(4,128)}, f32[3,512]{1,0:T(4,128)}) custom-call(s32[8,128]{1,0:T(8,128)S(1)} %get-tuple-element.16.list_smem, f32[4,128]{1,0:T(4,128)S(1)} %get-tuple-element.13.mob_ref, f32[12,128]{1,0:T(8,128)S(1)} %get-tuple-element.17.vel_ref, f32[416,1,128]{2,1,0:T(1,128)S(1)} %bitcast.8, f32[416,1,128]{2,1,0:T(1,128)S(1)} %bitcast.9, ...), custom_call_target="tpu_custom_call" | custom-call | tf_op jit(solution)/shard_map/step_two/pallas_call | solution.py:479
  (3 shorter events, 0.0 us)
Async XLA Ops:
  3.0 9.1 %collective-permute-start = (f32[1,1,1664]{2,1,0:T(1,128)S(1)}, f32[1,1,1664]{2,1,0:T(1,128)S(1)}, u32[]{:S(2)}, u32[]{:S(2)}) collective-permute-start(f32[1,1,1664]{2,1,0:T(1,128)S(1)} %get-tuple-element.15), channel_id=1, source_target_pairs={{0,4},{4,8},{8,12},{12,16},{16,20},{20,24},{24,28},{28,0},{1,5},{5... | collective-permute-start | bytes 19976 | tf_op jit(solution)/shard_map/ppermute | solution.py:390
  3.6 8.6 %collective-permute-start.1 = (f32[1,1,1664]{2,1,0:T(1,128)S(1)}, f32[1,1,1664]{2,1,0:T(1,128)S(1)}, u32[]{:S(2)}, u32[]{:S(2)}) collective-permute-start(f32[1,1,1664]{2,1,0:T(1,128)S(1)} %get-tuple-element.15), channel_id=1, source_target_pairs={{4,0},{8,4},{12,8},{16,12},{20,16},{24,20},{28,24},{0,28},{5,1},{9... | collective-permute-start | bytes 19976 | tf_op jit(solution)/shard_map/ppermute | solution.py:391
  7.7 14.3 %all-to-all-start = ((f32[32,1,1664]{2,1,0:T(1,128)}), f32[32,1,1664]{2,1,0:T(1,128)S(1)}, u32[]{:S(2)}, u32[]{:S(2)}) async-start(f32[32,1,1664]{2,1,0:T(1,128)} %get-tuple-element.14), calls=%async_computation | async-start | bytes 425984 | tf_op jit(solution)/shard_map/all_to_all | solution.py:446
  12.2 4.2 %collective-permute-start.3 = (f32[3,1,1664]{2,1,0:T(1,128)S(1)}, f32[3,1,1664]{2,1,0:T(1,128)S(1)}, u32[]{:S(2)}, u32[]{:S(2)}) collective-permute-start(f32[3,1,1664]{2,1,0:T(1,128)S(1)} %constant_dynamic-update-slice_fusion), channel_id=1, source_target_pairs={{1,0},{2,1},{3,2},{0,3},{5,4},{6,5},{7,6},{4,7},{9,8},{10,9},{11,1... | collective-permute-start | bytes 59912 | tf_op jit(solution)/shard_map/ppermute | solution.py:391
  14.9 4.7 %collective-permute-start.2 = (f32[3,1,1664]{2,1,0:T(1,128)S(1)}, f32[3,1,1664]{2,1,0:T(1,128)S(1)}, u32[]{:S(2)}, u32[]{:S(2)}) collective-permute-start(f32[3,1,1664]{2,1,0:T(1,128)S(1)} %constant_dynamic-update-slice_fusion), channel_id=1, source_target_pairs={{0,1},{1,2},{2,3},{3,0},{4,5},{5,6},{6,7},{7,4},{8,9},{9,10},{10,1... | collective-permute-start | bytes 59912 | tf_op jit(solution)/shard_map/ppermute | solution.py:390

commit v4 on v3

--- a/solution.py
+++ b/solution.py
@@ -84,7 +84,7 @@
 def first_kernel(
     count_ref, cells_hbm, pos_hbm, bur_hbm, pairs_hbm, mob_hbm,
     out_ref, win_ref, mob_ref, cells_out_ref,
-    pos_ref, bur_ref, pairs_ref, cells_ref, stack_ref, load_ref, flat_ref, ids_ref, sem,
+    pos_ref, bur_ref, pairs_ref, cells_ref, stack_ref, load_ref, ids_ref, sem,
 ):
     moves = (
         (cells_hbm, cells_ref), (pos_hbm, pos_ref), (bur_hbm, bur_ref),
@@ -111,13 +111,10 @@
     slot = lax.broadcasted_iota(jnp.int32, (1, LANES), 1)
     slot = jnp.where(slot < slots, slot, slot - slots)
     listed = jnp.where(slot < count_ref[0], ids_ref[0:1, :], -1).astype(jnp.float32)
-    for r in range(3 * nblk):
-        lanes = slice(r * LANES, (r + 1) * LANES)
-        flat_ref[:, lanes] = load_ref[r : r + 1, :]
-        win_ref[0, :, lanes] = load_ref[3 * nblk + r : 3 * nblk + r + 1, :]
-    win_ref[0, :, 3 * nblk * LANES :] = listed
-    flat_ref[:, 3 * nblk * LANES :] = moment_row(pos, bur, cells_ref, stack_ref)
-    spread(out_ref, flat_ref[...])
+    for r in range(6 * nblk):
+        win_ref[0, :, r * LANES : (r + 1) * LANES] = load_ref[r : r + 1, :]
+    win_ref[0, :, 6 * nblk * LANES :] = listed
+    spread(out_ref, moment_row(pos, bur, cells_ref, stack_ref))
 
 
 def far_into(own_ref, bur_ref, mom_ref, center_ref, acc_ref, nblk, chunks):
@@ -280,7 +277,7 @@
 def second_kernel(
     n_slab, n_dom, far_scale,
     cells_ref, mob_ref, got_ref, low_ref, mid_ref, high_ref,
-    out_ref, vel_ref, list_ref, coef_ref, wide_ref, moved_ref,
+    out_ref, vel_ref, list_ref, coef_ref, wide_ref, moved_ref, old_ref,
     stack_ref, own_ref, acc_ref, force_ref, mom_ref, center_ref, take_ref,
     win_ref, count_ref, mult_ref, next_ref, flat_ref, list_smem, mult_smem, sem,
 ):
@@ -289,26 +286,24 @@
     rows = got_ref.shape[0] // ndev
     each = coef_ref.shape[0] // nblk
     my_slab, my_dom = lax.axis_index("slab"), lax.axis_index("dom")
-    me = my_slab * n_dom + my_dom
     third = low_ref.shape[0]
     places = third // 3
     for j, ref in enumerate((low_ref, mid_ref, high_ref)):
         win_ref[j * third : (j + 1) * third] = ref[...]
 
     def own_row(k, b):
-        return got_ref[me * rows + k * nblk + b]
+        return win_ref[4 * places + k * nblk + b]
 
     def own_bur(k, b):
-        return win_ref[4 * places + k * nblk + b]
+        return own_row(3 + k, b)
 
     def block_row(a, e, k):
-        g = list_smem[a, e]
-        return got_ref[(g // nblk) * rows + g % nblk + k * nblk]
+        w = list_smem[nblk + a, e]
+        return win_ref[(w // nblk) * places + w % nblk + k * nblk]
 
     def coef_of(a, e):
-        w, mult = list_smem[nblk + a, e], mult_smem[a, e]
-        first = (w // nblk) * places + w % nblk
-        c = [jnp.broadcast_to(win_ref[first + k * nblk] * mult, (SUB, LANES)) for k in range(3)]
+        mult = mult_smem[a, e]
+        c = [jnp.broadcast_to(block_row(a, e, 3 + k) * mult, (SUB, LANES)) for k in range(3)]
 
         def tile(t, rows):
             value = wide_ref[a, 0, rows, :] * c[0] + wide_ref[a, 1, rows, :] * c[1] + wide_ref[a, 2, rows, :] * c[2]
@@ -340,6 +335,7 @@
         for b in range(nblk):
             next_ref[k * nblk + b : k * nblk + b + 1, :] = own_row(k, b)
             next_ref[(3 + k) * nblk + b : (3 + k) * nblk + b + 1, :] = own_bur(k, b)
+        old_ref[here, :] = next_ref[here, :]
         moved = next_ref[here, :] + TIME_INCREMENT * vel
         moved_ref[here, :] = moved
         pos.append(moved)
@@ -361,7 +357,6 @@
     ndev = n_slab * n_dom
     rows = got_ref.shape[0] // ndev
     each = coef_ref.shape[0] // nblk
-    me = lax.axis_index("slab") * n_dom + lax.axis_index("dom")
 
     def block_row(a, e, k):
         g = list_smem[a, e]
@@ -382,7 +377,7 @@
             lanes = slice(b * LANES, (b + 1) * LANES)
             mean = force_ref[k * nblk + b : k * nblk + b + 1, :]
             velocity_ref[k : k + 1, lanes] = mean
-            moved_ref[k : k + 1, lanes] = old_ref[me * rows + k * nblk + b] + TIME_INCREMENT * mean
+            moved_ref[k : k + 1, lanes] = old_ref[k * nblk + b : k * nblk + b + 1, :] + TIME_INCREMENT * mean
 
 
 def neighbours(x, axis):
@@ -400,7 +395,7 @@
     n_slab, n_dom = lax.axis_size("slab"), lax.axis_size("dom")
     ndev = n_slab * n_dom
     far_scale = math.sqrt(16 * n_slab / (segs * ndev))
-    rows = 3 * nblk + 1
+    rows, places = 3 * nblk + 1, 6 * nblk + 1
     each = 9 * nblk + 2
     chunks = ndev * nblk // LANES
     high = -(-(3 * nblk) // SUB) * SUB
@@ -416,8 +411,8 @@
     load, window, mob, cells = pl.pallas_call(
         first_kernel,
         out_shape=(
-            payload,
-            jax.ShapeDtypeStruct((1, 1, rows * LANES), f32),
+            jax.ShapeDtypeStruct((ndev, 1, LANES), f32),
+            jax.ShapeDtypeStruct((1, 1, places * LANES), f32),
             jax.ShapeDtypeStruct((nblk, LANES), f32),
             jax.ShapeDtypeStruct((nblk,), jnp.int32),
         ),
@@ -430,7 +425,6 @@
             pltpu.SMEM((nblk,), jnp.int32),
             pltpu.VMEM((LANES, LANES), f32),
             pltpu.VMEM((-(-6 * nblk // SUB) * SUB, LANES), f32),
-            pltpu.VMEM((1, rows * LANES), f32),
             pltpu.VMEM((SUB, LANES), jnp.int32),
             pltpu.SemaphoreType.DMA((6,)),
         ],
@@ -443,12 +437,12 @@
             for x in (block_cells, positions, burgers, pairs.T, mobility.reshape(nblk, LANES))
         ),
     )
-    got = lax.all_to_all(load, ("slab", "dom"), 0, 0, tiled=True).reshape(ndev * rows, 1, LANES)
+    got = lax.all_to_all(load, ("slab", "dom"), 0, 0, tiled=True)
     below, above = neighbours(window, "slab")
     column = jnp.concatenate([below, window, above], axis=0)
     left, right = neighbours(column, "dom")
-    left, column, right = (x.reshape(3 * rows, 1, LANES) for x in (left, column, right))
-    load2, vel, lists, coef, bur_wide, moved = pl.pallas_call(
+    left, column, right = (x.reshape(3 * places, 1, LANES) for x in (left, column, right))
+    load2, vel, lists, coef, bur_wide, moved, old = pl.pallas_call(
         functools.partial(second_kernel, n_slab, n_dom, far_scale),
         out_shape=(
             payload,
@@ -457,13 +451,14 @@
             jax.ShapeDtypeStruct((nblk * each, LANES, LANES), f32),
             wide,
             jax.ShapeDtypeStruct((3 * nblk, LANES), f32),
+            jax.ShapeDtypeStruct((3 * nblk, LANES), f32),
         ),
         in_specs=[SMEM] + [VMEM] * 5,
-        out_specs=(VMEM,) * 6,
+        out_specs=(VMEM,) * 7,
         scratch_shapes=[pltpu.VMEM((LANES, LANES), f32), pltpu.VMEM((nblk, 3, LANES, LANES), f32)]
         + scratch
         + [
-            pltpu.VMEM((9 * rows, 1, LANES), f32),
+            pltpu.VMEM((9 * places, 1, LANES), f32),
             pltpu.VMEM((SUB, LANES), f32),
             pltpu.VMEM((SUB, LANES), f32),
             pltpu.VMEM((6 * nblk, LANES), f32),
@@ -484,7 +479,7 @@
         scratch_shapes=[pltpu.VMEM((nblk, 3, LANES, LANES), f32)] + scratch,
         compiler_params=PARAMS,
         name="step_two",
-    )(lists, mob, vel, got, got2, coef, bur_wide, moved)
+    )(lists, mob, vel, old, got2, coef, bur_wide, moved)
 
 
 def solution(mesh):

time: 47.5 us -> 48.9 us (1.029)
  blocking collectives: 12.7 us -> 24.8 us
  waiting for transfers between devices: 7.07 us -> 1.4 us
  starting transfers between devices: 11.8 us -> 7.57 us
  Pallas kernels: 14.3 us -> 13.6 us
    all_to_all x0 -> x1, blocking collectives: none -> 12.6 us  [body(): got = lax.all_to_all(load, ('slab', 'dom'), 0, 0, tiled=True)]
    all_to_all x1 -> x0, starting transfers between devices: 4.49 us -> none  [body(): lax.all_to_all(load, ('slab', 'dom'), 0, 0, tiled=True)]
    all_to_all x1 -> x0, waiting for transfers between devices: 2.34 us -> none  [body(): lax.all_to_all(load, ('slab', 'dom'), 0, 0, tiled=True)]
    ppermute x2, waiting for transfers between devices: 3.25 us -> 1.32 us  [neighbours(): below = lax.ppermute(x, axis, [(i, (i + 1) % count) for i in range(count)])]
    ppermute x2, waiting for transfers between devices: 1.48 us -> 0.08 us  [neighbours(): above = lax.ppermute(x, axis, [((i + 1) % count, i) for i in range(count)])]
    pallas_call x1, Pallas kernels: 1.73 us -> 1.05 us  [body(): pl.pallas_call(first_kernel, out_shape=(jax.ShapeDtypeStruct((ndev, 1, LA...]
    all_to_all x1, blocking collectives: 12.7 us -> 12.2 us  [body(): lax.all_to_all(load2, ('slab', 'dom'), 0, 0, tiled=True)]
  transfers between devices with their start and end apart: 5 -> 4, of which waited for: 3 -> 2; matrix products, arithmetic and copies ran while one was open for 0% -> 0% of each run, Pallas kernels for 0% -> 0%
where the time goes in v4:
time: 48.9 us; the launch traced here: 48.7 us
  blocking collectives  24.8 us (51%)
  Pallas kernels  13.6 us (28%)
  starting transfers between devices  7.57 us (15%)
  waiting for transfers between devices  1.4 us (3%)
  between operations  1.3 us (3%)
    all_to_all x1, blocking collectives, body(): got = lax.all_to_all(load, ('slab', 'dom'), 0, 0, tiled=True)  12.6 us
    all_to_all x1, blocking collectives, body(): lax.all_to_all(load2, ('slab', 'dom'), 0, 0, tiled=True)  12.2 us
    ppermute x2, starting transfers between devices, neighbours(): above = lax.ppermute(x, axis, [((i + 1) % count, i) for i in range(count)])  7.02 us
    pallas_call x1, Pallas kernels, body(): pl.pallas_call(functools.partial(second_kernel, n_slab, n_dom, far_scale)...  6.61 us
    pallas_call x1, Pallas kernels, body(): pl.pallas_call(functools.partial(third_kernel, n_slab, n_dom, far_scale),...  5.99 us
    ppermute x2, waiting for transfers between devices, neighbours(): below = lax.ppermute(x, axis, [(i, (i + 1) % count) for i in range(count)])  1.32 us
    pallas_call x1, Pallas kernels, body(): pl.pallas_call(first_kernel, out_shape=(jax.ShapeDtypeStruct((ndev, 1, LA...  1.05 us
  transfers between devices with their start and end apart: 4, of which 2 were waited for; matrix products, arithmetic and copies ran while one was open for 0% of the time, Pallas kernels for 0%

profile of v4, /device:TPU:0, one launch (start us, length us, event | category | flops | bytes accessed | tf_op | source)
XLA Modules:
  0.0 48.7 jit_solution(17676548592576192717)
XLA Ops:
  1.3 1.0 %pack.1 = (f32[32,1,128]{2,1,0:T(1,128)S(1)}, f32[1,1,3200]{2,1,0:T(1,128)S(1)}, f32[4,128]{1,0:T(4,128)S(1)}, s32[4]{0:T(128)S(1)}) custom-call(s32[1]{0:T(128)S(6)} %copy.10.count_ref, s32[4]{0:T(128)} %cells_hbm.1, f32[3,512]{1,0:T(4,128)} %pos_hbm.1, f32[3,512]{1,0:T(4,128)} %bur_hbm.1, s32[2,64]{1,0:T(2,128)} %bitcast.11, f32[4,128]{1,0:T(4,128)} %bitcast.10), custom_call_target="tpu_custom_call" | custom-call | tf_op jit(solution)/shard_map/pack/pallas_call | solution.py:411
  2.3 0.5 %collective-permute-start = (f32[1,1,3200]{2,1,0:T(1,128)S(1)}, f32[1,1,3200]{2,1,0:T(1,128)S(1)}, u32[]{:S(2)}, u32[]{:S(2)}) collective-permute-start(f32[1,1,3200]{2,1,0:T(1,128)S(1)} %get-tuple-element.16), channel_id=1, source_target_pairs={{0,4},{4,8},{8,12},{12,16},{16,20},{20,24},{24,28},{28,0},{1,5},{5... | collective-permute-start | bytes 38408 | tf_op jit(solution)/shard_map/ppermute | solution.py:385
  2.9 4.1 %collective-permute-start.1 = (f32[1,1,3200]{2,1,0:T(1,128)S(1)}, f32[1,1,3200]{2,1,0:T(1,128)S(1)}, u32[]{:S(2)}, u32[]{:S(2)}) collective-permute-start(f32[1,1,3200]{2,1,0:T(1,128)S(1)} %get-tuple-element.16), channel_id=1, source_target_pairs={{4,0},{8,4},{12,8},{16,12},{20,16},{24,20},{28,24},{0,28},{5,1},{9... | collective-permute-start | bytes 38408 | tf_op jit(solution)/shard_map/ppermute | solution.py:386
  7.0 1.3 %collective-permute-done = f32[1,1,3200]{2,1,0:T(1,128)S(1)} collective-permute-done((f32[1,1,3200]{2,1,0:T(1,128)S(1)}, f32[1,1,3200]{2,1,0:T(1,128)S(1)}, u32[]{:S(2)}, u32[]{:S(2)}) %collective-permute-start) | collective-permute-done | bytes 12832 | tf_op jit(solution)/shard_map/ppermute | solution.py:385
  8.3 0.1 collective-permute-done.1
  8.4 2.9 %collective-permute-start.3 = (f32[3,1,3200]{2,1,0:T(1,128)S(1)}, f32[3,1,3200]{2,1,0:T(1,128)S(1)}, u32[]{:S(2)}, u32[]{:S(2)}) collective-permute-start(f32[3,1,3200]{2,1,0:T(1,128)S(1)} %constant_dynamic-update-slice_fusion), channel_id=1, source_target_pairs={{1,0},{2,1},{3,2},{0,3},{5,4},{6,5},{7,6},{4,7},{9,8},{10,9},{11,1... | collective-permute-start | bytes 115208 | tf_op jit(solution)/shard_map/ppermute | solution.py:386
  11.3 0.0 collective-permute-start.2
  11.3 12.6 %all_to_all.10.got_ref = f32[32,1,128]{2,1,0:T(1,128)S(1)} all-to-all(f32[32,1,128]{2,1,0:T(1,128)S(1)} %get-tuple-element.15), channel_id=1, replica_groups=mesh['slab'=8,'dom'=4] {'slab','dom'}, dimensions={0} | all-to-all | bytes 32768 | tf_op jit(solution)/shard_map/all_to_all | solution.py:440
  23.9 0.0 collective-permute-done.3
  24.0 0.0 collective-permute-done.2
  24.0 6.6 %step_one.1 = (f32[32,1,1664]{2,1,0:T(1,128)S(1)}, f32[12,128]{1,0:T(8,128)S(1)}, s32[8,128]{1,0:T(8,128)S(1)}, f32[152,128,128]{2,1,0:T(8,128)S(1)}, f32[4,3,12...) custom-call(s32[4]{0:T(128)S(1)} %get-tuple-element.13.cells_ref, ...), custom_call_target="tpu_custom_call" | custom-call | tf_op jit(solution)/shard_map/step_one/pallas_call | solution.py:445
  30.6 12.2 %all_to_all.11 = f32[32,1,1664]{2,1,0:T(1,128)S(1)} all-to-all(f32[32,1,1664]{2,1,0:T(1,128)S(1)} %get-tuple-element.20), channel_id=1, replica_groups=mesh['slab'=8,'dom'=4] {'slab','dom'}, dimensions={0} | all-to-all | bytes 425984 | tf_op jit(solution)/shard_map/all_to_all | solution.py:473
  42.8 6.0 %step_two.1 = (f32[3,512]{1,0:T(4,128)}, f32[3,512]{1,0:T(4,128)}) custom-call(s32[8,128]{1,0:T(8,128)S(1)} %get-tuple-element.17.list_smem, f32[4,128]{1,0:T(4,128)S(1)} %get-tuple-element.14.mob_ref, f32[12,128]{1,0:T(8,128)S(1)} %get-tuple-element.18.vel_ref, f32[12,128]{1,0:T(8,128)S(1)} %get-tuple-element.19.old_ref, f32[416,1,128]{2,1,0:T(1,128)S(1)} %bitcast.6, ...), custom_call_target="tpu_custom_call" | custom-call | tf_op jit(solution)/shard_map/step_two/pallas_call | solution.py:474
  (3 shorter events, 0.0 us)
Async XLA Ops:
  2.3 6.0 %collective-permute-start = (f32[1,1,3200]{2,1,0:T(1,128)S(1)}, f32[1,1,3200]{2,1,0:T(1,128)S(1)}, u32[]{:S(2)}, u32[]{:S(2)}) collective-permute-start(f32[1,1,3200]{2,1,0:T(1,128)S(1)} %get-tuple-element.16), channel_id=1, source_target_pairs={{0,4},{4,8},{8,12},{12,16},{16,20},{20,24},{24,28},{28,0},{1,5},{5... | collective-permute-start | bytes 38408 | tf_op jit(solution)/shard_map/ppermute | solution.py:385
  2.9 5.5 %collective-permute-start.1 = (f32[1,1,3200]{2,1,0:T(1,128)S(1)}, f32[1,1,3200]{2,1,0:T(1,128)S(1)}, u32[]{:S(2)}, u32[]{:S(2)}) collective-permute-start(f32[1,1,3200]{2,1,0:T(1,128)S(1)} %get-tuple-element.16), channel_id=1, source_target_pairs={{4,0},{8,4},{12,8},{16,12},{20,16},{24,20},{28,24},{0,28},{5,1},{9... | collective-permute-start | bytes 38408 | tf_op jit(solution)/shard_map/ppermute | solution.py:386
  8.4 15.6 %collective-permute-start.3 = (f32[3,1,3200]{2,1,0:T(1,128)S(1)}, f32[3,1,3200]{2,1,0:T(1,128)S(1)}, u32[]{:S(2)}, u32[]{:S(2)}) collective-permute-start(f32[3,1,3200]{2,1,0:T(1,128)S(1)} %constant_dynamic-update-slice_fusion), channel_id=1, source_target_pairs={{1,0},{2,1},{3,2},{0,3},{5,4},{6,5},{7,6},{4,7},{9,8},{10,9},{11,1... | collective-permute-start | bytes 115208 | tf_op jit(solution)/shard_map/ppermute | solution.py:386
  11.3 12.6 %collective-permute-start.2 = (f32[3,1,3200]{2,1,0:T(1,128)S(1)}, f32[3,1,3200]{2,1,0:T(1,128)S(1)}, u32[]{:S(2)}, u32[]{:S(2)}) collective-permute-start(f32[3,1,3200]{2,1,0:T(1,128)S(1)} %constant_dynamic-update-slice_fusion), channel_id=1, source_target_pairs={{0,1},{1,2},{2,3},{3,0},{4,5},{5,6},{6,7},{7,4},{8,9},{9,10},{10,1... | collective-permute-start | bytes 115208 | tf_op jit(solution)/shard_map/ppermute | solution.py:385

commit v5 on v4

--- a/solution.py
+++ b/solution.py
@@ -19,6 +19,7 @@
 SMEM = pl.BlockSpec(memory_space=pltpu.SMEM)
 HBM = pl.BlockSpec(memory_space=pltpu.HBM)
 PARAMS = pltpu.CompilerParams(vmem_limit_bytes=8 * 1024 * 1024)
+PARAMS_EVEN = pltpu.CompilerParams(vmem_limit_bytes=8 * 1024 * 1024)
 SYM = ((0, 0), (0, 1), (0, 2), (1, 1), (1, 2), (2, 2))
 MOMS = 3 + 9 + 18
 
@@ -37,18 +38,20 @@
     return (4.0 * slab + 2.0, 2.0 * row + 1.0, 2.0 * col + 1.0)
 
 
-def column_of(values, like):
-    index = lax.broadcasted_iota(jnp.int32, like, 0)
-    out = jnp.full(like, values[-1], jnp.float32)
-    for j, value in enumerate(values[:-1]):
-        out = jnp.where(index == j, value, out)
-    return out
-
-
-def moment_row(pos, bur, cells_ref, stack_ref):
+def put_cells(cells_smem, cell_ref):
+    nblk = cells_smem.shape[0]
+    lane = lax.broadcasted_iota(jnp.int32, (1, LANES), 1)
+    last = jnp.zeros((1, LANES), jnp.float32)
+    for b in range(nblk):
+        cell = cells_smem[b].astype(jnp.float32)
+        cell_ref[b : b + 1, :] = jnp.full((1, LANES), cell, jnp.float32)
+        last = jnp.where(lane == MOMS * nblk + b, cell, last)
+    cell_ref[nblk : nblk + 1, :] = last
+
+
+def moment_row(pos, bur, cell_ref, stack_ref):
     nblk = pos[0].shape[0]
-    cell = column_of([cells_ref[b].astype(jnp.float32) for b in range(nblk)], pos[0].shape)
-    z = center_of(cell)
+    z = center_of(cell_ref[0:nblk, :])
     d = [pos[k] - z[k] for k in range(3)]
     dd = [d[a] * d[e] for a, e in SYM]
     stack_ref[...] = jnp.zeros_like(stack_ref)
@@ -66,9 +69,7 @@
             m += 1
     sums = dot_lanes(jnp.ones((SUB, LANES), jnp.float32), stack_ref[...])[0:1, :]
     lane = lax.broadcasted_iota(jnp.int32, (1, LANES), 1)
-    for b in range(nblk):
-        sums = jnp.where(lane == MOMS * nblk + b, cells_ref[b].astype(jnp.float32), sums)
-    return sums
+    return jnp.where(lane < MOMS * nblk, sums, cell_ref[nblk : nblk + 1, :])
 
 
 def spread(out_ref, value):
@@ -83,12 +84,12 @@
 
 def first_kernel(
     count_ref, cells_hbm, pos_hbm, bur_hbm, pairs_hbm, mob_hbm,
-    out_ref, win_ref, mob_ref, cells_out_ref,
+    out_ref, win_ref, mob_ref, cell_ref,
     pos_ref, bur_ref, pairs_ref, cells_ref, stack_ref, load_ref, ids_ref, sem,
 ):
     moves = (
         (cells_hbm, cells_ref), (pos_hbm, pos_ref), (bur_hbm, bur_ref),
-        (pairs_hbm, pairs_ref), (mob_hbm, mob_ref), (cells_hbm, cells_out_ref),
+        (pairs_hbm, pairs_ref), (mob_hbm, mob_ref),
     )
     copies = [pltpu.make_async_copy(src, dst, sem.at[j]) for j, (src, dst) in enumerate(moves)]
     for copy in copies:
@@ -114,7 +115,8 @@
     for r in range(6 * nblk):
         win_ref[0, :, r * LANES : (r + 1) * LANES] = load_ref[r : r + 1, :]
     win_ref[0, :, 6 * nblk * LANES :] = listed
-    spread(out_ref, moment_row(pos, bur, cells_ref, stack_ref))
+    put_cells(cells_ref, cell_ref)
+    spread(out_ref, moment_row(pos, bur, cell_ref, stack_ref))
 
 
 def far_into(own_ref, bur_ref, mom_ref, center_ref, acc_ref, nblk, chunks):
@@ -161,13 +163,16 @@
         lax.fori_loop(0, nblk * (chunks - 1), more, 0)
 
 
-def near_into(row_pos, coef_of, own_ref, used_of, acc_ref, nblk):
+def near_into(first_of, rows_at, coef_of, own_ref, used_of, acc_ref, nblk):
     for a in range(nblk):
 
+        def ahead(n):
+            return tuple(rows_at(first_of(a, 2 * n + j)) for j in range(2))
+
         def visit(n, carry):
-            pair = (2 * n, 2 * n + 1)
-            p = [[jnp.broadcast_to(row_pos(a, e, k), (SUB, LANES)) for k in range(3)] for e in pair]
-            weigh = [coef_of(a, e) for e in pair]
+            following = ahead(n + 1)
+            p = [carry[j][:3] for j in range(2)]
+            weigh = [coef_of(a, 2 * n + j, carry[j]) for j in range(2)]
             for t in range(LANES // SUB):
                 rows = slice(t * SUB, (t + 1) * SUB)
                 own = [own_ref[a, k, rows, :] for k in range(3)]
@@ -181,9 +186,9 @@
                     f.append([wgt * r[k] for k in range(3)])
                 for k in range(3):
                     acc_ref[a, k, rows, :] = acc_ref[a, k, rows, :] + (f[0][k] + f[1][k])
-            return carry
-
-        lax.fori_loop(0, (used_of(a) + 1) // 2, visit, 0)
+            return following
+
+        lax.fori_loop(0, (used_of(a) + 1) // 2, visit, ahead(0))
 
 
 def sum_lanes(acc_ref, force_ref, nblk):
@@ -215,7 +220,7 @@
     return ids
 
 
-def build_lists(win_ref, rows, nblk, my_slab, my_dom, n_slab, n_dom, count_ref, list_ref, mult_ref):
+def build_lists(win_ref, rows, nblk, my_slab, my_dom, n_slab, n_dom, next_rows, count_ref, list_ref, mult_ref):
     high = -(-9 * nblk // SUB) * SUB
     place = (my_slab, my_dom, n_slab, n_dom, nblk)
     gid = window_ids(lax.broadcasted_iota(jnp.int32, (high, LANES), 0), *place)
@@ -223,7 +228,7 @@
     sub = lax.broadcasted_iota(jnp.int32, (SUB, LANES), 0)
     lane = lax.broadcasted_iota(jnp.int32, (SUB, LANES), 1)
     mine = jnp.where(sub < nblk, sub + own, -3).astype(jnp.float32)
-    total = jnp.zeros((SUB, high), jnp.float32)
+    total = jnp.zeros((high, SUB), jnp.float32)
     for k in range(9):
         s, e = my_slab + k % 3 - 1, my_dom + k // 3 - 1
         inside = (s >= 0) & (s < n_slab) & (e >= 0) & (e < n_dom)
@@ -231,28 +236,35 @@
         other = pltpu.roll(row, LANES // 2, 1)
         left = (mine == row).astype(jnp.float32)
         right = (gid == other).astype(jnp.float32)
-        total = total + dot_lanes(left, right, None)
+        total = total + dot_lanes(right, left, None)
     count_ref[...] = jnp.zeros_like(count_ref)
-    count_ref[:, 0:high] = total
-    count = count_ref[...]
+    count_ref[0:high, 0:SUB] = total
+    count = jnp.transpose(count_ref[...])[0:SUB, :]
     met = jnp.where(count > 0.5, 1.0, 0.0)
-    before = lax.broadcasted_iota(jnp.int32, (LANES, LANES), 1) < lax.broadcasted_iota(
-        jnp.int32, (LANES, LANES), 0
+    before = lax.broadcasted_iota(jnp.int32, (LANES, LANES), 0) < lax.broadcasted_iota(
+        jnp.int32, (LANES, LANES), 1
     )
-    rank = dot_lanes(met, before.astype(jnp.float32), None)
+    rank = jnp.dot(met, before.astype(jnp.float32), preferred_element_type=jnp.float32)
     used = jnp.sum(met, axis=1, keepdims=True).astype(jnp.int32)
     list_ref[...] = jnp.where(lane == LANES - 1, used, 0)
     mult_ref[...] = jnp.zeros_like(mult_ref)
     line = window_ids(lane, *place)
+    line = jnp.floor((line + 0.5) / nblk) * (next_rows - nblk) + line
     here = lane.astype(jnp.float32)
+    here = jnp.floor((here + 0.5) / nblk) * (rows - nblk) + here
     spot = lax.broadcasted_iota(jnp.int32, (high, LANES), 0).astype(jnp.float32)
+    line_high, here_high, count_high = (jnp.floor(x * 0.015625) for x in (line, here, count))
+    line_low, here_low, count_low = line - 64.0 * line_high, here - 64.0 * here_high, count - 64.0 * count_high
     for a in range(nblk):
         pick = (rank[a : a + 1, :] == spot) & (met[a : a + 1, :] > 0.5)
-        what = jnp.where(sub == 0, line, jnp.where(sub == 1, count[a : a + 1, :], here))
-        out = dot_lanes(what, pick.astype(jnp.float32))
-        list_ref[a : a + 1, 0:high] = (out[0:1, :] + 0.5).astype(jnp.int32)
-        mult_ref[a : a + 1, 0:high] = out[1:2, :]
-        list_ref[nblk + a : nblk + a + 1, 0:high] = (out[2:3, :] + 0.5).astype(jnp.int32)
+        what = jnp.zeros((SUB, LANES), jnp.float32)
+        parts = (line_high, line_low, here_high, here_low, count_high[a : a + 1, :], count_low[a : a + 1, :])
+        for j, part in enumerate(parts):
+            what = jnp.where(sub == j, part, what)
+        out = dot_lanes(what, pick.astype(jnp.float32), None)
+        list_ref[a : a + 1, 0:high] = (64.0 * out[0:1, :] + out[1:2, :] + 0.5).astype(jnp.int32)
+        list_ref[nblk + a : nblk + a + 1, 0:high] = (64.0 * out[2:3, :] + out[3:4, :] + 0.5).astype(jnp.int32)
+        mult_ref[a : a + 1, 0:high] = 64.0 * out[4:5, :] + out[5:6, :]
 
 
 def gather_moments(got_ref, rows, mom_ref, center_ref, take_ref, nblk, ndev, far_scale):
@@ -276,12 +288,13 @@
 
 def second_kernel(
     n_slab, n_dom, far_scale,
-    cells_ref, mob_ref, got_ref, low_ref, mid_ref, high_ref,
-    out_ref, vel_ref, list_ref, coef_ref, wide_ref, moved_ref, old_ref,
-    stack_ref, own_ref, acc_ref, force_ref, mom_ref, center_ref, take_ref,
+    cell_ref, mob_ref, got_ref, low_ref, mid_ref, high_ref,
+    own_ref, wide_ref,
+    out_ref, vel_ref, list_ref, coef_ref, moved_ref, old_ref,
+    stack_ref, acc_ref, force_ref, mom_ref, center_ref, take_ref,
     win_ref, count_ref, mult_ref, next_ref, flat_ref, list_smem, mult_smem, sem,
 ):
-    nblk = cells_ref.shape[0]
+    nblk = mob_ref.shape[0]
     ndev = n_slab * n_dom
     rows = got_ref.shape[0] // ndev
     each = coef_ref.shape[0] // nblk
@@ -297,22 +310,28 @@
     def own_bur(k, b):
         return own_row(3 + k, b)
 
-    def block_row(a, e, k):
-        w = list_smem[nblk + a, e]
-        return win_ref[(w // nblk) * places + w % nblk + k * nblk]
-
-    def coef_of(a, e):
-        mult = mult_smem[a, e]
-        c = [jnp.broadcast_to(block_row(a, e, 3 + k) * mult, (SUB, LANES)) for k in range(3)]
-
+    def first_of(a, e):
+        return list_smem[nblk + a, e], mult_smem[a, e]
+
+    def rows_at(found):
+        first, mult = found
+        rows = [win_ref[first + k * nblk] for k in range(6)]
+        rows = rows[:3] + [row * mult for row in rows[3:]]
+        return tuple(jnp.broadcast_to(row, (SUB, LANES)) for row in rows)
+
+    def coef_of(a, e, found):
         def tile(t, rows):
-            value = wide_ref[a, 0, rows, :] * c[0] + wide_ref[a, 1, rows, :] * c[1] + wide_ref[a, 2, rows, :] * c[2]
+            value = (
+                wide_ref[a, 0, rows, :] * found[3]
+                + wide_ref[a, 1, rows, :] * found[4]
+                + wide_ref[a, 2, rows, :] * found[5]
+            )
             coef_ref[a * each + e, rows, :] = value
             return value
 
         return tile
 
-    build_lists(win_ref, places, nblk, my_slab, my_dom, n_slab, n_dom, count_ref, list_ref, mult_ref)
+    build_lists(win_ref, places, nblk, my_slab, my_dom, n_slab, n_dom, 3 * nblk + 1, count_ref, list_ref, mult_ref)
     copies = [
         pltpu.make_async_copy(list_ref, list_smem, sem.at[0]),
         pltpu.make_async_copy(mult_ref, mult_smem, sem.at[1]),
@@ -320,12 +339,10 @@
     for copy in copies:
         copy.start()
     gather_moments(got_ref, rows, mom_ref, center_ref, take_ref, nblk, ndev, far_scale)
-    widen_own(own_row, own_ref, nblk)
-    widen_own(own_bur, wide_ref, nblk)
     far_into(own_ref, wide_ref, mom_ref, center_ref, acc_ref, nblk, mom_ref.shape[0])
     for copy in copies:
         copy.wait()
-    near_into(block_row, coef_of, own_ref, lambda a: list_smem[a, LANES - 1], acc_ref, nblk)
+    near_into(first_of, rows_at, coef_of, own_ref, lambda a: list_smem[a, LANES - 1], acc_ref, nblk)
     sum_lanes(acc_ref, force_ref, nblk)
     pos, bur = [], []
     for k in range(3):
@@ -340,35 +357,46 @@
         moved_ref[here, :] = moved
         pos.append(moved)
         bur.append(next_ref[(3 + k) * nblk : (4 + k) * nblk, :])
-    last = moment_row(pos, bur, cells_ref, stack_ref)
+    last = moment_row(pos, bur, cell_ref, stack_ref)
     for r in range(3 * nblk):
         flat_ref[:, r * LANES : (r + 1) * LANES] = moved_ref[r : r + 1, :]
     flat_ref[:, 3 * nblk * LANES :] = last
     spread(out_ref, flat_ref[...])
 
 
+def widen_kernel(row_ref, own_ref, wide_ref):
+    nblk = own_ref.shape[0]
+    widen_own(lambda k, b: row_ref[k * nblk + b], own_ref, nblk)
+    widen_own(lambda k, b: row_ref[(3 + k) * nblk + b], wide_ref, nblk)
+
+
 def third_kernel(
     n_slab, n_dom, far_scale,
-    list_smem, mob_ref, vel_ref, old_ref, got_ref, coef_ref, wide_ref, next_ref,
+    list_ref, mob_ref, vel_ref, old_ref, got_ref, coef_ref, wide_ref, next_ref,
     moved_ref, velocity_ref,
-    own_ref, acc_ref, force_ref, mom_ref, center_ref, take_ref,
+    own_ref, acc_ref, force_ref, mom_ref, center_ref, take_ref, list_smem, sem,
 ):
+    copy = pltpu.make_async_copy(list_ref, list_smem, sem)
+    copy.start()
     nblk = mob_ref.shape[0]
     ndev = n_slab * n_dom
     rows = got_ref.shape[0] // ndev
     each = coef_ref.shape[0] // nblk
 
-    def block_row(a, e, k):
-        g = list_smem[a, e]
-        return got_ref[(g // nblk) * rows + g % nblk + k * nblk]
-
-    def coef_of(a, e):
+    def first_of(a, e):
+        return list_smem[a, e]
+
+    def rows_at(first):
+        return tuple(jnp.broadcast_to(got_ref[first + k * nblk], (SUB, LANES)) for k in range(3))
+
+    def coef_of(a, e, found):
         return lambda t, rows: coef_ref[a * each + e, rows, :]
 
     widen_own(lambda k, b: next_ref[k * nblk + b : k * nblk + b + 1, :], own_ref, nblk)
     gather_moments(got_ref, rows, mom_ref, center_ref, take_ref, nblk, ndev, far_scale)
     far_into(own_ref, wide_ref, mom_ref, center_ref, acc_ref, nblk, mom_ref.shape[0])
-    near_into(block_row, coef_of, own_ref, lambda a: list_smem[a, LANES - 1], acc_ref, nblk)
+    copy.wait()
+    near_into(first_of, rows_at, coef_of, own_ref, lambda a: list_smem[a, LANES - 1], acc_ref, nblk)
     sum_lanes(acc_ref, force_ref, nblk)
     for k in range(3):
         here = slice(k * nblk, (k + 1) * nblk)
@@ -414,7 +442,7 @@
             jax.ShapeDtypeStruct((ndev, 1, LANES), f32),
             jax.ShapeDtypeStruct((1, 1, places * LANES), f32),
             jax.ShapeDtypeStruct((nblk, LANES), f32),
-            jax.ShapeDtypeStruct((nblk,), jnp.int32),
+            jax.ShapeDtypeStruct((SUB, LANES), f32),
         ),
         in_specs=[SMEM] + [HBM] * 5,
         out_specs=(VMEM,) * 4,
@@ -426,7 +454,7 @@
             pltpu.VMEM((LANES, LANES), f32),
             pltpu.VMEM((-(-6 * nblk // SUB) * SUB, LANES), f32),
             pltpu.VMEM((SUB, LANES), jnp.int32),
-            pltpu.SemaphoreType.DMA((6,)),
+            pltpu.SemaphoreType.DMA((5,)),
         ],
         compiler_params=PARAMS,
         name="pack",
@@ -442,24 +470,31 @@
     column = jnp.concatenate([below, window, above], axis=0)
     left, right = neighbours(column, "dom")
     left, column, right = (x.reshape(3 * places, 1, LANES) for x in (left, column, right))
-    load2, vel, lists, coef, bur_wide, moved, old = pl.pallas_call(
+    pos_wide, bur_wide = pl.pallas_call(
+        widen_kernel,
+        out_shape=(wide, wide),
+        in_specs=[VMEM],
+        out_specs=(VMEM, VMEM),
+        compiler_params=PARAMS,
+        name="widen",
+    )(window.reshape(places, 1, LANES))
+    load2, vel, lists, coef, moved, old = pl.pallas_call(
         functools.partial(second_kernel, n_slab, n_dom, far_scale),
         out_shape=(
             payload,
             jax.ShapeDtypeStruct((3 * nblk, LANES), f32),
             jax.ShapeDtypeStruct((SUB, LANES), jnp.int32),
             jax.ShapeDtypeStruct((nblk * each, LANES, LANES), f32),
-            wide,
             jax.ShapeDtypeStruct((3 * nblk, LANES), f32),
             jax.ShapeDtypeStruct((3 * nblk, LANES), f32),
         ),
-        in_specs=[SMEM] + [VMEM] * 5,
-        out_specs=(VMEM,) * 7,
-        scratch_shapes=[pltpu.VMEM((LANES, LANES), f32), pltpu.VMEM((nblk, 3, LANES, LANES), f32)]
+        in_specs=[VMEM] * 8,
+        out_specs=(VMEM,) * 6,
+        scratch_shapes=[pltpu.VMEM((LANES, LANES), f32)]
         + scratch
         + [
             pltpu.VMEM((9 * places, 1, LANES), f32),
-            pltpu.VMEM((SUB, LANES), f32),
+            pltpu.VMEM((LANES, LANES), f32),
             pltpu.VMEM((SUB, LANES), f32),
             pltpu.VMEM((6 * nblk, LANES), f32),
             pltpu.VMEM((1, rows * LANES), f32),
@@ -469,15 +504,17 @@
         ],
         compiler_params=PARAMS,
         name="step_one",
-    )(cells, mob, got, left, column, right)
+    )(cells, mob, got, left, column, right, pos_wide, bur_wide)
     got2 = lax.all_to_all(load2, ("slab", "dom"), 0, 0, tiled=True).reshape(ndev * rows, 1, LANES)
     return pl.pallas_call(
         functools.partial(third_kernel, n_slab, n_dom, far_scale),
         out_shape=(jax.ShapeDtypeStruct((3, segs), f32),) * 2,
-        in_specs=[SMEM] + [VMEM] * 7,
+        in_specs=[VMEM] * 8,
         out_specs=(VMEM, VMEM),
-        scratch_shapes=[pltpu.VMEM((nblk, 3, LANES, LANES), f32)] + scratch,
-        compiler_params=PARAMS,
+        scratch_shapes=[pltpu.VMEM((nblk, 3, LANES, LANES), f32)]
+        + scratch
+        + [pltpu.SMEM((SUB, LANES), jnp.int32), pltpu.SemaphoreType.DMA(())],
+        compiler_params=PARAMS_EVEN,
         name="step_two",
     )(lists, mob, vel, old, got2, coef, bur_wide, moved)
 

time: 48.9 us -> 48 us (0.982)
  blocking collectives: 24.8 us -> 12.1 us
  waiting for transfers between devices: 1.4 us -> 8.13 us
  starting transfers between devices: 7.57 us -> 13.2 us
  Pallas kernels: 13.6 us -> 13.1 us
    all_to_all x1 -> x0, blocking collectives: 12.6 us -> none  [body(): got = lax.all_to_all(load, ('slab', 'dom'), 0, 0, tiled=True)]
    all_to_all x0 -> x1, waiting for transfers between devices: none -> 6.73 us  [body(): got = lax.all_to_all(load, ('slab', 'dom'), 0, 0, tiled=True)]
    all_to_all x0 -> x1, starting transfers between devices: none -> 5.63 us  [body(): got = lax.all_to_all(load, ('slab', 'dom'), 0, 0, tiled=True)]
    pallas_call x1, Pallas kernels: 6.61 us -> 5.71 us  [body(): pl.pallas_call(functools.partial(second_kernel, n_slab, n_dom, far_scale)...]
    pallas_call x1, Pallas kernels: 5.99 us -> 5.27 us  [body(): pl.pallas_call(functools.partial(third_kernel, n_slab, n_dom, far_scale),...]
    pallas_call x1, Pallas kernels: 1.05 us -> 1.63 us  [body(): pl.pallas_call(first_kernel, out_shape=(jax.ShapeDtypeStruct((ndev, 1, LA...]
  transfers between devices with their start and end apart: 4 -> 5, of which waited for: 2 -> 3; matrix products, arithmetic and copies ran while one was open for 0% -> 0% of each run, Pallas kernels for 0% -> 1%
where the time goes in v5:
time: 48 us; the launch traced here: 47.8 us
  starting transfers between devices  13.2 us (28%)
  Pallas kernels  13.1 us (27%)
  blocking collectives  12.1 us (25%)
  waiting for transfers between devices  8.13 us (17%)
  between operations  1.32 us (3%)
    all_to_all x1, blocking collectives, body(): lax.all_to_all(load2, ('slab', 'dom'), 0, 0, tiled=True)  12.1 us
    ppermute x2, starting transfers between devices, neighbours(): above = lax.ppermute(x, axis, [((i + 1) % count, i) for i in range(count)])  7.02 us
    all_to_all x1, waiting for transfers between devices, body(): got = lax.all_to_all(load, ('slab', 'dom'), 0, 0, tiled=True)  6.73 us
    pallas_call x1, Pallas kernels, body(): pl.pallas_call(functools.partial(second_kernel, n_slab, n_dom, far_scale)...  5.71 us
    all_to_all x1, starting transfers between devices, body(): got = lax.all_to_all(load, ('slab', 'dom'), 0, 0, tiled=True)  5.63 us
    pallas_call x1, Pallas kernels, body(): pl.pallas_call(functools.partial(third_kernel, n_slab, n_dom, far_scale),...  5.27 us
    pallas_call x1, Pallas kernels, body(): pl.pallas_call(first_kernel, out_shape=(jax.ShapeDtypeStruct((ndev, 1, LA...  1.63 us
    ppermute x2, waiting for transfers between devices, neighbours(): below = lax.ppermute(x, axis, [(i, (i + 1) % count) for i in range(count)])  1.32 us
  transfers between devices with their start and end apart: 5, of which 3 were waited for; matrix products, arithmetic and copies ran while one was open for 0% of the time, Pallas kernels for 1%

profile of v5, /device:TPU:0, one launch (start us, length us, event | category | flops | bytes accessed | tf_op | source)
XLA Modules:
  0.0 47.8 jit_solution(1898142377814849391)
XLA Ops:
  1.3 1.6 %pack.1 = (f32[32,1,128]{2,1,0:T(1,128)}, f32[1,1,3200]{2,1,0:T(1,128)S(1)}, f32[4,128]{1,0:T(4,128)S(1)}, f32[8,128]{1,0:T(8,128)S(1)}) custom-call(s32[1]{0:T(128)S(6)} %copy.10.count_ref, s32[4]{0:T(128)} %cells_hbm.1, f32[3,512]{1,0:T(4,128)} %pos_hbm.1, f32[3,512]{1,0:T(4,128)} %bur_hbm.1, s32[2,64]{1,0:T(2,128)} %bitcast.13, f32[4,128]{1,0:T(4,128)} %bitcast.12), custom_call_target="tpu_custom_call" | custom-call | tf_op jit(solution)/shard_map/pack/pallas_call | solution.py:439
  2.9 0.5 %collective-permute-start = (f32[1,1,3200]{2,1,0:T(1,128)S(1)}, f32[1,1,3200]{2,1,0:T(1,128)S(1)}, u32[]{:S(2)}, u32[]{:S(2)}) collective-permute-start(f32[1,1,3200]{2,1,0:T(1,128)S(1)} %get-tuple-element.17), channel_id=1, source_target_pairs={{0,4},{4,8},{8,12},{12,16},{16,20},{20,24},{24,28},{28,0},{1,5},{5... | collective-permute-start | bytes 38408 | tf_op jit(solution)/shard_map/ppermute | solution.py:413
  3.5 4.1 %collective-permute-start.1 = (f32[1,1,3200]{2,1,0:T(1,128)S(1)}, f32[1,1,3200]{2,1,0:T(1,128)S(1)}, u32[]{:S(2)}, u32[]{:S(2)}) collective-permute-start(f32[1,1,3200]{2,1,0:T(1,128)S(1)} %get-tuple-element.17), channel_id=1, source_target_pairs={{4,0},{8,4},{12,8},{16,12},{20,16},{24,20},{28,24},{0,28},{5,1},{9... | collective-permute-start | bytes 38408 | tf_op jit(solution)/shard_map/ppermute | solution.py:414
  7.6 1.3 %collective-permute-done = f32[1,1,3200]{2,1,0:T(1,128)S(1)} collective-permute-done((f32[1,1,3200]{2,1,0:T(1,128)S(1)}, f32[1,1,3200]{2,1,0:T(1,128)S(1)}, u32[]{:S(2)}, u32[]{:S(2)}) %collective-permute-start) | collective-permute-done | bytes 12832 | tf_op jit(solution)/shard_map/ppermute | solution.py:413
  8.9 0.1 collective-permute-done.1
  9.0 2.9 %collective-permute-start.3 = (f32[3,1,3200]{2,1,0:T(1,128)S(1)}, f32[3,1,3200]{2,1,0:T(1,128)S(1)}, u32[]{:S(2)}, u32[]{:S(2)}) collective-permute-start(f32[3,1,3200]{2,1,0:T(1,128)S(1)} %constant_dynamic-update-slice_fusion), channel_id=1, source_target_pairs={{1,0},{2,1},{3,2},{0,3},{5,4},{6,5},{7,6},{4,7},{9,8},{10,9},{11,1... | collective-permute-start | bytes 115208 | tf_op jit(solution)/shard_map/ppermute | solution.py:414
  11.9 0.0 collective-permute-start.2
  11.9 5.6 %all-to-all-start = ((f32[32,1,128]{2,1,0:T(1,128)}), f32[32,1,128]{2,1,0:T(1,128)S(1)}, u32[]{:S(2)}, u32[]{:S(2)}) async-start(f32[32,1,128]{2,1,0:T(1,128)} %get-tuple-element.16), calls=%async_computation | async-start | bytes 32768 | tf_op jit(solution)/shard_map/all_to_all | solution.py:468
  17.5 0.5 widen.1
  18.0 6.7 %all-to-all-done.got_ref = f32[32,1,128]{2,1,0:T(1,128)S(1)} async-done(((f32[32,1,128]{2,1,0:T(1,128)}), f32[32,1,128]{2,1,0:T(1,128)S(1)}, u32[]{:S(2)}, u32[]{:S(2)}) %all-to-all-start) | async-done | bytes 16416 | tf_op jit(solution)/shard_map/all_to_all | solution.py:468
  24.7 0.0 collective-permute-done.3
  24.7 0.0 collective-permute-done.2
  24.7 5.7 %step_one.1 = (f32[32,1,1664]{2,1,0:T(1,128)S(1)}, f32[12,128]{1,0:T(8,128)S(1)}, s32[8,128]{1,0:T(8,128)S(1)}, f32[152,128,128]{2,1,0:T(8,128)S(1)}, f32[12,128]{1,0:T(8,128)S(1)}, /*index=5*/f32[12,128]{1,0:T(8,128)S(1)}) custom-call(f32[8,128]{1,0:T(8,128)S(1)} %get-tuple-element.14.cell_ref, f32[4,128]{1,0:T(4,128)S(1)} %get-tuple-element.15.mob_ref, ...), custom_call_target="tpu_custom_call" | custom-call | tf_op jit(solution)/shard_map/step_one/pallas_call | solution.py:481
  30.5 12.1 %all_to_all.10 = f32[32,1,1664]{2,1,0:T(1,128)S(1)} all-to-all(f32[32,1,1664]{2,1,0:T(1,128)S(1)} %get-tuple-element.23), channel_id=1, replica_groups=mesh['slab'=8,'dom'=4] {'slab','dom'}, dimensions={0} | all-to-all | bytes 425984 | tf_op jit(solution)/shard_map/all_to_all | solution.py:508
  42.5 5.3 %step_two.1 = (f32[3,512]{1,0:T(4,128)}, f32[3,512]{1,0:T(4,128)}) custom-call(s32[8,128]{1,0:T(8,128)S(1)} %get-tuple-element.20.list_ref, f32[4,128]{1,0:T(4,128)S(1)} %get-tuple-element.15.mob_ref, f32[12,128]{1,0:T(8,128)S(1)} %get-tuple-element.21.vel_ref, f32[12,128]{1,0:T(8,128)S(1)} %get-tuple-element.22.old_ref, f32[416,1,128]{2,1,0:T(1,128)S(1)} %bitcast.7, ...), custom_call_target="tpu_custom_call" | custom-call | tf_op jit(solution)/shard_map/step_two/pallas_call | solution.py:509
  (3 shorter events, 0.0 us)
Async XLA Ops:
  2.9 6.0 %collective-permute-start = (f32[1,1,3200]{2,1,0:T(1,128)S(1)}, f32[1,1,3200]{2,1,0:T(1,128)S(1)}, u32[]{:S(2)}, u32[]{:S(2)}) collective-permute-start(f32[1,1,3200]{2,1,0:T(1,128)S(1)} %get-tuple-element.17), channel_id=1, source_target_pairs={{0,4},{4,8},{8,12},{12,16},{16,20},{20,24},{24,28},{28,0},{1,5},{5... | collective-permute-start | bytes 38408 | tf_op jit(solution)/shard_map/ppermute | solution.py:413
  3.5 5.5 %collective-permute-start.1 = (f32[1,1,3200]{2,1,0:T(1,128)S(1)}, f32[1,1,3200]{2,1,0:T(1,128)S(1)}, u32[]{:S(2)}, u32[]{:S(2)}) collective-permute-start(f32[1,1,3200]{2,1,0:T(1,128)S(1)} %get-tuple-element.17), channel_id=1, source_target_pairs={{4,0},{8,4},{12,8},{16,12},{20,16},{24,20},{28,24},{0,28},{5,1},{9... | collective-permute-start | bytes 38408 | tf_op jit(solution)/shard_map/ppermute | solution.py:414
  9.0 15.8 %collective-permute-start.3 = (f32[3,1,3200]{2,1,0:T(1,128)S(1)}, f32[3,1,3200]{2,1,0:T(1,128)S(1)}, u32[]{:S(2)}, u32[]{:S(2)}) collective-permute-start(f32[3,1,3200]{2,1,0:T(1,128)S(1)} %constant_dynamic-update-slice_fusion), channel_id=1, source_target_pairs={{1,0},{2,1},{3,2},{0,3},{5,4},{6,5},{7,6},{4,7},{9,8},{10,9},{11,1... | collective-permute-start | bytes 115208 | tf_op jit(solution)/shard_map/ppermute | solution.py:414
  11.9 12.8 %collective-permute-start.2 = (f32[3,1,3200]{2,1,0:T(1,128)S(1)}, f32[3,1,3200]{2,1,0:T(1,128)S(1)}, u32[]{:S(2)}, u32[]{:S(2)}) collective-permute-start(f32[3,1,3200]{2,1,0:T(1,128)S(1)} %constant_dynamic-update-slice_fusion), channel_id=1, source_target_pairs={{0,1},{1,2},{2,3},{3,0},{4,5},{5,6},{6,7},{7,4},{8,9},{9,10},{10,1... | collective-permute-start | bytes 115208 | tf_op jit(solution)/shard_map/ppermute | solution.py:413
  11.9 12.8 %all-to-all-start = ((f32[32,1,128]{2,1,0:T(1,128)}), f32[32,1,128]{2,1,0:T(1,128)S(1)}, u32[]{:S(2)}, u32[]{:S(2)}) async-start(f32[32,1,128]{2,1,0:T(1,128)} %get-tuple-element.16), calls=%async_computation | async-start | bytes 32768 | tf_op jit(solution)/shard_map/all_to_all | solution.py:468

commit v6 on v5

--- a/solution.py
+++ b/solution.py
@@ -164,31 +164,40 @@
 
 
 def near_into(first_of, rows_at, coef_of, own_ref, used_of, acc_ref, nblk):
+    def ahead(a, n):
+        return tuple(rows_at(first_of(a, 2 * n + j)) for j in range(2))
+
+    def add(a, n, found):
+        weigh = [coef_of(a, 2 * n + j, rows) for j, rows in enumerate(found)]
+        for t in range(LANES // SUB):
+            rows = slice(t * SUB, (t + 1) * SUB)
+            own = [own_ref[a, k, rows, :] for k in range(3)]
+            f = [None] * 3
+            for j, other in enumerate(found):
+                r = [own[k] - other[k] for k in range(3)]
+                sq = r[0] * r[0] + r[1] * r[1] + (r[2] * r[2] + CORE_NEAR)
+                u = lax.rsqrt(sq)
+                w = lax.rsqrt(sq + (CORE_FAR - CORE_NEAR))
+                wgt = weigh[j](t, rows) * (u * u * u - w * w * w)
+                f = [wgt * r[k] if f[k] is None else f[k] + wgt * r[k] for k in range(3)]
+            for k in range(3):
+                acc_ref[a, k, rows, :] = acc_ref[a, k, rows, :] + f[k]
+
     for a in range(nblk):
-
-        def ahead(n):
-            return tuple(rows_at(first_of(a, 2 * n + j)) for j in range(2))
+        used = used_of(a)
 
         def visit(n, carry):
-            following = ahead(n + 1)
-            p = [carry[j][:3] for j in range(2)]
-            weigh = [coef_of(a, 2 * n + j, carry[j]) for j in range(2)]
-            for t in range(LANES // SUB):
-                rows = slice(t * SUB, (t + 1) * SUB)
-                own = [own_ref[a, k, rows, :] for k in range(3)]
-                f = []
-                for j in range(2):
-                    r = [own[k] - p[j][k] for k in range(3)]
-                    sq = r[0] * r[0] + r[1] * r[1] + (r[2] * r[2] + CORE_NEAR)
-                    u = lax.rsqrt(sq)
-                    w = lax.rsqrt(sq + (CORE_FAR - CORE_NEAR))
-                    wgt = weigh[j](t, rows) * (u * u * u - w * w * w)
-                    f.append([wgt * r[k] for k in range(3)])
-                for k in range(3):
-                    acc_ref[a, k, rows, :] = acc_ref[a, k, rows, :] + (f[0][k] + f[1][k])
+            following = ahead(a, n + 1)
+            add(a, n, carry)
             return following
 
-        lax.fori_loop(0, (used_of(a) + 1) // 2, visit, ahead(0))
+        def last(n, carry):
+            add(a, n, carry[:1])
+            return carry
+
+        turns = used // 2
+        rest = lax.fori_loop(0, turns, visit, ahead(a, 0))
+        lax.fori_loop(turns, turns + used % 2, last, rest)
 
 
 def sum_lanes(acc_ref, force_ref, nblk):
@@ -212,7 +221,7 @@
 def window_ids(index, my_slab, my_dom, n_slab, n_dom, nblk):
     ids = jnp.full(index.shape, -2.0, jnp.float32)
     for k in range(9):
-        s, e = my_slab + k % 3 - 1, my_dom + k // 3 - 1
+        s, e = my_slab + k // 3 - 1, my_dom + k % 3 - 1
         inside = (s >= 0) & (s < n_slab) & (e >= 0) & (e < n_dom)
         first = jnp.where(inside, (s * n_dom + e) * nblk - k * nblk, -100000)
         here = (index >= k * nblk) & (index < (k + 1) * nblk)
@@ -230,7 +239,7 @@
     mine = jnp.where(sub < nblk, sub + own, -3).astype(jnp.float32)
     total = jnp.zeros((high, SUB), jnp.float32)
     for k in range(9):
-        s, e = my_slab + k % 3 - 1, my_dom + k // 3 - 1
+        s, e = my_slab + k // 3 - 1, my_dom + k % 3 - 1
         inside = (s >= 0) & (s < n_slab) & (e >= 0) & (e < n_dom)
         row = jnp.where(inside, win_ref[k * rows + rows - 1], -1.0)
         other = pltpu.roll(row, LANES // 2, 1)
@@ -410,8 +419,8 @@
 
 def neighbours(x, axis):
     count = lax.axis_size(axis)
+    above = lax.ppermute(x, axis, [((i + 1) % count, i) for i in range(count)])
     below = lax.ppermute(x, axis, [(i, (i + 1) % count) for i in range(count)])
-    above = lax.ppermute(x, axis, [((i + 1) % count, i) for i in range(count)])
     return below, above
 
 
@@ -466,10 +475,10 @@
         ),
     )
     got = lax.all_to_all(load, ("slab", "dom"), 0, 0, tiled=True)
-    below, above = neighbours(window, "slab")
-    column = jnp.concatenate([below, window, above], axis=0)
-    left, right = neighbours(column, "dom")
-    left, column, right = (x.reshape(3 * places, 1, LANES) for x in (left, column, right))
+    below, above = neighbours(window, "dom")
+    row = jnp.concatenate([below, window, above], axis=0)
+    left, right = neighbours(row, "slab")
+    left, row, right = (x.reshape(3 * places, 1, LANES) for x in (left, row, right))
     pos_wide, bur_wide = pl.pallas_call(
         widen_kernel,
         out_shape=(wide, wide),
@@ -504,7 +513,7 @@
         ],
         compiler_params=PARAMS,
         name="step_one",
-    )(cells, mob, got, left, column, right, pos_wide, bur_wide)
+    )(cells, mob, got, left, row, right, pos_wide, bur_wide)
     got2 = lax.all_to_all(load2, ("slab", "dom"), 0, 0, tiled=True).reshape(ndev * rows, 1, LANES)
     return pl.pallas_call(
         functools.partial(third_kernel, n_slab, n_dom, far_scale),

time: 48 us -> 47.3 us (0.985)
  starting transfers between devices: 13.2 us -> 11.5 us
  waiting for transfers between devices: 8.13 us -> 9.4 us
    ppermute x2, starting transfers between devices: 7.02 us -> 2.63 us  [neighbours(): above = lax.ppermute(x, axis, [((i + 1) % count, i) for i in range(count)])]
    ppermute x2, starting transfers between devices: 0.55 us -> 3.02 us  [neighbours(): below = lax.ppermute(x, axis, [(i, (i + 1) % count) for i in range(count)])]
    ppermute x2, waiting for transfers between devices: 0.08 us -> 1.06 us  [neighbours(): above = lax.ppermute(x, axis, [((i + 1) % count, i) for i in range(count)])]
where the time goes in v6:
time: 47.3 us; the launch traced here: 47.1 us
  Pallas kernels  12.7 us (27%)
  blocking collectives  12.1 us (26%)
  starting transfers between devices  11.5 us (24%)
  waiting for transfers between devices  9.4 us (20%)
  between operations  1.32 us (3%)
    all_to_all x1, blocking collectives, body(): lax.all_to_all(load2, ('slab', 'dom'), 0, 0, tiled=True)  12.1 us
    all_to_all x1, waiting for transfers between devices, body(): got = lax.all_to_all(load, ('slab', 'dom'), 0, 0, tiled=True)  6.73 us
    all_to_all x1, starting transfers between devices, body(): got = lax.all_to_all(load, ('slab', 'dom'), 0, 0, tiled=True)  5.85 us
    pallas_call x1, Pallas kernels, body(): pl.pallas_call(functools.partial(second_kernel, n_slab, n_dom, far_scale)...  5.53 us
    pallas_call x1, Pallas kernels, body(): pl.pallas_call(functools.partial(third_kernel, n_slab, n_dom, far_scale),...  5.12 us
    ppermute x2, starting transfers between devices, neighbours(): below = lax.ppermute(x, axis, [(i, (i + 1) % count) for i in range(count)])  3.02 us
    ppermute x2, starting transfers between devices, neighbours(): above = lax.ppermute(x, axis, [((i + 1) % count, i) for i in range(count)])  2.63 us
    pallas_call x1, Pallas kernels, body(): pl.pallas_call(first_kernel, out_shape=(jax.ShapeDtypeStruct((ndev, 1, LA...  1.63 us
  transfers between devices with their start and end apart: 5, of which 3 were waited for; matrix products, arithmetic and copies ran while one was open for 0% of the time, Pallas kernels for 1%

profile of v6, /device:TPU:0, one launch (start us, length us, event | category | flops | bytes accessed | tf_op | source)
XLA Modules:
  0.0 47.1 jit_solution(10756329481129789138)
XLA Ops:
  1.3 1.6 %pack.1 = (f32[32,1,128]{2,1,0:T(1,128)}, f32[1,1,3200]{2,1,0:T(1,128)S(1)}, f32[4,128]{1,0:T(4,128)S(1)}, f32[8,128]{1,0:T(8,128)S(1)}) custom-call(s32[1]{0:T(128)S(6)} %copy.10.count_ref, s32[4]{0:T(128)} %cells_hbm.1, f32[3,512]{1,0:T(4,128)} %pos_hbm.1, f32[3,512]{1,0:T(4,128)} %bur_hbm.1, s32[2,64]{1,0:T(2,128)} %bitcast.13, f32[4,128]{1,0:T(4,128)} %bitcast.12), custom_call_target="tpu_custom_call" | custom-call | tf_op jit(solution)/shard_map/pack/pallas_call | solution.py:448
  2.9 3.0 %collective-permute-start = (f32[1,1,3200]{2,1,0:T(1,128)S(1)}, f32[1,1,3200]{2,1,0:T(1,128)S(1)}, u32[]{:S(2)}, u32[]{:S(2)}) collective-permute-start(f32[1,1,3200]{2,1,0:T(1,128)S(1)} %get-tuple-element.17), channel_id=1, source_target_pairs={{0,1},{1,2},{2,3},{3,0},{4,5},{5,6},{6,7},{7,4},{8,9},{9,10},{10,1... | collective-permute-start | bytes 38408 | tf_op jit(solution)/shard_map/ppermute | solution.py:423
  5.9 1.0 %collective-permute-start.1 = (f32[1,1,3200]{2,1,0:T(1,128)S(1)}, f32[1,1,3200]{2,1,0:T(1,128)S(1)}, u32[]{:S(2)}, u32[]{:S(2)}) collective-permute-start(f32[1,1,3200]{2,1,0:T(1,128)S(1)} %get-tuple-element.17), channel_id=1, source_target_pairs={{1,0},{2,1},{3,2},{0,3},{5,4},{6,5},{7,6},{4,7},{9,8},{10,9},{11,1... | collective-permute-start | bytes 38408 | tf_op jit(solution)/shard_map/ppermute | solution.py:422
  7.0 1.6 %collective-permute-done = f32[1,1,3200]{2,1,0:T(1,128)S(1)} collective-permute-done((f32[1,1,3200]{2,1,0:T(1,128)S(1)}, f32[1,1,3200]{2,1,0:T(1,128)S(1)}, u32[]{:S(2)}, u32[]{:S(2)}) %collective-permute-start) | collective-permute-done | bytes 12832 | tf_op jit(solution)/shard_map/ppermute | solution.py:423
  8.6 1.1 %collective-permute-done.1 = f32[1,1,3200]{2,1,0:T(1,128)S(1)} collective-permute-done((f32[1,1,3200]{2,1,0:T(1,128)S(1)}, f32[1,1,3200]{2,1,0:T(1,128)S(1)}, u32[]{:S(2)}, u32[]{:S(2)}) %collective-permute-start.1) | collective-permute-done | bytes 12832 | tf_op jit(solution)/shard_map/ppermute | solution.py:422
  9.6 1.6 %collective-permute-start.3 = (f32[3,1,3200]{2,1,0:T(1,128)S(1)}, f32[3,1,3200]{2,1,0:T(1,128)S(1)}, u32[]{:S(2)}, u32[]{:S(2)}) collective-permute-start(f32[3,1,3200]{2,1,0:T(1,128)S(1)} %constant_dynamic-update-slice_fusion), channel_id=1, source_target_pairs={{4,0},{8,4},{12,8},{16,12},{20,16},{24,20},{28,24},{0,28},{5,1},{9... | collective-permute-start | bytes 115208 | tf_op jit(solution)/shard_map/ppermute | solution.py:422
  11.3 0.0 collective-permute-start.2
  11.3 5.9 %all-to-all-start = ((f32[32,1,128]{2,1,0:T(1,128)}), f32[32,1,128]{2,1,0:T(1,128)S(1)}, u32[]{:S(2)}, u32[]{:S(2)}) async-start(f32[32,1,128]{2,1,0:T(1,128)} %get-tuple-element.16), calls=%async_computation | async-start | bytes 32768 | tf_op jit(solution)/shard_map/all_to_all | solution.py:477
  17.1 0.5 widen.1
  17.6 6.7 %all-to-all-done.got_ref = f32[32,1,128]{2,1,0:T(1,128)S(1)} async-done(((f32[32,1,128]{2,1,0:T(1,128)}), f32[32,1,128]{2,1,0:T(1,128)S(1)}, u32[]{:S(2)}, u32[]{:S(2)}) %all-to-all-start) | async-done | bytes 16416 | tf_op jit(solution)/shard_map/all_to_all | solution.py:477
  24.3 0.0 collective-permute-done.3
  24.3 0.0 collective-permute-done.2
  24.3 5.5 %step_one.1 = (f32[32,1,1664]{2,1,0:T(1,128)S(1)}, f32[12,128]{1,0:T(8,128)S(1)}, s32[8,128]{1,0:T(8,128)S(1)}, f32[152,128,128]{2,1,0:T(8,128)S(1)}, f32[12,128]{1,0:T(8,128)S(1)}, /*index=5*/f32[12,128]{1,0:T(8,128)S(1)}) custom-call(f32[8,128]{1,0:T(8,128)S(1)} %get-tuple-element.14.cell_ref, f32[4,128]{1,0:T(4,128)S(1)} %get-tuple-element.15.mob_ref, ...), custom_call_target="tpu_custom_call" | custom-call | tf_op jit(solution)/shard_map/step_one/pallas_call | solution.py:490
  29.9 12.1 %all_to_all.10 = f32[32,1,1664]{2,1,0:T(1,128)S(1)} all-to-all(f32[32,1,1664]{2,1,0:T(1,128)S(1)} %get-tuple-element.23), channel_id=1, replica_groups=mesh['slab'=8,'dom'=4] {'slab','dom'}, dimensions={0} | all-to-all | bytes 425984 | tf_op jit(solution)/shard_map/all_to_all | solution.py:517
  41.9 5.1 %step_two.1 = (f32[3,512]{1,0:T(4,128)}, f32[3,512]{1,0:T(4,128)}) custom-call(s32[8,128]{1,0:T(8,128)S(1)} %get-tuple-element.20.list_ref, f32[4,128]{1,0:T(4,128)S(1)} %get-tuple-element.15.mob_ref, f32[12,128]{1,0:T(8,128)S(1)} %get-tuple-element.21.vel_ref, f32[12,128]{1,0:T(8,128)S(1)} %get-tuple-element.22.old_ref, f32[416,1,128]{2,1,0:T(1,128)S(1)} %bitcast.7, ...), custom_call_target="tpu_custom_call" | custom-call | tf_op jit(solution)/shard_map/step_two/pallas_call | solution.py:518
  (3 shorter events, 0.0 us)
Async XLA Ops:
  2.9 5.7 %collective-permute-start = (f32[1,1,3200]{2,1,0:T(1,128)S(1)}, f32[1,1,3200]{2,1,0:T(1,128)S(1)}, u32[]{:S(2)}, u32[]{:S(2)}) collective-permute-start(f32[1,1,3200]{2,1,0:T(1,128)S(1)} %get-tuple-element.17), channel_id=1, source_target_pairs={{0,1},{1,2},{2,3},{3,0},{4,5},{5,6},{6,7},{7,4},{8,9},{9,10},{10,1... | collective-permute-start | bytes 38408 | tf_op jit(solution)/shard_map/ppermute | solution.py:423
  5.9 3.7 %collective-permute-start.1 = (f32[1,1,3200]{2,1,0:T(1,128)S(1)}, f32[1,1,3200]{2,1,0:T(1,128)S(1)}, u32[]{:S(2)}, u32[]{:S(2)}) collective-permute-start(f32[1,1,3200]{2,1,0:T(1,128)S(1)} %get-tuple-element.17), channel_id=1, source_target_pairs={{1,0},{2,1},{3,2},{0,3},{5,4},{6,5},{7,6},{4,7},{9,8},{10,9},{11,1... | collective-permute-start | bytes 38408 | tf_op jit(solution)/shard_map/ppermute | solution.py:422
  9.6 14.7 %collective-permute-start.3 = (f32[3,1,3200]{2,1,0:T(1,128)S(1)}, f32[3,1,3200]{2,1,0:T(1,128)S(1)}, u32[]{:S(2)}, u32[]{:S(2)}) collective-permute-start(f32[3,1,3200]{2,1,0:T(1,128)S(1)} %constant_dynamic-update-slice_fusion), channel_id=1, source_target_pairs={{4,0},{8,4},{12,8},{16,12},{20,16},{24,20},{28,24},{0,28},{5,1},{9... | collective-permute-start | bytes 115208 | tf_op jit(solution)/shard_map/ppermute | solution.py:422
  11.3 13.1 %collective-permute-start.2 = (f32[3,1,3200]{2,1,0:T(1,128)S(1)}, f32[3,1,3200]{2,1,0:T(1,128)S(1)}, u32[]{:S(2)}, u32[]{:S(2)}) collective-permute-start(f32[3,1,3200]{2,1,0:T(1,128)S(1)} %constant_dynamic-update-slice_fusion), channel_id=1, source_target_pairs={{0,4},{4,8},{8,12},{12,16},{16,20},{20,24},{24,28},{28,0},{1,5},{5... | collective-permute-start | bytes 115208 | tf_op jit(solution)/shard_map/ppermute | solution.py:423
  11.3 13.1 %all-to-all-start = ((f32[32,1,128]{2,1,0:T(1,128)}), f32[32,1,128]{2,1,0:T(1,128)S(1)}, u32[]{:S(2)}, u32[]{:S(2)}) async-start(f32[32,1,128]{2,1,0:T(1,128)} %get-tuple-element.16), calls=%async_computation | async-start | bytes 32768 | tf_op jit(solution)/shard_map/all_to_all | solution.py:477

commit v7 on v5

--- a/solution.py
+++ b/solution.py
@@ -212,7 +212,7 @@
 def window_ids(index, my_slab, my_dom, n_slab, n_dom, nblk):
     ids = jnp.full(index.shape, -2.0, jnp.float32)
     for k in range(9):
-        s, e = my_slab + k % 3 - 1, my_dom + k // 3 - 1
+        s, e = my_slab + k // 3 - 1, my_dom + k % 3 - 1
         inside = (s >= 0) & (s < n_slab) & (e >= 0) & (e < n_dom)
         first = jnp.where(inside, (s * n_dom + e) * nblk - k * nblk, -100000)
         here = (index >= k * nblk) & (index < (k + 1) * nblk)
@@ -230,7 +230,7 @@
     mine = jnp.where(sub < nblk, sub + own, -3).astype(jnp.float32)
     total = jnp.zeros((high, SUB), jnp.float32)
     for k in range(9):
-        s, e = my_slab + k % 3 - 1, my_dom + k // 3 - 1
+        s, e = my_slab + k // 3 - 1, my_dom + k % 3 - 1
         inside = (s >= 0) & (s < n_slab) & (e >= 0) & (e < n_dom)
         row = jnp.where(inside, win_ref[k * rows + rows - 1], -1.0)
         other = pltpu.roll(row, LANES // 2, 1)
@@ -410,8 +410,8 @@
 
 def neighbours(x, axis):
     count = lax.axis_size(axis)
+    above = lax.ppermute(x, axis, [((i + 1) % count, i) for i in range(count)])
     below = lax.ppermute(x, axis, [(i, (i + 1) % count) for i in range(count)])
-    above = lax.ppermute(x, axis, [((i + 1) % count, i) for i in range(count)])
     return below, above
 
 
@@ -466,10 +466,10 @@
         ),
     )
     got = lax.all_to_all(load, ("slab", "dom"), 0, 0, tiled=True)
-    below, above = neighbours(window, "slab")
-    column = jnp.concatenate([below, window, above], axis=0)
-    left, right = neighbours(column, "dom")
-    left, column, right = (x.reshape(3 * places, 1, LANES) for x in (left, column, right))
+    below, above = neighbours(window, "dom")
+    row = jnp.concatenate([below, window, above], axis=0)
+    left, right = neighbours(row, "slab")
+    left, row, right = (x.reshape(3 * places, 1, LANES) for x in (left, row, right))
     pos_wide, bur_wide = pl.pallas_call(
         widen_kernel,
         out_shape=(wide, wide),
@@ -504,7 +504,7 @@
         ],
         compiler_params=PARAMS,
         name="step_one",
-    )(cells, mob, got, left, column, right, pos_wide, bur_wide)
+    )(cells, mob, got, left, row, right, pos_wide, bur_wide)
     got2 = lax.all_to_all(load2, ("slab", "dom"), 0, 0, tiled=True).reshape(ndev * rows, 1, LANES)
     return pl.pallas_call(
         functools.partial(third_kernel, n_slab, n_dom, far_scale),

time: 48 us -> 47.6 us (level)
  starting transfers between devices: 13.2 us -> 11.5 us
  waiting for transfers between devices: 8.13 us -> 9.4 us
    ppermute x2, starting transfers between devices: 7.02 us -> 2.63 us  [neighbours(): above = lax.ppermute(x, axis, [((i + 1) % count, i) for i in range(count)])]
    ppermute x2, starting transfers between devices: 0.55 us -> 3.02 us  [neighbours(): below = lax.ppermute(x, axis, [(i, (i + 1) % count) for i in range(count)])]
    ppermute x2, waiting for transfers between devices: 0.08 us -> 1.06 us  [neighbours(): above = lax.ppermute(x, axis, [((i + 1) % count, i) for i in range(count)])]
where the time goes in v7:
time: 47.6 us; the launch traced here: 47.4 us
  Pallas kernels  13.1 us (28%)
  blocking collectives  12.1 us (25%)
  starting transfers between devices  11.5 us (24%)
  waiting for transfers between devices  9.4 us (20%)
  between operations  1.32 us (3%)
    all_to_all x1, blocking collectives, body(): lax.all_to_all(load2, ('slab', 'dom'), 0, 0, tiled=True)  12.1 us
    all_to_all x1, waiting for transfers between devices, body(): got = lax.all_to_all(load, ('slab', 'dom'), 0, 0, tiled=True)  6.73 us
    all_to_all x1, starting transfers between devices, body(): got = lax.all_to_all(load, ('slab', 'dom'), 0, 0, tiled=True)  5.85 us
    pallas_call x1, Pallas kernels, body(): pl.pallas_call(functools.partial(second_kernel, n_slab, n_dom, far_scale)...  5.71 us
    pallas_call x1, Pallas kernels, body(): pl.pallas_call(functools.partial(third_kernel, n_slab, n_dom, far_scale),...  5.27 us
    ppermute x2, starting transfers between devices, neighbours(): below = lax.ppermute(x, axis, [(i, (i + 1) % count) for i in range(count)])  3.02 us
    ppermute x2, starting transfers between devices, neighbours(): above = lax.ppermute(x, axis, [((i + 1) % count, i) for i in range(count)])  2.63 us
    pallas_call x1, Pallas kernels, body(): pl.pallas_call(first_kernel, out_shape=(jax.ShapeDtypeStruct((ndev, 1, LA...  1.63 us
  transfers between devices with their start and end apart: 5, of which 3 were waited for; matrix products, arithmetic and copies ran while one was open for 0% of the time, Pallas kernels for 1%

profile of v7, /device:TPU:0, one launch (start us, length us, event | category | flops | bytes accessed | tf_op | source)
XLA Modules:
  0.0 47.4 jit_solution(11730990732570759140)
XLA Ops:
  1.3 1.6 %pack.1 = (f32[32,1,128]{2,1,0:T(1,128)}, f32[1,1,3200]{2,1,0:T(1,128)S(1)}, f32[4,128]{1,0:T(4,128)S(1)}, f32[8,128]{1,0:T(8,128)S(1)}) custom-call(s32[1]{0:T(128)S(6)} %copy.10.count_ref, s32[4]{0:T(128)} %cells_hbm.1, f32[3,512]{1,0:T(4,128)} %pos_hbm.1, f32[3,512]{1,0:T(4,128)} %bur_hbm.1, s32[2,64]{1,0:T(2,128)} %bitcast.13, f32[4,128]{1,0:T(4,128)} %bitcast.12), custom_call_target="tpu_custom_call" | custom-call | tf_op jit(solution)/shard_map/pack/pallas_call | solution.py:439
  2.9 3.0 %collective-permute-start = (f32[1,1,3200]{2,1,0:T(1,128)S(1)}, f32[1,1,3200]{2,1,0:T(1,128)S(1)}, u32[]{:S(2)}, u32[]{:S(2)}) collective-permute-start(f32[1,1,3200]{2,1,0:T(1,128)S(1)} %get-tuple-element.17), channel_id=1, source_target_pairs={{0,1},{1,2},{2,3},{3,0},{4,5},{5,6},{6,7},{7,4},{8,9},{9,10},{10,1... | collective-permute-start | bytes 38408 | tf_op jit(solution)/shard_map/ppermute | solution.py:414
  5.9 1.0 %collective-permute-start.1 = (f32[1,1,3200]{2,1,0:T(1,128)S(1)}, f32[1,1,3200]{2,1,0:T(1,128)S(1)}, u32[]{:S(2)}, u32[]{:S(2)}) collective-permute-start(f32[1,1,3200]{2,1,0:T(1,128)S(1)} %get-tuple-element.17), channel_id=1, source_target_pairs={{1,0},{2,1},{3,2},{0,3},{5,4},{6,5},{7,6},{4,7},{9,8},{10,9},{11,1... | collective-permute-start | bytes 38408 | tf_op jit(solution)/shard_map/ppermute | solution.py:413
  7.0 1.6 %collective-permute-done = f32[1,1,3200]{2,1,0:T(1,128)S(1)} collective-permute-done((f32[1,1,3200]{2,1,0:T(1,128)S(1)}, f32[1,1,3200]{2,1,0:T(1,128)S(1)}, u32[]{:S(2)}, u32[]{:S(2)}) %collective-permute-start) | collective-permute-done | bytes 12832 | tf_op jit(solution)/shard_map/ppermute | solution.py:414
  8.6 1.1 %collective-permute-done.1 = f32[1,1,3200]{2,1,0:T(1,128)S(1)} collective-permute-done((f32[1,1,3200]{2,1,0:T(1,128)S(1)}, f32[1,1,3200]{2,1,0:T(1,128)S(1)}, u32[]{:S(2)}, u32[]{:S(2)}) %collective-permute-start.1) | collective-permute-done | bytes 12832 | tf_op jit(solution)/shard_map/ppermute | solution.py:413
  9.6 1.6 %collective-permute-start.3 = (f32[3,1,3200]{2,1,0:T(1,128)S(1)}, f32[3,1,3200]{2,1,0:T(1,128)S(1)}, u32[]{:S(2)}, u32[]{:S(2)}) collective-permute-start(f32[3,1,3200]{2,1,0:T(1,128)S(1)} %constant_dynamic-update-slice_fusion), channel_id=1, source_target_pairs={{4,0},{8,4},{12,8},{16,12},{20,16},{24,20},{28,24},{0,28},{5,1},{9... | collective-permute-start | bytes 115208 | tf_op jit(solution)/shard_map/ppermute | solution.py:413
  11.3 0.0 collective-permute-start.2
  11.3 5.9 %all-to-all-start = ((f32[32,1,128]{2,1,0:T(1,128)}), f32[32,1,128]{2,1,0:T(1,128)S(1)}, u32[]{:S(2)}, u32[]{:S(2)}) async-start(f32[32,1,128]{2,1,0:T(1,128)} %get-tuple-element.16), calls=%async_computation | async-start | bytes 32768 | tf_op jit(solution)/shard_map/all_to_all | solution.py:468
  17.1 0.5 widen.1
  17.6 6.7 %all-to-all-done.got_ref = f32[32,1,128]{2,1,0:T(1,128)S(1)} async-done(((f32[32,1,128]{2,1,0:T(1,128)}), f32[32,1,128]{2,1,0:T(1,128)S(1)}, u32[]{:S(2)}, u32[]{:S(2)}) %all-to-all-start) | async-done | bytes 16416 | tf_op jit(solution)/shard_map/all_to_all | solution.py:468
  24.3 0.0 collective-permute-done.3
  24.3 0.0 collective-permute-done.2
  24.3 5.7 %step_one.1 = (f32[32,1,1664]{2,1,0:T(1,128)S(1)}, f32[12,128]{1,0:T(8,128)S(1)}, s32[8,128]{1,0:T(8,128)S(1)}, f32[152,128,128]{2,1,0:T(8,128)S(1)}, f32[12,128]{1,0:T(8,128)S(1)}, /*index=5*/f32[12,128]{1,0:T(8,128)S(1)}) custom-call(f32[8,128]{1,0:T(8,128)S(1)} %get-tuple-element.14.cell_ref, f32[4,128]{1,0:T(4,128)S(1)} %get-tuple-element.15.mob_ref, ...), custom_call_target="tpu_custom_call" | custom-call | tf_op jit(solution)/shard_map/step_one/pallas_call | solution.py:481
  30.0 12.1 %all_to_all.10 = f32[32,1,1664]{2,1,0:T(1,128)S(1)} all-to-all(f32[32,1,1664]{2,1,0:T(1,128)S(1)} %get-tuple-element.23), channel_id=1, replica_groups=mesh['slab'=8,'dom'=4] {'slab','dom'}, dimensions={0} | all-to-all | bytes 425984 | tf_op jit(solution)/shard_map/all_to_all | solution.py:508
  42.1 5.3 %step_two.1 = (f32[3,512]{1,0:T(4,128)}, f32[3,512]{1,0:T(4,128)}) custom-call(s32[8,128]{1,0:T(8,128)S(1)} %get-tuple-element.20.list_ref, f32[4,128]{1,0:T(4,128)S(1)} %get-tuple-element.15.mob_ref, f32[12,128]{1,0:T(8,128)S(1)} %get-tuple-element.21.vel_ref, f32[12,128]{1,0:T(8,128)S(1)} %get-tuple-element.22.old_ref, f32[416,1,128]{2,1,0:T(1,128)S(1)} %bitcast.7, ...), custom_call_target="tpu_custom_call" | custom-call | tf_op jit(solution)/shard_map/step_two/pallas_call | solution.py:509
  (3 shorter events, 0.0 us)
Async XLA Ops:
  2.9 5.7 %collective-permute-start = (f32[1,1,3200]{2,1,0:T(1,128)S(1)}, f32[1,1,3200]{2,1,0:T(1,128)S(1)}, u32[]{:S(2)}, u32[]{:S(2)}) collective-permute-start(f32[1,1,3200]{2,1,0:T(1,128)S(1)} %get-tuple-element.17), channel_id=1, source_target_pairs={{0,1},{1,2},{2,3},{3,0},{4,5},{5,6},{6,7},{7,4},{8,9},{9,10},{10,1... | collective-permute-start | bytes 38408 | tf_op jit(solution)/shard_map/ppermute | solution.py:414
  5.9 3.7 %collective-permute-start.1 = (f32[1,1,3200]{2,1,0:T(1,128)S(1)}, f32[1,1,3200]{2,1,0:T(1,128)S(1)}, u32[]{:S(2)}, u32[]{:S(2)}) collective-permute-start(f32[1,1,3200]{2,1,0:T(1,128)S(1)} %get-tuple-element.17), channel_id=1, source_target_pairs={{1,0},{2,1},{3,2},{0,3},{5,4},{6,5},{7,6},{4,7},{9,8},{10,9},{11,1... | collective-permute-start | bytes 38408 | tf_op jit(solution)/shard_map/ppermute | solution.py:413
  9.6 14.7 %collective-permute-start.3 = (f32[3,1,3200]{2,1,0:T(1,128)S(1)}, f32[3,1,3200]{2,1,0:T(1,128)S(1)}, u32[]{:S(2)}, u32[]{:S(2)}) collective-permute-start(f32[3,1,3200]{2,1,0:T(1,128)S(1)} %constant_dynamic-update-slice_fusion), channel_id=1, source_target_pairs={{4,0},{8,4},{12,8},{16,12},{20,16},{24,20},{28,24},{0,28},{5,1},{9... | collective-permute-start | bytes 115208 | tf_op jit(solution)/shard_map/ppermute | solution.py:413
  11.3 13.1 %collective-permute-start.2 = (f32[3,1,3200]{2,1,0:T(1,128)S(1)}, f32[3,1,3200]{2,1,0:T(1,128)S(1)}, u32[]{:S(2)}, u32[]{:S(2)}) collective-permute-start(f32[3,1,3200]{2,1,0:T(1,128)S(1)} %constant_dynamic-update-slice_fusion), channel_id=1, source_target_pairs={{0,4},{4,8},{8,12},{12,16},{16,20},{20,24},{24,28},{28,0},{1,5},{5... | collective-permute-start | bytes 115208 | tf_op jit(solution)/shard_map/ppermute | solution.py:414
  11.3 13.1 %all-to-all-start = ((f32[32,1,128]{2,1,0:T(1,128)}), f32[32,1,128]{2,1,0:T(1,128)S(1)}, u32[]{:S(2)}, u32[]{:S(2)}) async-start(f32[32,1,128]{2,1,0:T(1,128)} %get-tuple-element.16), calls=%async_computation | async-start | bytes 32768 | tf_op jit(solution)/shard_map/all_to_all | solution.py:468
